TPU v7x, 128 devices: a whole 4x4x4 slice. The times are simulated.
128 devices in a mesh: brick: 8 (over y, core), grp: 16 (over x, z).
Axes of the slice: x: 4, y: 4, z: 4, core: 2. Of those that a mesh axis runs over, the one named last changes fastest.
Arguments:
- source: float32 [16, 8, 2, 32, 1024], P('grp', 'brick'), may hold values from -21 to 21
- uptake: float32 [16, 8, 2, 32, 1024], P('grp', 'brick'), may hold values from 0.00015 to 0.006
- conductance: float32 [16, 8, 6, 2, 32, 1024], P('grp', 'brick'), may hold values from 0 to 3, as said below
- occupancy: int32 [16, 2, 8], replicated, may hold values from 0 to 1, as said below
- assignment: int32 [8], replicated, may hold values from 0 to 7, as said below
Outputs:
- solution_field: float32 [16, 8, 2, 32, 1024], P('grp', 'brick')
- residual: float32 [16, 8, 2, 32, 1024], P('grp', 'brick')
Inputs may be any that keep to these rules, and one draw needn't show every extreme that they name: `occupancy`: 1 marks an occupied brick; in every draw one patch of some slab has all its bricks occupied. `assignment`: each patch is held by exactly one index of brick. `conductance`: equal at both ends of a bond: the value toward +x at a cell is the value toward -x at its +x neighbour, likewise for y and z, the lattice being read cyclically; values toward +z and -z are 0.3 or more.
All inputs are finite; a program needn't handle non-finite values.
Results may differ from a plain program's by a relative error of at most 0.0003.
Values sent between devices are 32-bit elements; how exact they have to be, the bound alone decides.
A program may use at most 128 MiB of HBM per device.

v0:
```python
import functools

import jax
import jax.numpy as jnp
from jax import lax
from jax.experimental import pallas as pl
from jax.experimental.pallas import tpu as pltpu
from jax.sharding import PartitionSpec as P

MESH_IDS = pl.DeviceIdType.MESH

BS = 32
PATCH_X = 1
PATCH_Y = 2
ITERS = 3


OMEGA = 0.6


def exchange_kernel(
    x_ref, xy_ref, z_ref, o_ref, xy_out, z_out,
    landed_b, landed_g, landed_xy, landed_z,
    send_b, recv_b, send_g, recv_g, send_xy, recv_xy, send_z, recv_z,
):
    here_brick = lax.axis_index("brick")
    here_grp = lax.axis_index("grp")
    n_brick = landed_b.shape[0]
    n_grp = landed_g.shape[0]
    brick_peers = [(lax.rem(here_brick + k, n_brick), here_grp) for k in range(1, n_brick)]
    grp_peers = [(here_brick, lax.rem(here_grp + k, n_grp)) for k in range(1, n_grp)]
    barrier = pltpu.get_barrier_semaphore()
    for peer in brick_peers + grp_peers:
        pl.semaphore_signal(barrier, inc=1, device_id=peer, device_id_type=MESH_IDS)
    pl.semaphore_wait(barrier, len(brick_peers) + len(grp_peers))

    def send(src, dst, sends, recvs, index, peer):
        copy = pltpu.make_async_remote_copy(
            src_ref=src,
            dst_ref=dst.at[index],
            send_sem=sends.at[index],
            recv_sem=recvs.at[index],
            device_id=peer,
            device_id_type=MESH_IDS,
        )
        copy.start()
        return copy

    face_copies = [
        send(z_ref, landed_z, send_z, recv_z, 0, grp_peers[0]),
        send(z_ref, landed_z, send_z, recv_z, 1, grp_peers[-1]),
    ]
    face_copies += [
        send(xy_ref, landed_xy, send_xy, recv_xy, k, peer)
        for k, peer in enumerate(brick_peers, start=1)
    ]
    copies = [
        send(x_ref, landed_b, send_b, recv_b, k, peer)
        for k, peer in enumerate(brick_peers, start=1)
    ]
    landed_b[0] = x_ref[...]
    for copy in copies:
        copy.wait()
    total = landed_b[lax.rem(here_brick, n_brick)]
    for j in range(1, n_brick):
        total = total + landed_b[lax.rem(here_brick + n_brick - j, n_brick)]
    o_ref[...] = total
    landed_g[0] = total
    copies = [
        send(o_ref, landed_g, send_g, recv_g, k, peer)
        for k, peer in enumerate(grp_peers, start=1)
    ]
    for copy in copies:
        copy.wait()
    total = landed_g[lax.rem(here_grp, n_grp)]
    for j in range(1, n_grp):
        total = total + landed_g[lax.rem(here_grp + n_grp - j, n_grp)]
    o_ref[...] = total
    for copy in face_copies:
        copy.wait()
    landed_xy[0] = xy_ref[...]
    xy_out[...] = landed_xy[...]
    z_out[...] = landed_z[...]


def exchange(tile, xy, z, kernel_id):
    n_brick = lax.axis_size("brick")
    n_grp = lax.axis_size("grp")
    vmem = pl.BlockSpec(memory_space=pltpu.VMEM)
    dma = pltpu.SemaphoreType.DMA
    return pl.pallas_call(
        exchange_kernel,
        out_shape=(
            jax.ShapeDtypeStruct(tile.shape, jnp.float32),
            jax.ShapeDtypeStruct((n_brick,) + xy.shape, jnp.float32),
            jax.ShapeDtypeStruct((2,) + z.shape, jnp.float32),
        ),
        in_specs=[vmem] * 3,
        out_specs=(vmem, vmem, vmem),
        scratch_shapes=[
            pltpu.VMEM((n_brick,) + tile.shape, jnp.float32),
            pltpu.VMEM((n_grp,) + tile.shape, jnp.float32),
            pltpu.VMEM((n_brick,) + xy.shape, jnp.float32),
            pltpu.VMEM((2,) + z.shape, jnp.float32),
            dma((n_brick,)),
            dma((n_brick,)),
            dma((n_grp,)),
            dma((n_grp,)),
            dma((n_brick,)),
            dma((n_brick,)),
            dma((2,)),
            dma((2,)),
        ],
        compiler_params=pltpu.CompilerParams(collective_id=kernel_id, has_side_effects=True),
    )(tile, xy, z)


def stencil_kernel(f_ref, bonds_ref, masks_ref, diag_ref, rows_ref, faces_ref, o_ref):
    slots, width, lanes = f_ref.shape
    row = lax.broadcasted_iota(jnp.int32, (width, lanes), 0)
    lane = lax.broadcasted_iota(jnp.int32, (width, lanes), 1)
    pick = lax.broadcasted_iota(jnp.int32, (BS, lanes), 0)
    spot = lax.broadcasted_iota(jnp.int32, (BS, lanes), 1)
    spread_z = (spot // BS == pick).astype(jnp.float32)
    spread_y = (spot % BS == pick).astype(jnp.float32)

    def spread(face, table):
        return jnp.dot(face, table, precision=lax.Precision.HIGHEST, preferred_element_type=jnp.float32)

    for s in range(slots):
        fs = f_ref[s]
        xp = jnp.where(row == width - 1, rows_ref[0, s], pltpu.roll(fs, width - 1, 0))
        xm = jnp.where(row == 0, rows_ref[1, s], pltpu.roll(fs, 1, 0))
        yp = jnp.where(lane >= lanes - BS, spread(faces_ref[0, s], spread_y), pltpu.roll(fs, lanes - BS, 1))
        ym = jnp.where(lane < BS, spread(faces_ref[1, s], spread_y), pltpu.roll(fs, BS, 1))
        zp = jnp.where(lane % BS == BS - 1, spread(faces_ref[2, s], spread_z), pltpu.roll(fs, lanes - 1, 1))
        zm = jnp.where(lane % BS == 0, spread(faces_ref[3, s], spread_z), pltpu.roll(fs, 1, 1))
        borders = [
            row == width - 1,
            row == 0,
            lane >= lanes - BS,
            lane < BS,
            lane % BS == BS - 1,
            lane % BS == 0,
        ]
        total = diag_ref[s] * fs
        for d, beyond in enumerate([xp, xm, yp, ym, zp, zm]):
            base = 2 * (d * slots + s)
            active = jnp.where(borders[d], masks_ref[base + 1], masks_ref[base])
            total = total - bonds_ref[d, s] * active * beyond
        o_ref[s] = total


def stencil(field, bonds, masks, diag, rows, faces):
    vmem = pl.BlockSpec(memory_space=pltpu.VMEM)
    smem = pl.BlockSpec(memory_space=pltpu.SMEM)
    return pl.pallas_call(
        stencil_kernel,
        out_shape=jax.ShapeDtypeStruct(field.shape, jnp.float32),
        in_specs=[vmem, vmem, smem, vmem, vmem, vmem],
        out_specs=vmem,
    )(field, bonds, masks, diag, rows, faces)


def assemble(coarse_diag, couplings, strides):
    extent = coarse_diag.shape[0]
    matrix = jnp.diag(coarse_diag)
    for coupling, stride in zip(couplings, strides):
        banded = coupling[: extent - stride]
        matrix = matrix - jnp.diag(banded, stride) - jnp.diag(banded, -stride)
    return matrix


def on_device(source, uptake, conductance, occupancy, assignment):
    face_size = BS * BS
    slot_count = PATCH_X * PATCH_Y
    slab_index = lax.axis_index("grp")
    brick_index = lax.axis_index("brick")
    brick_count = lax.axis_size("brick")
    across = brick_count // 2
    peer_ids = jnp.arange(brick_count, dtype=jnp.int32)
    patch_index = assignment[brick_index]
    patch_row = patch_index // across
    patch_column = patch_index % across

    def owner_of(row_shift, column_shift):
        row_target = patch_row + row_shift
        column_target = patch_column + column_shift
        inside = (
            (row_target >= 0) & (row_target < 2) & (column_target >= 0) & (column_target < across)
        )
        holder = jnp.sum(jnp.where(assignment == row_target * across + column_target, peer_ids, 0))
        return jnp.where(inside, holder, -1)

    wanted = jnp.stack([owner_of(1, 0), owner_of(-1, 0), owner_of(0, 1), owner_of(0, -1)])
    padded = jnp.pad(occupancy, 1)
    window = lax.dynamic_slice(
        padded,
        (slab_index, patch_row * PATCH_X, patch_column * PATCH_Y),
        (3, PATCH_X + 2, PATCH_Y + 2),
    ).astype(jnp.float32)
    centre = window[1, 1:-1, 1:-1].reshape(slot_count)
    toward = [
        window[1, 2:, 1:-1],
        window[1, :-2, 1:-1],
        window[1, 1:-1, 2:],
        window[1, 1:-1, :-2],
        window[2, 1:-1, 1:-1],
        window[0, 1:-1, 1:-1],
    ]
    first_axis = lax.broadcasted_iota(jnp.int32, (1, BS, face_size), 1)
    flat_axis = lax.broadcasted_iota(jnp.int32, (1, BS, face_size), 2)
    second_axis = flat_axis // BS
    third_axis = flat_axis % BS
    cube_third = lax.broadcasted_iota(jnp.int32, (1, BS, BS, BS), 3)
    borders = [
        first_axis == BS - 1,
        first_axis == 0,
        second_axis == BS - 1,
        second_axis == 0,
        third_axis == BS - 1,
        third_axis == 0,
    ]
    bonds = conductance[0, 0]
    live_here = centre[:, None, None]
    effective = []
    for direction in range(6):
        neighbour_live = toward[direction].reshape(slot_count)[:, None, None]
        active = jnp.where(borders[direction], live_here * neighbour_live, live_here)
        effective.append(bonds[direction] * active)
    absorb = uptake[0, 0]
    diagonal = absorb
    for direction in range(6):
        diagonal = diagonal + effective[direction]

    masks = jnp.stack(
        [
            jnp.stack([centre, centre * toward[direction].reshape(slot_count)], axis=1)
            for direction in range(6)
        ]
    ).reshape(-1)

    lane_ids = jnp.arange(face_size, dtype=jnp.int32)[:, None]
    layer_ids = BS * jnp.arange(BS, dtype=jnp.int32)[None, :]
    picker = jnp.concatenate([lane_ids == layer_ids, lane_ids == layer_ids + BS - 1], axis=1)
    picker = picker.astype(jnp.float32)

    def side_faces(field):
        picked = jnp.dot(
            field.reshape(slot_count * BS, face_size), picker, precision=lax.Precision.HIGHEST
        )
        z = picked.reshape(slot_count, BS, 2, BS).transpose(2, 0, 1, 3)
        xy = jnp.concatenate(
            [
                field[:, 0, :],
                field[:, BS - 1, :],
                field[0, :, :BS].reshape(1, face_size),
                field[slot_count - 1, :, face_size - BS :].reshape(1, face_size),
            ]
        )
        return xy, z.reshape(2 * slot_count, face_size)

    def pick(landed, holder, fill):
        offset = lax.rem(brick_index - holder + brick_count, brick_count)
        got = lax.dynamic_index_in_dim(landed, offset, keepdims=False)
        return jnp.where(holder >= 0, got, fill)

    def halo(field, xy_land, z_land, fill):
        xplus = pick(xy_land, wanted[0], fill)
        xminus = pick(xy_land, wanted[1], fill)
        yplus = pick(xy_land, wanted[2], fill)
        yminus = pick(xy_land, wanted[3], fill)
        rows = jnp.stack([xplus[:slot_count], xminus[slot_count : 2 * slot_count]])[:, :, None, :]
        beyond_yplus = jnp.stack([field[1, :, :BS], yplus[2 * slot_count].reshape(BS, BS)])
        beyond_yminus = jnp.stack(
            [yminus[2 * slot_count + 1].reshape(BS, BS), field[0, :, face_size - BS :]]
        )
        above = jnp.where(slab_index < grp_count - 1, z_land[1, :slot_count], fill)
        below = jnp.where(slab_index > 0, z_land[0, slot_count:], fill)
        faces = jnp.stack(
            [
                beyond_yplus,
                beyond_yminus,
                above.reshape(slot_count, BS, BS),
                below.reshape(slot_count, BS, BS),
            ]
        )
        return rows, faces

    slot_ids = jnp.arange(slot_count)
    brick_first = slot_ids // PATCH_Y
    brick_second = slot_ids % PATCH_Y
    inside = [
        (brick_first < PATCH_X - 1).astype(jnp.float32),
        (brick_first > 0).astype(jnp.float32),
        (brick_second < PATCH_Y - 1).astype(jnp.float32),
        (brick_second > 0).astype(jnp.float32),
    ]
    face_sums = [
        jnp.sum(effective[0][:, BS - 1, :], axis=1),
        jnp.sum(effective[1][:, 0, :], axis=1),
        jnp.sum(effective[2][:, :, face_size - BS :], axis=(1, 2)),
        jnp.sum(effective[3][:, :, :BS], axis=(1, 2)),
        jnp.sum(jnp.where(borders[4], effective[4], 0.0), axis=(1, 2)),
        jnp.sum(jnp.where(borders[5], effective[5], 0.0), axis=(1, 2)),
    ]
    coarse_diag = jnp.sum(absorb, axis=(1, 2))
    for direction in range(4):
        coarse_diag = coarse_diag + face_sums[direction] * inside[direction]
    coarse_diag = coarse_diag + face_sums[4] + face_sums[5]
    grp_count = lax.axis_size("grp")
    grp_ids = jnp.arange(grp_count, dtype=jnp.int32)

    def slab_slot(values):
        here = (grp_ids == slab_index).astype(jnp.float32)
        return here[:, None, None] * values[None]

    forcing = source[0, 0] * live_here

    def as_tile(values):
        rows = -(-values.shape[0] // 128)
        rows = -(-rows // 8) * 8
        return jnp.pad(values, (0, rows * 128 - values.shape[0])).reshape(rows, 128)

    record = jnp.stack(
        [
            coarse_diag,
            face_sums[0] * inside[0],
            face_sums[2] * inside[2],
            face_sums[4],
            jnp.sum(forcing, axis=(1, 2)),
        ]
    )
    brick_here = (peer_ids == brick_index).astype(jnp.float32)
    spread = (brick_here[:, None, None, None] * slab_slot(record)[None]).reshape(-1)
    forcing_xy, forcing_z = side_faces(forcing)
    diagonal_xy, diagonal_z = side_faces(diagonal)
    summed, xy_land, z_land = exchange(
        as_tile(spread),
        jnp.concatenate([forcing_xy, diagonal_xy]),
        jnp.concatenate([forcing_z, diagonal_z]),
        2,
    )
    summed = summed.reshape(-1)[: spread.shape[0]]
    xy_rows = forcing_xy.shape[0]
    z_rows = forcing_z.shape[0]
    residual_halo = halo(forcing, xy_land[:, :xy_rows], z_land[:, :z_rows], 0.0)
    diagonal_halo = halo(diagonal, xy_land[:, xy_rows:], z_land[:, z_rows:], 1.0)
    gathered = lax.dynamic_index_in_dim(
        summed.reshape(brick_count, grp_count, 5, slot_count), brick_index, keepdims=False
    )
    columns = jnp.transpose(gathered, (1, 0, 2)).reshape(5, -1)
    matrix = assemble(columns[0], (columns[1], columns[2], columns[3]), (PATCH_Y, 1, slot_count))
    factor = jnp.linalg.cholesky(matrix)

    def coarse_solve(terms):
        middle = lax.linalg.triangular_solve(factor, terms[:, None], left_side=True, lower=True)
        result = lax.linalg.triangular_solve(
            factor, middle, left_side=True, lower=True, transpose_a=True
        )
        return lax.dynamic_slice_in_dim(result[:, 0], slab_index * slot_count, slot_count)

    def precondition(residual_field, field_halo, terms):
        smoothed = OMEGA * residual_field / diagonal
        smoothed_halo = [OMEGA * part / scale for part, scale in zip(field_halo, diagonal_halo)]
        applied = stencil(smoothed, bonds, masks, diagonal, *smoothed_halo)
        smoothed = smoothed + OMEGA * (residual_field - applied) / diagonal
        return smoothed + coarse_solve(terms)[:, None, None]

    def sum_and_share(product, field, with_sums):
        values = [jnp.sum(product)[None]]
        if with_sums:
            sums = slab_slot(jnp.sum(field, axis=(1, 2))[None])[:, 0]
            values.append((brick_here[:, None, None] * sums[None]).reshape(-1))
        packed = jnp.concatenate(values)
        xy, z = side_faces(field)
        total, xy_land, z_land = exchange(as_tile(packed), xy, z, 1)
        total = total.reshape(-1)[: packed.shape[0]]
        field_halo = halo(field, xy_land, z_land, 0.0)
        if not with_sums:
            return total[0], None, field_halo
        mine = lax.dynamic_index_in_dim(
            total[1:].reshape(brick_count, -1), brick_index, keepdims=False
        )
        return total[0], mine, field_halo

    terms = columns[4]
    solution_field = jnp.zeros_like(forcing)
    residual = forcing
    search = precondition(residual, residual_halo, terms)
    energy, _, search_halo = sum_and_share(residual * search, search, False)
    for iteration in range(ITERS):
        mapped = stencil(search, bonds, masks, diagonal, *search_halo)
        curvature, mapped_terms, mapped_halo = sum_and_share(search * mapped, mapped, True)
        step_size = energy / curvature
        solution_field = solution_field + step_size * search
        residual = residual - step_size * mapped
        if iteration + 1 < ITERS:
            residual_halo = [
                part - step_size * change for part, change in zip(residual_halo, mapped_halo)
            ]
            terms = terms - step_size * mapped_terms
            smoothed = precondition(residual, residual_halo, terms)
            renewed, _, smoothed_halo = sum_and_share(residual * smoothed, smoothed, False)
            search = smoothed + renewed / energy * search
            search_halo = [
                part + renewed / energy * old for part, old in zip(smoothed_halo, search_halo)
            ]
            energy = renewed
    return (solution_field[None, None], residual[None, None])


def solution(mesh):
    return jax.shard_map(
        on_device,
        mesh=mesh,
        in_specs=(
            P("grp", "brick", None, None, None),
            P("grp", "brick", None, None, None),
            P("grp", "brick", None, None, None, None),
            P(),
            P(),
        ),
        out_specs=(P("grp", "brick", None, None, None), P("grp", "brick", None, None, None)),
        check_vma=False,
    )
```

profile of v0, /device:TPU:0, one launch (start us, length us, event | category | flops | bytes accessed | tf_op | source)
XLA Modules:
  0.0 244.3 jit_solution(1227679002815813800)
XLA Ops:
  0.6 1.3 dynamic_slice.111
  4.6 0.8 fusion.80
  5.7 1.4 select_reduce_fusion.1
  7.2 2.6 %multiply_divide_fusion.2 = (f32[2,32,1024]{2,1,0:T(8,128)}, f32[2,32,1024]{2,1,0:T(8,128)S(1)}, f32[2,32,1024]{2,1,0:T(8,128)S(1)}, f32[2,32,1024]{2,1,0:T(8,12...) fusion(f32[2,32,1024]{2,1,0:T(8,128)S(1)} %get-tuple-element.198, f32[2]{0:T(128)S(1)} %get-tuple-element.200, ...), kind=kLoop, calls=%fused_computation.74 | loop fusion | flops 1310720 | bytes 3801208 | tf_op jit(solution)/shard_map/div | solution.py:364
  10.4 1.3 concatenate.122.xy_ref
  13.5 2.0 convolution_bitcast_fusion.6
  16.8 23.0 %shard_map.68 = (f32[16,128]{1,0:T(8,128)}, f32[8,12,1024]{2,1,0:T(8,128)}, f32[2,8,1024]{2,1,0:T(8,128)}) custom-call(f32[16,128]{1,0:T(8,128)} %pad_bitcast_fusion.x_ref, f32[12,1024]{1,0:T(8,128)} %concatenate.122.xy_ref, f32[8,1024]{1,0:T(8,128)} %pad_maximum_fusion.3.z_ref), custom_call_target="tpu_custom_call" | custom-call | tf_op jit(solution)/shard_map/pallas_call | solution.py:91
  39.8 1.3 copy.325
  48.0 3.3 %shard_map.69 = f32[2,32,1024]{2,1,0:T(8,128)} custom-call(f32[2,32,1024]{2,1,0:T(8,128)} %get-tuple-element.87.f_ref, f32[6,2,32,1024]{3,2,1,0:T(8,128)} %bitcast.455, f32[24]{0:T(128)} %reshape.1794.masks_ref, f32[2,32,1024]{2,1,0:T(8,128)} %copy-done, f32[2,2,1,1024]{3,2,1,0:T(1,128)} %copy.327.rows_ref, f32[4,2,32,32]{3,2,1,0:T(8,128)} %multiply_divide_fusion.4.faces_ref), custom_call_target="tpu_custom_call" | custom-call | tf_op jit(solution)/shard_map/pallas_call | solution.py:157
  52.7 2.9 %cholesky.19 = f32[32,32]{1,0:T(8,128)S(1)} custom-call(f32[32,32]{1,0:T(8,128)S(1)} %add_multiply_fusion), custom_call_target="Cholesky" | custom-call | tf_op jit(solution)/shard_map/jit(cholesky)/cholesky | solution.py:354
  57.0 2.4 custom-call.14
  60.0 1.7 multiply_reduce_fusion.5
  63.7 1.1 pad_bitcast_fusion.3.x_ref
  64.8 15.7 %shard_map.70 = (f32[8,128]{1,0:T(8,128)}, f32[8,6,1024]{2,1,0:T(8,128)}, f32[2,4,1024]{2,1,0:T(4,128)}) custom-call(f32[8,128]{1,0:T(8,128)} %pad_bitcast_fusion.3.x_ref, f32[6,1024]{1,0:T(8,128)} %pad_maximum_fusion.4.xy_ref, f32[4,1024]{1,0:T(4,128)} %reshape.1800.z_ref), custom_call_target="tpu_custom_call" | custom-call | tf_op jit(solution)/shard_map/pallas_call | solution.py:91
  80.5 1.1 copy.336
  81.8 0.8 slice_select_fusion.9
  84.1 3.2 %shard_map.71 = f32[2,32,1024]{2,1,0:T(8,128)} custom-call(f32[2,32,1024]{2,1,0:T(8,128)} %copy-done.6, f32[6,2,32,1024]{3,2,1,0:T(8,128)} %bitcast.456, f32[24]{0:T(128)} %reshape.1794.masks_ref, f32[2,32,1024]{2,1,0:T(8,128)} %copy-done, f32[2,2,1,1024]{3,2,1,0:T(1,128)} %copy.340.rows_ref, f32[4,2,32,32]{3,2,1,0:T(8,128)} %pad_maximum_fusion.2.faces_ref), custom_call_target="tpu_custom_call" | custom-call | tf_op jit(solution)/shard_map/pallas_call | solution.py:157
  87.3 1.5 convolution_bitcast_fusion.4
  89.5 0.8 fusion.136
  90.5 0.9 fusion.137
  92.1 1.8 multiply_reduce_fusion.4
  94.2 1.3 fusion.103.x_ref
  95.5 14.6 %shard_map.72 = (f32[8,128]{1,0:T(8,128)}, f32[8,6,1024]{2,1,0:T(8,128)}, f32[2,4,1024]{2,1,0:T(4,128)}) custom-call(f32[8,128]{1,0:T(8,128)} %fusion.103.x_ref, f32[6,1024]{1,0:T(8,128)} %pad_maximum_fusion.5.xy_ref, f32[4,1024]{1,0:T(4,128)} %reshape.1803.z_ref), custom_call_target="tpu_custom_call" | custom-call | tf_op jit(solution)/shard_map/pallas_call | solution.py:91
  110.0 1.1 copy.344
  111.3 0.8 slice_select_fusion.7
  112.2 1.2 slice.510
  113.5 1.2 slice.497
  117.4 0.8 multiply_divide_fusion.1
  118.1 3.5 %shard_map.73 = f32[2,32,1024]{2,1,0:T(8,128)} custom-call(f32[2,32,1024]{2,1,0:T(8,128)} %get-tuple-element.81.f_ref, f32[6,2,32,1024]{3,2,1,0:T(8,128)} %bitcast.457, f32[24]{0:T(128)} %reshape.1794.masks_ref, f32[2,32,1024]{2,1,0:T(8,128)} %copy-done, f32[2,2,1,1024]{3,2,1,0:T(1,128)} %copy.348.rows_ref, f32[4,2,32,32]{3,2,1,0:T(8,128)} %multiply_divide_fusion.3.faces_ref), custom_call_target="tpu_custom_call" | custom-call | tf_op jit(solution)/shard_map/pallas_call | solution.py:157
  121.6 0.8 slice.519
  122.8 1.7 multiply_reduce_fusion.3
  126.6 1.1 pad_bitcast_fusion.2.x_ref
  127.7 15.3 %shard_map.74 = (f32[8,128]{1,0:T(8,128)}, f32[8,6,1024]{2,1,0:T(8,128)}, f32[2,4,1024]{2,1,0:T(4,128)}) custom-call(f32[8,128]{1,0:T(8,128)} %pad_bitcast_fusion.2.x_ref, f32[6,1024]{1,0:T(8,128)} %pad_maximum_fusion.6.xy_ref, f32[4,1024]{1,0:T(4,128)} %reshape.1807.z_ref), custom_call_target="tpu_custom_call" | custom-call | tf_op jit(solution)/shard_map/pallas_call | solution.py:91
  143.0 1.1 copy.351
  144.3 0.8 slice_select_fusion.5
  145.2 1.3 slice.524
  150.0 3.3 %shard_map.75 = f32[2,32,1024]{2,1,0:T(8,128)} custom-call(f32[2,32,1024]{2,1,0:T(8,128)} %multiply_add_fusion.1.f_ref, f32[6,2,32,1024]{3,2,1,0:T(8,128)} %bitcast.458, f32[24]{0:T(128)} %reshape.1794.masks_ref, f32[2,32,1024]{2,1,0:T(8,128)} %copy-done, f32[2,2,1,1024]{3,2,1,0:T(1,128)} %fusion.58.rows_ref, f32[4,2,32,32]{3,2,1,0:T(8,128)} %maximum_add_fusion.faces_ref), custom_call_target="tpu_custom_call" | custom-call | tf_op jit(solution)/shard_map/pallas_call | solution.py:157
  153.2 1.5 convolution_bitcast_fusion.2
  155.4 0.8 fusion.132
  156.4 0.9 fusion.133
  158.0 1.7 multiply_reduce_fusion.2
  160.0 1.3 fusion.102.x_ref
  161.3 14.4 %shard_map.76 = (f32[8,128]{1,0:T(8,128)}, f32[8,6,1024]{2,1,0:T(8,128)}, f32[2,4,1024]{2,1,0:T(4,128)}) custom-call(f32[8,128]{1,0:T(8,128)} %fusion.102.x_ref, f32[6,1024]{1,0:T(8,128)} %pad_maximum_fusion.7.xy_ref, f32[4,1024]{1,0:T(4,128)} %reshape.1810.z_ref), custom_call_target="tpu_custom_call" | custom-call | tf_op jit(solution)/shard_map/pallas_call | solution.py:91
  175.8 1.1 copy.361
  177.0 0.8 slice_select_fusion.3
  178.0 1.2 slice.537
  182.0 0.8 multiply_divide_fusion
  182.7 3.3 %shard_map.77 = f32[2,32,1024]{2,1,0:T(8,128)} custom-call(f32[2,32,1024]{2,1,0:T(8,128)} %get-tuple-element.77.f_ref, f32[6,2,32,1024]{3,2,1,0:T(8,128)} %bitcast.459, f32[24]{0:T(128)} %reshape.1794.masks_ref, f32[2,32,1024]{2,1,0:T(8,128)} %copy-done, f32[2,2,1,1024]{3,2,1,0:T(1,128)} %copy.365.rows_ref, f32[4,2,32,32]{3,2,1,0:T(8,128)} %fusion.41.faces_ref), custom_call_target="tpu_custom_call" | custom-call | tf_op jit(solution)/shard_map/pallas_call | solution.py:157
  186.0 0.7 slice.546
  187.2 1.8 multiply_reduce_fusion.1
  191.1 1.3 pad_bitcast_fusion.1.x_ref
  192.3 15.3 %shard_map.78 = (f32[8,128]{1,0:T(8,128)}, f32[8,6,1024]{2,1,0:T(8,128)}, f32[2,4,1024]{2,1,0:T(4,128)}) custom-call(f32[8,128]{1,0:T(8,128)} %pad_bitcast_fusion.1.x_ref, f32[6,1024]{1,0:T(8,128)} %pad_maximum_fusion.8.xy_ref, f32[4,1024]{1,0:T(4,128)} %reshape.1814.z_ref), custom_call_target="tpu_custom_call" | custom-call | tf_op jit(solution)/shard_map/pallas_call | solution.py:91
  207.6 1.1 copy.368
  208.9 0.8 slice_select_fusion.1
  209.8 1.3 slice.551
  214.6 3.3 %shard_map.79 = f32[2,32,1024]{2,1,0:T(8,128)} custom-call(f32[2,32,1024]{2,1,0:T(8,128)} %multiply_add_fusion.f_ref, f32[6,2,32,1024]{3,2,1,0:T(8,128)} %bitcast.460, f32[24]{0:T(128)} %reshape.1794.masks_ref, f32[2,32,1024]{2,1,0:T(8,128)} %copy-done, f32[2,2,1,1024]{3,2,1,0:T(1,128)} %copy_add_fusion.rows_ref, f32[4,2,32,32]{3,2,1,0:T(8,128)} %maximum_add_fusion.1.faces_ref), custom_call_target="tpu_custom_call" | custom-call | tf_op jit(solution)/shard_map/pallas_call | solution.py:157
  217.9 1.5 convolution_bitcast_fusion
  220.1 0.8 fusion.129
  221.0 0.9 fusion.128
  222.6 1.7 multiply_reduce_fusion
  224.6 1.3 fusion.101.x_ref
  225.9 14.4 %shard_map.80 = (f32[8,128]{1,0:T(8,128)}, f32[8,6,1024]{2,1,0:T(8,128)}, f32[2,4,1024]{2,1,0:T(4,128)}) custom-call(f32[8,128]{1,0:T(8,128)} %fusion.101.x_ref, f32[6,1024]{1,0:T(8,128)} %pad_maximum_fusion.9.xy_ref, f32[4,1024]{1,0:T(4,128)} %reshape.1817.z_ref), custom_call_target="tpu_custom_call" | custom-call | tf_op jit(solution)/shard_map/pallas_call | solution.py:91
  240.3 1.2 slice.564
  243.6 0.8 add_bitcast_fusion
  (272 shorter events, 34.7 us)
Async XLA Ops:
  0.6 6.6 %copy-start.13 = (f32[1,1,2,32,1024]{4,3,2,1,0:T(8,128)S(1)}, f32[1,1,2,32,1024]{4,3,2,1,0:T(8,128)}, u32[]{:S(2)}) copy-start(f32[1,1,2,32,1024]{4,3,2,1,0:T(8,128)} %param.10) | copy-start | bytes 786436
  9.8 5.7 %copy-start = (f32[2,32,1024]{2,1,0:T(8,128)}, f32[2,32,1024]{2,1,0:T(8,128)S(1)}, u32[]{:S(2)}) copy-start(f32[2,32,1024]{2,1,0:T(8,128)S(1)} %get-tuple-element.88.diag_ref) | copy-start | bytes 786436
  12.5 3.1 %copy-start.14 = (f32[1,1,2,32,1024]{4,3,2,1,0:T(8,128)S(1)}, f32[1,1,2,32,1024]{4,3,2,1,0:T(8,128)}, u32[]{:S(2)}) copy-start(f32[1,1,2,32,1024]{4,3,2,1,0:T(8,128)} %param.9) | copy-start | bytes 786436
  15.5 25.7 %copy-start.17 = (s32[8]{0:T(128)S(1)}, s32[8]{0:T(128)}, u32[]{:S(2)}) copy-start(s32[8]{0:T(128)} %param.13) | copy-start | bytes 100
  39.8 3.8 %copy-start.15 = (f32[2,8,1024]{2,1,0:T(8,128)S(1)}, f32[2,8,1024]{2,1,0:T(8,128)}, u32[]{:S(2)}) copy-start(f32[2,8,1024]{2,1,0:T(8,128)} %get-tuple-element.24) | copy-start | bytes 196612
  44.0 7.3 %copy-start.16 = (f32[16,128]{1,0:T(8,128)S(1)}, f32[16,128]{1,0:T(8,128)}, u32[]{:S(2)}) copy-start(f32[16,128]{1,0:T(8,128)} %get-tuple-element.25) | copy-start | bytes 24580
  48.0 3.8 %copy-start.18 = (pred[32]{0:T(512)(128)(4,1)S(1)}, pred[32]{0:T(512)(128)(4,1)}, u32[]{:S(2)}) copy-start(pred[32]{0:T(512)(128)(4,1)} %constant.267.clone.1) | copy-start | bytes 100
  48.0 12.0 %copy-start.1 = (f32[2,32,1024]{2,1,0:T(8,128)S(1)}, f32[2,32,1024]{2,1,0:T(8,128)}, u32[]{:S(2)}) copy-start(f32[2,32,1024]{2,1,0:T(8,128)} %copy-done) | copy-start | bytes 786436
  61.6 22.4 %copy-start.6 = (f32[2,32,1024]{2,1,0:T(8,128)}, f32[2,32,1024]{2,1,0:T(8,128)S(1)}, u32[]{:S(2)}) copy-start(f32[2,32,1024]{2,1,0:T(8,128)S(1)} %get-tuple-element.84.f_ref) | copy-start | bytes 786436
  87.3 30.1 %copy-start.2 = (f32[2,32,1024]{2,1,0:T(8,128)S(1)}, f32[2,32,1024]{2,1,0:T(8,128)}, u32[]{:S(2)}) copy-start(f32[2,32,1024]{2,1,0:T(8,128)} %copy-done) | copy-start | bytes 786436
  87.3 30.1 %copy-start.10 = (f32[2,32,1024]{2,1,0:T(8,128)S(1)}, f32[2,32,1024]{2,1,0:T(8,128)}, u32[]{:S(2)}) copy-start(f32[2,32,1024]{2,1,0:T(8,128)} %shard_map.71) | copy-start | bytes 786436
  118.1 4.7 %copy-start.3 = (f32[2,32,1024]{2,1,0:T(8,128)S(1)}, f32[2,32,1024]{2,1,0:T(8,128)}, u32[]{:S(2)}) copy-start(f32[2,32,1024]{2,1,0:T(8,128)} %copy-done) | copy-start | bytes 786436
  122.8 26.4 %copy-start.7 = (f32[2,32,1024]{2,1,0:T(8,128)S(1)}, f32[2,32,1024]{2,1,0:T(8,128)}, u32[]{:S(2)}) copy-start(f32[2,32,1024]{2,1,0:T(8,128)} %copy-done.6) | copy-start | bytes 786436
  149.9 8.0 %copy-start.8 = (f32[2,32,1024]{2,1,0:T(8,128)S(1)}, f32[2,32,1024]{2,1,0:T(8,128)}, u32[]{:S(2)}) copy-start(f32[2,32,1024]{2,1,0:T(8,128)} %multiply_add_fusion.1.f_ref) | copy-start | bytes 786436
  153.2 28.7 %copy-start.4 = (f32[2,32,1024]{2,1,0:T(8,128)S(1)}, f32[2,32,1024]{2,1,0:T(8,128)}, u32[]{:S(2)}) copy-start(f32[2,32,1024]{2,1,0:T(8,128)} %copy-done) | copy-start | bytes 786436
  153.2 28.7 %copy-start.9 = (f32[2,32,1024]{2,1,0:T(8,128)S(1)}, f32[2,32,1024]{2,1,0:T(8,128)}, u32[]{:S(2)}) copy-start(f32[2,32,1024]{2,1,0:T(8,128)} %shard_map.75) | copy-start | bytes 786436
  182.7 4.5 %copy-start.5 = (f32[2,32,1024]{2,1,0:T(8,128)S(1)}, f32[2,32,1024]{2,1,0:T(8,128)}, u32[]{:S(2)}) copy-start(f32[2,32,1024]{2,1,0:T(8,128)} %copy-done) | copy-start | bytes 786436
  214.6 8.0 %copy-start.12 = (f32[2,32,1024]{2,1,0:T(8,128)S(1)}, f32[2,32,1024]{2,1,0:T(8,128)}, u32[]{:S(2)}) copy-start(f32[2,32,1024]{2,1,0:T(8,128)} %multiply_add_fusion.f_ref) | copy-start | bytes 786436
  217.9 25.0 %copy-start.11 = (f32[2,32,1024]{2,1,0:T(8,128)S(1)}, f32[2,32,1024]{2,1,0:T(8,128)}, u32[]{:S(2)}) copy-start(f32[2,32,1024]{2,1,0:T(8,128)} %shard_map.79) | copy-start | bytes 786436
where the time goes:
time: 247 us; the launch traced here: 244 us
  Pallas kernels  133 us (54%)
  other arithmetic  47 us (19%)
  local copies, waits for them, and re-layouts  42.3 us (17%)
  between operations  13.5 us (5%)
  matrix products  9.01 us (4%)
    pallas_call x7, Pallas kernels, exchange(): pl.pallas_call(exchange_kernel, out_shape=(jax.ShapeDtypeStruct(tile.shap...  113 us
    pallas_call x6, Pallas kernels, stencil(): pl.pallas_call(stencil_kernel, out_shape=jax.ShapeDtypeStruct(field.shape...  19.8 us
    reduce_sum x6, other arithmetic, sum_and_share(): values = [jnp.sum(product)[None]]  10.5 us
    dot_general x8, matrix products, side_faces(): jnp.dot(field.reshape(slot_count * BS, face_size), picker, precision=lax....  8.19 us
    pallas_call x6, local copies, waits for them, and re-layouts, exchange(): pl.pallas_call(exchange_kernel, out_shape=(jax.ShapeDtypeStruct(tile.shap...  6.65 us

commit v1 on v0

--- a/solution.py
+++ b/solution.py
@@ -115,7 +115,9 @@
     )(tile, xy, z)
 
 
-def stencil_kernel(f_ref, bonds_ref, masks_ref, diag_ref, rows_ref, faces_ref, o_ref):
+def stencil_kernel(
+    coef_ref, f_ref, bonds_ref, masks_ref, diag_ref, rows_ref, faces_ref, o_ref, part_ref, *, smooth
+):
     slots, width, lanes = f_ref.shape
     row = lax.broadcasted_iota(jnp.int32, (width, lanes), 0)
     lane = lax.broadcasted_iota(jnp.int32, (width, lanes), 1)
@@ -127,39 +129,63 @@
     def spread(face, table):
         return jnp.dot(face, table, precision=lax.Precision.HIGHEST, preferred_element_type=jnp.float32)
 
+    borders = [
+        row == width - 1,
+        row == 0,
+        lane >= lanes - BS,
+        lane < BS,
+        lane % BS == BS - 1,
+        lane % BS == 0,
+    ]
+    dot = jnp.float32(0.0)
     for s in range(slots):
-        fs = f_ref[s]
+        ds = diag_ref[s]
+        if smooth:
+            rs = f_ref[s]
+            fs = OMEGA * rs / ds
+        else:
+            fs = f_ref[s]
         xp = jnp.where(row == width - 1, rows_ref[0, s], pltpu.roll(fs, width - 1, 0))
         xm = jnp.where(row == 0, rows_ref[1, s], pltpu.roll(fs, 1, 0))
         yp = jnp.where(lane >= lanes - BS, spread(faces_ref[0, s], spread_y), pltpu.roll(fs, lanes - BS, 1))
         ym = jnp.where(lane < BS, spread(faces_ref[1, s], spread_y), pltpu.roll(fs, BS, 1))
         zp = jnp.where(lane % BS == BS - 1, spread(faces_ref[2, s], spread_z), pltpu.roll(fs, lanes - 1, 1))
         zm = jnp.where(lane % BS == 0, spread(faces_ref[3, s], spread_z), pltpu.roll(fs, 1, 1))
-        borders = [
-            row == width - 1,
-            row == 0,
-            lane >= lanes - BS,
-            lane < BS,
-            lane % BS == BS - 1,
-            lane % BS == 0,
-        ]
-        total = diag_ref[s] * fs
+        total = ds * fs
         for d, beyond in enumerate([xp, xm, yp, ym, zp, zm]):
             base = 2 * (d * slots + s)
             active = jnp.where(borders[d], masks_ref[base + 1], masks_ref[base])
             total = total - bonds_ref[d, s] * active * beyond
+        if smooth:
+            total = fs + OMEGA * (rs - total) / ds
+            total = total + coef_ref[s]
+            dot = dot + jnp.sum(rs * total)
+        else:
+            dot = dot + jnp.sum(fs * total)
+            part_ref[1 + s] = jnp.sum(total)
         o_ref[s] = total
-
-
-def stencil(field, bonds, masks, diag, rows, faces):
+    part_ref[0] = dot
+    if smooth:
+        for s in range(slots):
+            part_ref[1 + s] = jnp.float32(0.0)
+
+
+def stencil(field, bonds, masks, diag, rows, faces, coef=None):
+    slots = field.shape[0]
+    smooth = coef is not None
+    if coef is None:
+        coef = jnp.zeros((slots,), jnp.float32)
     vmem = pl.BlockSpec(memory_space=pltpu.VMEM)
     smem = pl.BlockSpec(memory_space=pltpu.SMEM)
     return pl.pallas_call(
-        stencil_kernel,
-        out_shape=jax.ShapeDtypeStruct(field.shape, jnp.float32),
-        in_specs=[vmem, vmem, smem, vmem, vmem, vmem],
-        out_specs=vmem,
-    )(field, bonds, masks, diag, rows, faces)
+        functools.partial(stencil_kernel, smooth=smooth),
+        out_shape=(
+            jax.ShapeDtypeStruct(field.shape, jnp.float32),
+            jax.ShapeDtypeStruct((1 + slots,), jnp.float32),
+        ),
+        in_specs=[smem, vmem, vmem, smem, vmem, vmem, vmem],
+        out_specs=(vmem, smem),
+    )(coef, field, bonds, masks, diag, rows, faces)
 
 
 def assemble(coarse_diag, couplings, strides):
@@ -361,16 +387,15 @@
         return lax.dynamic_slice_in_dim(result[:, 0], slab_index * slot_count, slot_count)
 
     def precondition(residual_field, field_halo, terms):
-        smoothed = OMEGA * residual_field / diagonal
         smoothed_halo = [OMEGA * part / scale for part, scale in zip(field_halo, diagonal_halo)]
-        applied = stencil(smoothed, bonds, masks, diagonal, *smoothed_halo)
-        smoothed = smoothed + OMEGA * (residual_field - applied) / diagonal
-        return smoothed + coarse_solve(terms)[:, None, None]
-
-    def sum_and_share(product, field, with_sums):
-        values = [jnp.sum(product)[None]]
+        return stencil(
+            residual_field, bonds, masks, diagonal, *smoothed_halo, coef=coarse_solve(terms)
+        )
+
+    def sum_and_share(part, field, with_sums):
+        values = [part[:1]]
         if with_sums:
-            sums = slab_slot(jnp.sum(field, axis=(1, 2))[None])[:, 0]
+            sums = slab_slot(part[1:][None])[:, 0]
             values.append((brick_here[:, None, None] * sums[None]).reshape(-1))
         packed = jnp.concatenate(values)
         xy, z = side_faces(field)
@@ -387,11 +412,11 @@
     terms = columns[4]
     solution_field = jnp.zeros_like(forcing)
     residual = forcing
-    search = precondition(residual, residual_halo, terms)
-    energy, _, search_halo = sum_and_share(residual * search, search, False)
+    search, part = precondition(residual, residual_halo, terms)
+    energy, _, search_halo = sum_and_share(part, search, False)
     for iteration in range(ITERS):
-        mapped = stencil(search, bonds, masks, diagonal, *search_halo)
-        curvature, mapped_terms, mapped_halo = sum_and_share(search * mapped, mapped, True)
+        mapped, part = stencil(search, bonds, masks, diagonal, *search_halo)
+        curvature, mapped_terms, mapped_halo = sum_and_share(part, mapped, True)
         step_size = energy / curvature
         solution_field = solution_field + step_size * search
         residual = residual - step_size * mapped
@@ -400,8 +425,8 @@
                 part - step_size * change for part, change in zip(residual_halo, mapped_halo)
             ]
             terms = terms - step_size * mapped_terms
-            smoothed = precondition(residual, residual_halo, terms)
-            renewed, _, smoothed_halo = sum_and_share(residual * smoothed, smoothed, False)
+            smoothed, part = precondition(residual, residual_halo, terms)
+            renewed, _, smoothed_halo = sum_and_share(part, smoothed, False)
             search = smoothed + renewed / energy * search
             search_halo = [
                 part + renewed / energy * old for part, old in zip(smoothed_halo, search_halo)

time: 247 us -> 250 us (1.012)
  other arithmetic: 47 us -> 35.8 us
  local copies, waits for them, and re-layouts: 42.3 us -> 53.5 us
  matrix products: 9.01 us -> 11.9 us
    reduce_sum x7 -> x1, other arithmetic: 11.9 us -> 0.29 us  [on_device(): jnp.sum(forcing, axis=(1, 2))]
    pallas_call x0 -> x6, local copies, waits for them, and re-layouts: none -> 6.95 us  [stencil(): pl.pallas_call(functools.partial(stencil_kernel, smooth=smooth), out_shap...]
    div x3 -> x0, other arithmetic: 4.11 us -> none  [precondition(): smoothed = OMEGA * residual_field / diagonal]
    dot_general x8, matrix products: 8.19 us -> 11.1 us  [side_faces(): jnp.dot(field.reshape(slot_count * BS, face_size), picker, precision=lax....]
where the time goes in v1:
time: 250 us; the launch traced here: 248 us
  Pallas kernels  133 us (53%)
  local copies, waits for them, and re-layouts  53.5 us (21%)
  other arithmetic  35.8 us (14%)
  between operations  13.6 us (5%)
  matrix products  11.9 us (5%)
    pallas_call x7, Pallas kernels, exchange(): pl.pallas_call(exchange_kernel, out_shape=(jax.ShapeDtypeStruct(tile.shap...  113 us
    pallas_call x6, Pallas kernels, stencil(): pl.pallas_call(functools.partial(stencil_kernel, smooth=smooth), out_shap...  20 us
    dot_general x8, matrix products, side_faces(): jnp.dot(field.reshape(slot_count * BS, face_size), picker, precision=lax....  11.1 us
    pallas_call x6, local copies, waits for them, and re-layouts, stencil(): pl.pallas_call(functools.partial(stencil_kernel, smooth=smooth), out_shap...  6.95 us
    pallas_call x6, local copies, waits for them, and re-layouts, exchange(): pl.pallas_call(exchange_kernel, out_shape=(jax.ShapeDtypeStruct(tile.shap...  6.67 us

profile of v1, /device:TPU:0, one launch (start us, length us, event | category | flops | bytes accessed | tf_op | source)
XLA Modules:
  0.0 247.5 jit_solution(18341236726624368816)
XLA Ops:
  0.7 1.2 dynamic_slice.117
  4.6 1.4 fusion.110
  8.6 1.1 reduce_sum.122
  9.8 0.8 fusion.80
  12.4 2.2 convolution_bitcast_fusion.6
  17.9 1.3 concatenate.122.xy_ref
  20.1 23.0 %shard_map.68 = (f32[16,128]{1,0:T(8,128)}, f32[8,12,1024]{2,1,0:T(8,128)}, f32[2,8,1024]{2,1,0:T(8,128)}) custom-call(f32[16,128]{1,0:T(8,128)} %pad_bitcast_fusion.x_ref, f32[12,1024]{1,0:T(8,128)} %concatenate.122.xy_ref, f32[8,1024]{1,0:T(8,128)} %pad_maximum_fusion.3.z_ref), custom_call_target="tpu_custom_call" | custom-call | tf_op jit(solution)/shard_map/pallas_call | solution.py:91
  43.1 0.9 slice_select_fusion.11
  44.3 1.3 copy.346
  49.1 2.9 %cholesky.19 = f32[32,32]{1,0:T(8,128)S(1)} custom-call(f32[32,32]{1,0:T(8,128)S(1)} %add_multiply_fusion), custom_call_target="Cholesky" | custom-call | tf_op jit(solution)/shard_map/jit(cholesky)/cholesky | solution.py:380
  53.5 2.4 custom-call.14
  56.9 3.3 %shard_map.69 = (f32[2,32,1024]{2,1,0:T(8,128)}, f32[3]{0:T(128)}) custom-call(f32[2]{0:T(128)} %fusion.112.coef_ref, f32[2,32,1024]{2,1,0:T(8,128)} %copy-done.5, f32[6,2,32,1024]{3,2,1,0:T(8,128)} %bitcast.440, f32[24]{0:T(128)} %reshape.1792.masks_ref, f32[2,32,1024]{2,1,0:T(8,128)} %copy-done.1, f32[2,2,1,1024]{3,2,1,0:T(1,128)} %copy.348.rows_ref, ...), custom_call_target="tpu_custom_call" | custom-call | tf_op jit(solution)/shard_map/pallas_call | solution.py:180
  60.2 1.2 pad_bitcast_fusion.3.x_ref
  61.4 1.4 convolution_bitcast_fusion.5
  63.5 0.8 fusion.132
  64.5 1.2 copy.349
  66.3 15.7 %shard_map.70 = (f32[8,128]{1,0:T(8,128)}, f32[8,6,1024]{2,1,0:T(8,128)}, f32[2,4,1024]{2,1,0:T(4,128)}) custom-call(f32[8,128]{1,0:T(8,128)} %pad_bitcast_fusion.3.x_ref, f32[6,1024]{1,0:T(8,128)} %pad_maximum_fusion.4.xy_ref, f32[4,1024]{1,0:T(4,128)} %reshape.1794.z_ref), custom_call_target="tpu_custom_call" | custom-call | tf_op jit(solution)/shard_map/pallas_call | solution.py:91
  82.0 1.2 slice.525
  84.2 1.1 copy.352
  87.3 3.3 %shard_map.71 = (f32[2,32,1024]{2,1,0:T(8,128)}, f32[3]{0:T(128)}) custom-call(f32[2]{0:T(128)} %broadcast_16_coef_ref.2.coef_ref, f32[2,32,1024]{2,1,0:T(8,128)} %get-tuple-element.39.f_ref, f32[6,2,32,1024]{3,2,1,0:T(8,128)} %bitcast.441, f32[24]{0:T(128)} %reshape.1792.masks_ref, f32[2,32,1024]{2,1,0:T(8,128)} %copy-done.1, ...), custom_call_target="tpu_custom_call" | custom-call | tf_op jit(solution)/shard_map/pallas_call | solution.py:180
  90.7 0.8 slice.535
  91.7 1.3 fusion.103.x_ref
  93.1 1.4 convolution_bitcast_fusion.4
  95.2 0.8 fusion.131
  96.2 1.2 copy.357
  98.0 14.5 %shard_map.72 = (f32[8,128]{1,0:T(8,128)}, f32[8,6,1024]{2,1,0:T(8,128)}, f32[2,4,1024]{2,1,0:T(4,128)}) custom-call(f32[8,128]{1,0:T(8,128)} %fusion.103.x_ref, f32[6,1024]{1,0:T(8,128)} %pad_maximum_fusion.5.xy_ref, f32[4,1024]{1,0:T(4,128)} %reshape.1797.z_ref), custom_call_target="tpu_custom_call" | custom-call | tf_op jit(solution)/shard_map/pallas_call | solution.py:91
  112.5 1.2 slice.540
  115.8 0.8 slice.541
  118.5 1.1 copy.360
  121.2 3.5 %shard_map.73 = (f32[2,32,1024]{2,1,0:T(8,128)}, f32[3]{0:T(128)}) custom-call(f32[2]{0:T(128)} %fusion.116.coef_ref, f32[2,32,1024]{2,1,0:T(8,128)} %multiply_subtract_fusion.1.f_ref, f32[6,2,32,1024]{3,2,1,0:T(8,128)} %bitcast.442, f32[24]{0:T(128)} %reshape.1792.masks_ref, f32[2,32,1024]{2,1,0:T(8,128)} %copy-done.1, f32[2,2,1,1024]{3,2,1,0:T(1,128)} %copy.364.rows_ref, ...), custom_call_target="tpu_custom_call" | custom-call | tf_op jit(solution)/shard_map/pallas_call | solution.py:180
  124.7 1.2 pad_bitcast_fusion.2.x_ref
  125.9 1.4 convolution_bitcast_fusion.3
  128.0 0.8 fusion.130
  129.0 1.2 copy.365
  130.8 15.3 %shard_map.74 = (f32[8,128]{1,0:T(8,128)}, f32[8,6,1024]{2,1,0:T(8,128)}, f32[2,4,1024]{2,1,0:T(4,128)}) custom-call(f32[8,128]{1,0:T(8,128)} %pad_bitcast_fusion.2.x_ref, f32[6,1024]{1,0:T(8,128)} %pad_maximum_fusion.6.xy_ref, f32[4,1024]{1,0:T(4,128)} %reshape.1801.z_ref), custom_call_target="tpu_custom_call" | custom-call | tf_op jit(solution)/shard_map/pallas_call | solution.py:91
  146.1 1.3 slice.555
  150.4 1.1 copy.368
  153.0 3.3 %shard_map.75 = (f32[2,32,1024]{2,1,0:T(8,128)}, f32[3]{0:T(128)}) custom-call(f32[2]{0:T(128)} %broadcast_16_coef_ref.2.coef_ref, f32[2,32,1024]{2,1,0:T(8,128)} %multiply_add_fusion.1.f_ref, f32[6,2,32,1024]{3,2,1,0:T(8,128)} %bitcast.443, f32[24]{0:T(128)} %reshape.1792.masks_ref, f32[2,32,1024]{2,1,0:T(8,128)} %copy-done.1, ...), custom_call_target="tpu_custom_call" | custom-call | tf_op jit(solution)/shard_map/pallas_call | solution.py:180
  156.4 0.8 slice.565
  157.5 1.3 fusion.102.x_ref
  158.7 1.4 convolution_bitcast_fusion.2
  160.8 0.8 fusion.129
  161.9 1.2 copy.375
  163.6 14.4 %shard_map.76 = (f32[8,128]{1,0:T(8,128)}, f32[8,6,1024]{2,1,0:T(8,128)}, f32[2,4,1024]{2,1,0:T(4,128)}) custom-call(f32[8,128]{1,0:T(8,128)} %fusion.102.x_ref, f32[6,1024]{1,0:T(8,128)} %pad_maximum_fusion.7.xy_ref, f32[4,1024]{1,0:T(4,128)} %reshape.1804.z_ref), custom_call_target="tpu_custom_call" | custom-call | tf_op jit(solution)/shard_map/pallas_call | solution.py:91
  178.1 1.3 slice.570
  181.5 0.8 slice.571
  184.1 1.1 copy.378
  186.8 3.3 %shard_map.77 = (f32[2,32,1024]{2,1,0:T(8,128)}, f32[3]{0:T(128)}) custom-call(f32[2]{0:T(128)} %fusion.121.coef_ref, f32[2,32,1024]{2,1,0:T(8,128)} %multiply_subtract_fusion.f_ref, f32[6,2,32,1024]{3,2,1,0:T(8,128)} %bitcast.444, f32[24]{0:T(128)} %reshape.1792.masks_ref, f32[2,32,1024]{2,1,0:T(8,128)} %copy-done.1, f32[2,2,1,1024]{3,2,1,0:T(1,128)} %copy.382.rows_ref, ...), custom_call_target="tpu_custom_call" | custom-call | tf_op jit(solution)/shard_map/pallas_call | solution.py:180
  190.2 1.2 pad_bitcast_fusion.1.x_ref
  191.4 1.4 convolution_bitcast_fusion.1
  193.5 0.8 fusion.128
  194.5 1.2 copy.383
  196.3 15.3 %shard_map.78 = (f32[8,128]{1,0:T(8,128)}, f32[8,6,1024]{2,1,0:T(8,128)}, f32[2,4,1024]{2,1,0:T(4,128)}) custom-call(f32[8,128]{1,0:T(8,128)} %pad_bitcast_fusion.1.x_ref, f32[6,1024]{1,0:T(8,128)} %pad_maximum_fusion.8.xy_ref, f32[4,1024]{1,0:T(4,128)} %reshape.1808.z_ref), custom_call_target="tpu_custom_call" | custom-call | tf_op jit(solution)/shard_map/pallas_call | solution.py:91
  211.6 1.2 slice.585
  214.1 0.7 slice_select_fusion.1
  215.1 1.1 copy.386
  218.5 3.3 %shard_map.79 = (f32[2,32,1024]{2,1,0:T(8,128)}, f32[3]{0:T(128)}) custom-call(f32[2]{0:T(128)} %broadcast_16_coef_ref.2.coef_ref, f32[2,32,1024]{2,1,0:T(8,128)} %multiply_add_fusion.f_ref, f32[6,2,32,1024]{3,2,1,0:T(8,128)} %bitcast.445, f32[24]{0:T(128)} %reshape.1792.masks_ref, f32[2,32,1024]{2,1,0:T(8,128)} %copy-done.1, ...), custom_call_target="tpu_custom_call" | custom-call | tf_op jit(solution)/shard_map/pallas_call | solution.py:180
  221.8 1.4 convolution_bitcast_fusion
  224.8 0.8 fusion.127
  225.9 1.3 fusion.101.x_ref
  227.2 1.2 copy.391
  229.0 14.4 %shard_map.80 = (f32[8,128]{1,0:T(8,128)}, f32[8,6,1024]{2,1,0:T(8,128)}, f32[2,4,1024]{2,1,0:T(4,128)}) custom-call(f32[8,128]{1,0:T(8,128)} %fusion.101.x_ref, f32[6,1024]{1,0:T(8,128)} %pad_maximum_fusion.9.xy_ref, f32[4,1024]{1,0:T(4,128)} %reshape.1811.z_ref), custom_call_target="tpu_custom_call" | custom-call | tf_op jit(solution)/shard_map/pallas_call | solution.py:91
  243.5 1.2 slice.600
  246.0 0.8 add_bitcast_fusion
  (260 shorter events, 40.5 us)
Async XLA Ops:
  8.6 6.1 %copy-start.13 = (f32[1,1,2,32,1024]{4,3,2,1,0:T(8,128)S(1)}, f32[1,1,2,32,1024]{4,3,2,1,0:T(8,128)}, u32[]{:S(2)}) copy-start(f32[1,1,2,32,1024]{4,3,2,1,0:T(8,128)} %param.9) | copy-start | bytes 786436
  12.4 3.5 %copy-start = (f32[1,1,6,2,32,1024]{5,4,3,2,1,0:T(8,128)S(1)}, f32[1,1,6,2,32,1024]{5,4,3,2,1,0:T(8,128)}, u32[]{:S(2)}) copy-start(f32[1,1,6,2,32,1024]{5,4,3,2,1,0:T(8,128)} %param.11) | copy-start | bytes 4718596
  14.6 1.9 copy-start.14
  16.2 0.7 copy-start.5
  17.0 28.7 %copy-start.1 = (f32[2,32,1024]{2,1,0:T(8,128)}, f32[2,32,1024]{2,1,0:T(8,128)S(1)}, u32[]{:S(2)}) copy-start(f32[2,32,1024]{2,1,0:T(8,128)S(1)} %get-tuple-element.93.diag_ref) | copy-start | bytes 786436
  43.1 4.4 %copy-start.15 = (f32[16,128]{1,0:T(8,128)S(1)}, f32[16,128]{1,0:T(8,128)}, u32[]{:S(2)}) copy-start(f32[16,128]{1,0:T(8,128)} %get-tuple-element.35) | copy-start | bytes 24580
  44.3 4.5 %copy-start.16 = (pred[32]{0:T(512)(128)(4,1)S(1)}, pred[32]{0:T(512)(128)(4,1)}, u32[]{:S(2)}) copy-start(pred[32]{0:T(512)(128)(4,1)} %constant.263.clone.1) | copy-start | bytes 100
  87.3 27.8 %copy-start.6 = (f32[2,32,1024]{2,1,0:T(8,128)S(1)}, f32[2,32,1024]{2,1,0:T(8,128)}, u32[]{:S(2)}) copy-start(f32[2,32,1024]{2,1,0:T(8,128)} %copy-done.5) | copy-start | bytes 786436
  90.7 24.4 %copy-start.7 = (f32[2,32,1024]{2,1,0:T(8,128)S(1)}, f32[2,32,1024]{2,1,0:T(8,128)}, u32[]{:S(2)}) copy-start(f32[2,32,1024]{2,1,0:T(8,128)} %get-tuple-element.44) | copy-start | bytes 786436
  121.2 27.5 %copy-start.2 = (f32[2,32,1024]{2,1,0:T(8,128)S(1)}, f32[2,32,1024]{2,1,0:T(8,128)}, u32[]{:S(2)}) copy-start(f32[2,32,1024]{2,1,0:T(8,128)} %get-tuple-element.39.f_ref) | copy-start | bytes 786436
  124.7 24.0 %copy-start.9 = (f32[2,32,1024]{2,1,0:T(8,128)S(1)}, f32[2,32,1024]{2,1,0:T(8,128)}, u32[]{:S(2)}) copy-start(f32[2,32,1024]{2,1,0:T(8,128)} %get-tuple-element.49) | copy-start | bytes 786436
  153.0 27.7 %copy-start.12 = (f32[2,32,1024]{2,1,0:T(8,128)S(1)}, f32[2,32,1024]{2,1,0:T(8,128)}, u32[]{:S(2)}) copy-start(f32[2,32,1024]{2,1,0:T(8,128)} %multiply_subtract_fusion.1.f_ref) | copy-start | bytes 786436
  156.4 24.4 %copy-start.8 = (f32[2,32,1024]{2,1,0:T(8,128)S(1)}, f32[2,32,1024]{2,1,0:T(8,128)}, u32[]{:S(2)}) copy-start(f32[2,32,1024]{2,1,0:T(8,128)} %get-tuple-element.54) | copy-start | bytes 786436
  190.1 27.6 %copy-start.3 = (f32[2,32,1024]{2,1,0:T(8,128)S(1)}, f32[2,32,1024]{2,1,0:T(8,128)}, u32[]{:S(2)}) copy-start(f32[2,32,1024]{2,1,0:T(8,128)} %get-tuple-element.59) | copy-start | bytes 786436
  190.2 27.6 %copy-start.4 = (f32[2,32,1024]{2,1,0:T(8,128)S(1)}, f32[2,32,1024]{2,1,0:T(8,128)}, u32[]{:S(2)}) copy-start(f32[2,32,1024]{2,1,0:T(8,128)} %multiply_add_fusion.1.f_ref) | copy-start | bytes 786436
  221.8 25.0 %copy-start.10 = (f32[2,32,1024]{2,1,0:T(8,128)S(1)}, f32[2,32,1024]{2,1,0:T(8,128)}, u32[]{:S(2)}) copy-start(f32[2,32,1024]{2,1,0:T(8,128)} %get-tuple-element.64) | copy-start | bytes 786436
  221.8 25.0 %copy-start.11 = (f32[2,32,1024]{2,1,0:T(8,128)S(1)}, f32[2,32,1024]{2,1,0:T(8,128)}, u32[]{:S(2)}) copy-start(f32[2,32,1024]{2,1,0:T(8,128)} %multiply_subtract_fusion.f_ref) | copy-start | bytes 786436

commit v2 on v1

--- a/solution.py
+++ b/solution.py
@@ -116,7 +116,8 @@
 
 
 def stencil_kernel(
-    coef_ref, f_ref, bonds_ref, masks_ref, diag_ref, rows_ref, faces_ref, o_ref, part_ref, *, smooth
+    coef_ref, f_ref, bonds_ref, masks_ref, diag_ref, rows_ref, faces_ref,
+    o_ref, part_ref, xy_ref, z_ref, *, smooth
 ):
     slots, width, lanes = f_ref.shape
     row = lax.broadcasted_iota(jnp.int32, (width, lanes), 0)
@@ -137,6 +138,18 @@
         lane % BS == BS - 1,
         lane % BS == 0,
     ]
+    source_lane = lax.broadcasted_iota(jnp.int32, (lanes, BS), 0)
+    place = lax.broadcasted_iota(jnp.int32, (lanes, BS), 1)
+    layers = [
+        (source_lane == offset + step * place).astype(jnp.float32)
+        for offset, step in ((0, 1), (lanes - BS, 1), (0, BS), (BS - 1, BS))
+    ]
+    flat_mask = spot // BS == pick
+
+    def flatten(layer):
+        spread_out = jnp.where(flat_mask, spread(layer, spread_y), 0.0)
+        return jnp.sum(spread_out, axis=0, keepdims=True)
+
     dot = jnp.float32(0.0)
     for s in range(slots):
         ds = diag_ref[s]
@@ -164,6 +177,14 @@
             dot = dot + jnp.sum(fs * total)
             part_ref[1 + s] = jnp.sum(total)
         o_ref[s] = total
+        xy_ref[pl.ds(s, 1), :] = total[0:1, :]
+        xy_ref[pl.ds(slots + s, 1), :] = total[width - 1 : width, :]
+        if s == 0:
+            xy_ref[pl.ds(2 * slots, 1), :] = flatten(spread(total, layers[0]))
+        if s == slots - 1:
+            xy_ref[pl.ds(2 * slots + 1, 1), :] = flatten(spread(total, layers[1]))
+        z_ref[pl.ds(s, 1), :] = flatten(spread(total, layers[2]))
+        z_ref[pl.ds(slots + s, 1), :] = flatten(spread(total, layers[3]))
     part_ref[0] = dot
     if smooth:
         for s in range(slots):
@@ -182,9 +203,11 @@
         out_shape=(
             jax.ShapeDtypeStruct(field.shape, jnp.float32),
             jax.ShapeDtypeStruct((1 + slots,), jnp.float32),
+            jax.ShapeDtypeStruct((2 * slots + 2, field.shape[2]), jnp.float32),
+            jax.ShapeDtypeStruct((2 * slots, field.shape[2]), jnp.float32),
         ),
         in_specs=[smem, vmem, vmem, smem, vmem, vmem, vmem],
-        out_specs=(vmem, smem),
+        out_specs=(vmem, smem, vmem, vmem),
     )(coef, field, bonds, masks, diag, rows, faces)
 
 
@@ -392,13 +415,12 @@
             residual_field, bonds, masks, diagonal, *smoothed_halo, coef=coarse_solve(terms)
         )
 
-    def sum_and_share(part, field, with_sums):
+    def sum_and_share(part, field, xy, z, with_sums):
         values = [part[:1]]
         if with_sums:
             sums = slab_slot(part[1:][None])[:, 0]
             values.append((brick_here[:, None, None] * sums[None]).reshape(-1))
         packed = jnp.concatenate(values)
-        xy, z = side_faces(field)
         total, xy_land, z_land = exchange(as_tile(packed), xy, z, 1)
         total = total.reshape(-1)[: packed.shape[0]]
         field_halo = halo(field, xy_land, z_land, 0.0)
@@ -412,11 +434,11 @@
     terms = columns[4]
     solution_field = jnp.zeros_like(forcing)
     residual = forcing
-    search, part = precondition(residual, residual_halo, terms)
-    energy, _, search_halo = sum_and_share(part, search, False)
+    search, part, xy, z = precondition(residual, residual_halo, terms)
+    energy, _, search_halo = sum_and_share(part, search, xy, z, False)
     for iteration in range(ITERS):
-        mapped, part = stencil(search, bonds, masks, diagonal, *search_halo)
-        curvature, mapped_terms, mapped_halo = sum_and_share(part, mapped, True)
+        mapped, part, xy, z = stencil(search, bonds, masks, diagonal, *search_halo)
+        curvature, mapped_terms, mapped_halo = sum_and_share(part, mapped, xy, z, True)
         step_size = energy / curvature
         solution_field = solution_field + step_size * search
         residual = residual - step_size * mapped
@@ -425,8 +447,8 @@
                 part - step_size * change for part, change in zip(residual_halo, mapped_halo)
             ]
             terms = terms - step_size * mapped_terms
-            smoothed, part = precondition(residual, residual_halo, terms)
-            renewed, _, smoothed_halo = sum_and_share(part, smoothed, False)
+            smoothed, part, xy, z = precondition(residual, residual_halo, terms)
+            renewed, _, smoothed_halo = sum_and_share(part, smoothed, xy, z, False)
             search = smoothed + renewed / energy * search
             search_halo = [
                 part + renewed / energy * old for part, old in zip(smoothed_halo, search_halo)

time: 250 us -> 246 us (0.984)
  Pallas kernels: 133 us -> 150 us
  local copies, waits for them, and re-layouts: 53.5 us -> 40.3 us
  matrix products: 11.9 us -> 3.5 us
    pallas_call x6, Pallas kernels: 20 us -> 37.3 us  [stencil(): pl.pallas_call(functools.partial(stencil_kernel, smooth=smooth), out_shap...]
    dot_general x8 -> x2, matrix products: 11.1 us -> 2.66 us  [side_faces(): jnp.dot(field.reshape(slot_count * BS, face_size), picker, precision=lax....]
    pallas_call x6 -> x0, local copies, waits for them, and re-layouts: 6.95 us -> none  [stencil(): pl.pallas_call(functools.partial(stencil_kernel, smooth=smooth), out_shap...]
    reshape x8 -> x2, local copies, waits for them, and re-layouts: 4.37 us -> 0.19 us  [side_faces(): return (xy, z.reshape(2 * slot_count, face_size))]
    concatenate x6 -> x0, other arithmetic: 3.75 us -> none  [side_faces(): jnp.concatenate([field[:, 0, :], field[:, BS - 1, :], field[0, :, :BS].re...]
where the time goes in v2:
time: 246 us; the launch traced here: 243 us
  Pallas kernels  150 us (61%)
  local copies, waits for them, and re-layouts  40.3 us (16%)
  other arithmetic  35.7 us (15%)
  between operations  13.4 us (5%)
  matrix products  3.5 us (1%)
    pallas_call x7, Pallas kernels, exchange(): pl.pallas_call(exchange_kernel, out_shape=(jax.ShapeDtypeStruct(tile.shap...  113 us
    pallas_call x6, Pallas kernels, stencil(): pl.pallas_call(functools.partial(stencil_kernel, smooth=smooth), out_shap...  37.3 us
    pallas_call x6, local copies, waits for them, and re-layouts, exchange(): pl.pallas_call(exchange_kernel, out_shape=(jax.ShapeDtypeStruct(tile.shap...  6.67 us

profile of v2, /device:TPU:0, one launch (start us, length us, event | category | flops | bytes accessed | tf_op | source)
XLA Modules:
  0.0 243.1 jit_solution(7629217562102292731)
XLA Ops:
  0.7 1.2 dynamic_slice.117
  4.6 1.4 fusion.104
  8.7 1.1 reduce_sum.122
  9.8 0.8 fusion.74
  12.4 2.2 convolution_bitcast_fusion
  17.9 1.3 concatenate.104.xy_ref
  20.1 23.0 %shard_map.68 = (f32[16,128]{1,0:T(8,128)}, f32[8,12,1024]{2,1,0:T(8,128)}, f32[2,8,1024]{2,1,0:T(8,128)}) custom-call(f32[16,128]{1,0:T(8,128)} %pad_bitcast_fusion.x_ref, f32[12,1024]{1,0:T(8,128)} %concatenate.104.xy_ref, f32[8,1024]{1,0:T(8,128)} %pad_maximum_fusion.3.z_ref), custom_call_target="tpu_custom_call" | custom-call | tf_op jit(solution)/shard_map/pallas_call | solution.py:91
  43.1 0.9 slice_select_fusion.11
  44.3 1.3 copy.256
  49.1 2.9 %cholesky.19 = f32[32,32]{1,0:T(8,128)S(1)} custom-call(f32[32,32]{1,0:T(8,128)S(1)} %add_multiply_fusion), custom_call_target="Cholesky" | custom-call | tf_op jit(solution)/shard_map/jit(cholesky)/cholesky | solution.py:403
  52.1 0.7 compare_reduce_fusion
  53.4 2.4 %custom-call.14 = f32[1,32,32]{1,2,0:T(8,128)S(1)} custom-call(f32[1,32,32]{2,1,0:T(8,128)S(1)} %fusion.50), custom_call_target="InvertDiagBlocksLowerTriangular" | custom-call | tf_op jit(solution)/shard_map/triangular_solve/custom-call.2 | solution.py:407
  56.8 6.2 %shard_map.69 = (f32[2,32,1024]{2,1,0:T(8,128)}, f32[3]{0:T(128)}, f32[6,1024]{1,0:T(8,128)}, f32[4,1024]{1,0:T(4,128)}) custom-call(f32[2]{0:T(128)} %fusion.106.coef_ref, f32[2,32,1024]{2,1,0:T(8,128)} %copy-done.3, f32[6,2,32,1024]{3,2,1,0:T(8,128)} %bitcast.356, f32[24]{0:T(128)} %reshape.1744.masks_ref, f32[2,32,1024]{2,1,0:T(8,128)} %copy-done.1, ...), custom_call_target="tpu_custom_call" | custom-call | tf_op jit(solution)/shard_map/pallas_call | solution.py:201
  63.0 1.2 pad_bitcast_fusion.3.x_ref
  64.2 0.8 fusion.125
  65.0 15.7 %shard_map.70 = (f32[8,128]{1,0:T(8,128)}, f32[8,6,1024]{2,1,0:T(8,128)}, f32[2,4,1024]{2,1,0:T(4,128)}) custom-call(f32[8,128]{1,0:T(8,128)} %pad_bitcast_fusion.3.x_ref, f32[6,1024]{1,0:T(8,128)} %get-tuple-element.51.xy_ref, f32[4,1024]{1,0:T(4,128)} %get-tuple-element.52.z_ref), custom_call_target="tpu_custom_call" | custom-call | tf_op jit(solution)/shard_map/pallas_call | solution.py:91
  80.7 1.2 slice.449
  81.9 0.7 slice_select_fusion.9
  82.9 1.1 copy.259
  86.0 6.3 %shard_map.71 = (f32[2,32,1024]{2,1,0:T(8,128)}, f32[3]{0:T(128)}, f32[6,1024]{1,0:T(8,128)}, f32[4,1024]{1,0:T(4,128)}) custom-call(f32[2]{0:T(128)} %broadcast_16_coef_ref.2.coef_ref, f32[2,32,1024]{2,1,0:T(8,128)} %get-tuple-element.54.f_ref, f32[6,2,32,1024]{3,2,1,0:T(8,128)} %bitcast.357, f32[24]{0:T(128)} %reshape.1744.masks_ref, ...), custom_call_target="tpu_custom_call" | custom-call | tf_op jit(solution)/shard_map/pallas_call | solution.py:201
  92.4 0.7 slice.459
  93.2 0.8 fusion.124
  94.2 1.3 fusion.97.x_ref
  95.5 14.5 %shard_map.72 = (f32[8,128]{1,0:T(8,128)}, f32[8,6,1024]{2,1,0:T(8,128)}, f32[2,4,1024]{2,1,0:T(4,128)}) custom-call(f32[8,128]{1,0:T(8,128)} %fusion.97.x_ref, f32[6,1024]{1,0:T(8,128)} %get-tuple-element.58.xy_ref, f32[4,1024]{1,0:T(4,128)} %get-tuple-element.59.z_ref), custom_call_target="tpu_custom_call" | custom-call | tf_op jit(solution)/shard_map/pallas_call | solution.py:91
  110.0 1.2 slice.460
  112.6 1.7 multiply_subtract_fusion.1.f_ref
  114.3 0.8 slice.461
  116.0 0.7 slice_select_fusion.7
  117.0 1.1 copy.264
  119.0 0.7 multiply_divide_fusion.faces_ref
  119.6 6.2 %shard_map.73 = (f32[2,32,1024]{2,1,0:T(8,128)}, f32[3]{0:T(128)}, f32[6,1024]{1,0:T(8,128)}, f32[4,1024]{1,0:T(4,128)}) custom-call(f32[2]{0:T(128)} %fusion.110.coef_ref, f32[2,32,1024]{2,1,0:T(8,128)} %multiply_subtract_fusion.1.f_ref, f32[6,2,32,1024]{3,2,1,0:T(8,128)} %bitcast.358, f32[24]{0:T(128)} %reshape.1744.masks_ref, f32[2,32,1024]{2,1,0:T(8,128)} %copy-done.1, ...), custom_call_target="tpu_custom_call" | custom-call | tf_op jit(solution)/shard_map/pallas_call | solution.py:201
  125.8 1.2 pad_bitcast_fusion.2.x_ref
  127.0 0.8 fusion.123
  127.8 15.3 %shard_map.74 = (f32[8,128]{1,0:T(8,128)}, f32[8,6,1024]{2,1,0:T(8,128)}, f32[2,4,1024]{2,1,0:T(4,128)}) custom-call(f32[8,128]{1,0:T(8,128)} %pad_bitcast_fusion.2.x_ref, f32[6,1024]{1,0:T(8,128)} %get-tuple-element.65.xy_ref, f32[4,1024]{1,0:T(4,128)} %get-tuple-element.66.z_ref), custom_call_target="tpu_custom_call" | custom-call | tf_op jit(solution)/shard_map/pallas_call | solution.py:91
  143.1 1.3 slice.471
  145.7 1.7 multiply_add_fusion.1.f_ref
  147.4 0.7 slice_select_fusion.5
  148.3 1.1 copy.269
  150.9 6.2 %shard_map.75 = (f32[2,32,1024]{2,1,0:T(8,128)}, f32[3]{0:T(128)}, f32[6,1024]{1,0:T(8,128)}, f32[4,1024]{1,0:T(4,128)}) custom-call(f32[2]{0:T(128)} %broadcast_16_coef_ref.2.coef_ref, f32[2,32,1024]{2,1,0:T(8,128)} %multiply_add_fusion.1.f_ref, f32[6,2,32,1024]{3,2,1,0:T(8,128)} %bitcast.359, f32[24]{0:T(128)} %reshape.1744.masks_ref, ...), custom_call_target="tpu_custom_call" | custom-call | tf_op jit(solution)/shard_map/pallas_call | solution.py:201
  157.1 0.7 slice.481
  157.9 0.8 fusion.122
  158.9 1.3 fusion.96.x_ref
  160.2 14.7 %shard_map.76 = (f32[8,128]{1,0:T(8,128)}, f32[8,6,1024]{2,1,0:T(8,128)}, f32[2,4,1024]{2,1,0:T(4,128)}) custom-call(f32[8,128]{1,0:T(8,128)} %fusion.96.x_ref, f32[6,1024]{1,0:T(8,128)} %get-tuple-element.72.xy_ref, f32[4,1024]{1,0:T(4,128)} %get-tuple-element.73.z_ref), custom_call_target="tpu_custom_call" | custom-call | tf_op jit(solution)/shard_map/pallas_call | solution.py:91
  174.9 1.3 slice.482
  177.6 1.7 multiply_subtract_fusion.f_ref
  179.2 0.8 slice.483
  181.0 0.7 slice_select_fusion.3
  181.9 1.1 copy.276
  183.9 0.7 fusion.35.faces_ref
  184.7 6.2 %shard_map.77 = (f32[2,32,1024]{2,1,0:T(8,128)}, f32[3]{0:T(128)}, f32[6,1024]{1,0:T(8,128)}, f32[4,1024]{1,0:T(4,128)}) custom-call(f32[2]{0:T(128)} %fusion.115.coef_ref, f32[2,32,1024]{2,1,0:T(8,128)} %multiply_subtract_fusion.f_ref, f32[6,2,32,1024]{3,2,1,0:T(8,128)} %bitcast.360, f32[24]{0:T(128)} %reshape.1744.masks_ref, f32[2,32,1024]{2,1,0:T(8,128)} %copy-done.1, ...), custom_call_target="tpu_custom_call" | custom-call | tf_op jit(solution)/shard_map/pallas_call | solution.py:201
  190.9 1.2 pad_bitcast_fusion.1.x_ref
  192.1 0.8 fusion.121
  192.9 15.3 %shard_map.78 = (f32[8,128]{1,0:T(8,128)}, f32[8,6,1024]{2,1,0:T(8,128)}, f32[2,4,1024]{2,1,0:T(4,128)}) custom-call(f32[8,128]{1,0:T(8,128)} %pad_bitcast_fusion.1.x_ref, f32[6,1024]{1,0:T(8,128)} %get-tuple-element.79.xy_ref, f32[4,1024]{1,0:T(4,128)} %get-tuple-element.80.z_ref), custom_call_target="tpu_custom_call" | custom-call | tf_op jit(solution)/shard_map/pallas_call | solution.py:91
  208.2 1.3 slice.493
  210.8 0.7 slice_select_fusion.1
  211.7 1.1 copy.281
  214.4 0.7 multiply_add_fusion.f_ref
  215.1 6.2 %shard_map.79 = (f32[2,32,1024]{2,1,0:T(8,128)}, f32[3]{0:T(128)}, f32[6,1024]{1,0:T(8,128)}, f32[4,1024]{1,0:T(4,128)}) custom-call(f32[2]{0:T(128)} %broadcast_16_coef_ref.2.coef_ref, f32[2,32,1024]{2,1,0:T(8,128)} %multiply_add_fusion.f_ref, f32[6,2,32,1024]{3,2,1,0:T(8,128)} %bitcast.361, f32[24]{0:T(128)} %reshape.1744.masks_ref, ...), custom_call_target="tpu_custom_call" | custom-call | tf_op jit(solution)/shard_map/pallas_call | solution.py:201
  221.4 0.7 slice.503
  222.4 1.3 fusion.95.x_ref
  223.7 14.4 %shard_map.80 = (f32[8,128]{1,0:T(8,128)}, f32[8,6,1024]{2,1,0:T(8,128)}, f32[2,4,1024]{2,1,0:T(4,128)}) custom-call(f32[8,128]{1,0:T(8,128)} %fusion.95.x_ref, f32[6,1024]{1,0:T(8,128)} %get-tuple-element.86.xy_ref, f32[4,1024]{1,0:T(4,128)} %get-tuple-element.87.z_ref), custom_call_target="tpu_custom_call" | custom-call | tf_op jit(solution)/shard_map/pallas_call | solution.py:91
  238.1 1.2 slice.504
  240.6 0.8 add_bitcast_fusion
  241.4 1.7 subtract_bitcast_fusion
  (203 shorter events, 22.0 us)
Async XLA Ops:
  6.6 8.0 %copy-start.9 = (f32[1,1,2,32,1024]{4,3,2,1,0:T(8,128)S(1)}, f32[1,1,2,32,1024]{4,3,2,1,0:T(8,128)}, u32[]{:S(2)}) copy-start(f32[1,1,2,32,1024]{4,3,2,1,0:T(8,128)} %param.9) | copy-start | bytes 786436
  12.4 3.5 %copy-start = (f32[1,1,6,2,32,1024]{5,4,3,2,1,0:T(8,128)S(1)}, f32[1,1,6,2,32,1024]{5,4,3,2,1,0:T(8,128)}, u32[]{:S(2)}) copy-start(f32[1,1,6,2,32,1024]{5,4,3,2,1,0:T(8,128)} %param.11) | copy-start | bytes 4718596
  14.6 1.9 copy-start.10
  16.2 0.7 copy-start.3
  17.0 28.7 %copy-start.1 = (f32[2,32,1024]{2,1,0:T(8,128)}, f32[2,32,1024]{2,1,0:T(8,128)S(1)}, u32[]{:S(2)}) copy-start(f32[2,32,1024]{2,1,0:T(8,128)S(1)} %get-tuple-element.117.diag_ref) | copy-start | bytes 786436
  43.1 4.4 %copy-start.11 = (f32[16,128]{1,0:T(8,128)S(1)}, f32[16,128]{1,0:T(8,128)}, u32[]{:S(2)}) copy-start(f32[16,128]{1,0:T(8,128)} %get-tuple-element.47) | copy-start | bytes 24580
  44.3 4.5 %copy-start.12 = (pred[32]{0:T(512)(128)(4,1)S(1)}, pred[32]{0:T(512)(128)(4,1)}, u32[]{:S(2)}) copy-start(pred[32]{0:T(512)(128)(4,1)} %constant.263.clone.1) | copy-start | bytes 100
  83.9 28.6 %copy-start.4 = (f32[2,32,1024]{2,1,0:T(8,128)S(1)}, f32[2,32,1024]{2,1,0:T(8,128)}, u32[]{:S(2)}) copy-start(f32[2,32,1024]{2,1,0:T(8,128)} %copy-done.3) | copy-start | bytes 786436
  118.2 27.5 %copy-start.5 = (f32[2,32,1024]{2,1,0:T(8,128)S(1)}, f32[2,32,1024]{2,1,0:T(8,128)}, u32[]{:S(2)}) copy-start(f32[2,32,1024]{2,1,0:T(8,128)} %get-tuple-element.54.f_ref) | copy-start | bytes 786436
  149.5 28.0 %copy-start.7 = (f32[2,32,1024]{2,1,0:T(8,128)S(1)}, f32[2,32,1024]{2,1,0:T(8,128)}, u32[]{:S(2)}) copy-start(f32[2,32,1024]{2,1,0:T(8,128)} %multiply_subtract_fusion.1.f_ref) | copy-start | bytes 786436
  184.6 29.8 %copy-start.2 = (f32[2,32,1024]{2,1,0:T(8,128)S(1)}, f32[2,32,1024]{2,1,0:T(8,128)}, u32[]{:S(2)}) copy-start(f32[2,32,1024]{2,1,0:T(8,128)} %multiply_add_fusion.1.f_ref) | copy-start | bytes 786436
  190.9 23.5 %copy-start.8 = (f32[2,32,1024]{2,1,0:T(8,128)S(1)}, f32[2,32,1024]{2,1,0:T(8,128)}, u32[]{:S(2)}) copy-start(f32[2,32,1024]{2,1,0:T(8,128)} %get-tuple-element.82) | copy-start | bytes 786436
  215.1 26.2 %copy-start.6 = (f32[2,32,1024]{2,1,0:T(8,128)S(1)}, f32[2,32,1024]{2,1,0:T(8,128)}, u32[]{:S(2)}) copy-start(f32[2,32,1024]{2,1,0:T(8,128)} %multiply_subtract_fusion.f_ref) | copy-start | bytes 786436

commit v3 on v2

--- a/solution.py
+++ b/solution.py
@@ -16,6 +16,64 @@
 
 
 OMEGA = 0.6
+
+
+def share(
+    x_ref, xy_ref, z_ref, o_ref, xy_out, z_out, landed_b, landed_g, landed_xy, landed_z,
+    send_b, recv_b, send_g, recv_g, send_xy, recv_xy, send_z, recv_z, brick_peers, grp_peers,
+):
+    here_brick = lax.axis_index("brick")
+    here_grp = lax.axis_index("grp")
+    n_brick = landed_b.shape[0]
+    n_grp = landed_g.shape[0]
+
+    def send(src, dst, sends, recvs, index, peer):
+        copy = pltpu.make_async_remote_copy(
+            src_ref=src,
+            dst_ref=dst.at[index],
+            send_sem=sends.at[index],
+            recv_sem=recvs.at[index],
+            device_id=peer,
+            device_id_type=MESH_IDS,
+        )
+        copy.start()
+        return copy
+
+    face_copies = [
+        send(z_ref, landed_z, send_z, recv_z, 0, grp_peers[0]),
+        send(z_ref, landed_z, send_z, recv_z, 1, grp_peers[-1]),
+    ]
+    face_copies += [
+        send(xy_ref, landed_xy, send_xy, recv_xy, k, peer)
+        for k, peer in enumerate(brick_peers, start=1)
+    ]
+    copies = [
+        send(x_ref, landed_b, send_b, recv_b, k, peer)
+        for k, peer in enumerate(brick_peers, start=1)
+    ]
+    landed_b[0] = x_ref[...]
+    for copy in copies:
+        copy.wait()
+    total = landed_b[lax.rem(here_brick, n_brick)]
+    for j in range(1, n_brick):
+        total = total + landed_b[lax.rem(here_brick + n_brick - j, n_brick)]
+    o_ref[...] = total
+    landed_g[0] = total
+    copies = [
+        send(o_ref, landed_g, send_g, recv_g, k, peer)
+        for k, peer in enumerate(grp_peers, start=1)
+    ]
+    for copy in copies:
+        copy.wait()
+    total = landed_g[lax.rem(here_grp, n_grp)]
+    for j in range(1, n_grp):
+        total = total + landed_g[lax.rem(here_grp + n_grp - j, n_grp)]
+    o_ref[...] = total
+    for copy in face_copies:
+        copy.wait()
+    landed_xy[0] = xy_ref[...]
+    xy_out[...] = landed_xy[...]
+    z_out[...] = landed_z[...]
 
 
 def exchange_kernel(
@@ -34,53 +92,10 @@
         pl.semaphore_signal(barrier, inc=1, device_id=peer, device_id_type=MESH_IDS)
     pl.semaphore_wait(barrier, len(brick_peers) + len(grp_peers))
 
-    def send(src, dst, sends, recvs, index, peer):
-        copy = pltpu.make_async_remote_copy(
-            src_ref=src,
-            dst_ref=dst.at[index],
-            send_sem=sends.at[index],
-            recv_sem=recvs.at[index],
-            device_id=peer,
-            device_id_type=MESH_IDS,
-        )
-        copy.start()
-        return copy
-
-    face_copies = [
-        send(z_ref, landed_z, send_z, recv_z, 0, grp_peers[0]),
-        send(z_ref, landed_z, send_z, recv_z, 1, grp_peers[-1]),
-    ]
-    face_copies += [
-        send(xy_ref, landed_xy, send_xy, recv_xy, k, peer)
-        for k, peer in enumerate(brick_peers, start=1)
-    ]
-    copies = [
-        send(x_ref, landed_b, send_b, recv_b, k, peer)
-        for k, peer in enumerate(brick_peers, start=1)
-    ]
-    landed_b[0] = x_ref[...]
-    for copy in copies:
-        copy.wait()
-    total = landed_b[lax.rem(here_brick, n_brick)]
-    for j in range(1, n_brick):
-        total = total + landed_b[lax.rem(here_brick + n_brick - j, n_brick)]
-    o_ref[...] = total
-    landed_g[0] = total
-    copies = [
-        send(o_ref, landed_g, send_g, recv_g, k, peer)
-        for k, peer in enumerate(grp_peers, start=1)
-    ]
-    for copy in copies:
-        copy.wait()
-    total = landed_g[lax.rem(here_grp, n_grp)]
-    for j in range(1, n_grp):
-        total = total + landed_g[lax.rem(here_grp + n_grp - j, n_grp)]
-    o_ref[...] = total
-    for copy in face_copies:
-        copy.wait()
-    landed_xy[0] = xy_ref[...]
-    xy_out[...] = landed_xy[...]
-    z_out[...] = landed_z[...]
+    share(
+        x_ref, xy_ref, z_ref, o_ref, xy_out, z_out, landed_b, landed_g, landed_xy, landed_z,
+        send_b, recv_b, send_g, recv_g, send_xy, recv_xy, send_z, recv_z, brick_peers, grp_peers,
+    )
 
 
 def exchange(tile, xy, z, kernel_id):
@@ -115,9 +130,8 @@
     )(tile, xy, z)
 
 
-def stencil_kernel(
-    coef_ref, f_ref, bonds_ref, masks_ref, diag_ref, rows_ref, faces_ref,
-    o_ref, part_ref, xy_ref, z_ref, *, smooth
+def stencil_body(
+    coef_ref, f_ref, bonds_ref, masks_ref, diag_ref, rows_ref, faces_ref, o_ref, xy_ref, z_ref, smooth
 ):
     slots, width, lanes = f_ref.shape
     row = lax.broadcasted_iota(jnp.int32, (width, lanes), 0)
@@ -151,6 +165,7 @@
         return jnp.sum(spread_out, axis=0, keepdims=True)
 
     dot = jnp.float32(0.0)
+    sums = []
     for s in range(slots):
         ds = diag_ref[s]
         if smooth:
@@ -175,7 +190,7 @@
             dot = dot + jnp.sum(rs * total)
         else:
             dot = dot + jnp.sum(fs * total)
-            part_ref[1 + s] = jnp.sum(total)
+            sums.append(jnp.sum(total))
         o_ref[s] = total
         xy_ref[pl.ds(s, 1), :] = total[0:1, :]
         xy_ref[pl.ds(slots + s, 1), :] = total[width - 1 : width, :]
@@ -185,29 +200,84 @@
             xy_ref[pl.ds(2 * slots + 1, 1), :] = flatten(spread(total, layers[1]))
         z_ref[pl.ds(s, 1), :] = flatten(spread(total, layers[2]))
         z_ref[pl.ds(slots + s, 1), :] = flatten(spread(total, layers[3]))
-    part_ref[0] = dot
-    if smooth:
-        for s in range(slots):
-            part_ref[1 + s] = jnp.float32(0.0)
-
-
-def stencil(field, bonds, masks, diag, rows, faces, coef=None):
-    slots = field.shape[0]
-    smooth = coef is not None
-    if coef is None:
-        coef = jnp.zeros((slots,), jnp.float32)
+    return dot, sums
+
+
+def round_kernel(
+    coef_ref, f_ref, bonds_ref, masks_ref, diag_ref, rows_ref, faces_ref,
+    o_ref, total_ref, xy_out, z_out,
+    xy_buf, z_buf, tile_buf, landed_b, landed_g, landed_xy, landed_z,
+    send_b, recv_b, send_g, recv_g, send_xy, recv_xy, send_z, recv_z, *, smooth
+):
+    here_brick = lax.axis_index("brick")
+    here_grp = lax.axis_index("grp")
+    n_brick = landed_b.shape[0]
+    n_grp = landed_g.shape[0]
+    brick_peers = [(lax.rem(here_brick + k, n_brick), here_grp) for k in range(1, n_brick)]
+    grp_peers = [(here_brick, lax.rem(here_grp + k, n_grp)) for k in range(1, n_grp)]
+    barrier = pltpu.get_barrier_semaphore()
+    for peer in brick_peers + grp_peers:
+        pl.semaphore_signal(barrier, inc=1, device_id=peer, device_id_type=MESH_IDS)
+    dot, sums = stencil_body(
+        coef_ref, f_ref, bonds_ref, masks_ref, diag_ref, rows_ref, faces_ref, o_ref, xy_buf, z_buf,
+        smooth,
+    )
+    tile_rows, tile_lanes = tile_buf.shape
+    flat = lax.broadcasted_iota(jnp.int32, (tile_rows, tile_lanes), 0) * tile_lanes
+    flat = flat + lax.broadcasted_iota(jnp.int32, (tile_rows, tile_lanes), 1)
+    tile = jnp.where(flat == 0, dot, 0.0)
+    slots = f_ref.shape[0]
+    for s, value in enumerate(sums):
+        position = 1 + (here_brick * n_grp + here_grp) * slots + s
+        tile = jnp.where(flat == position, value, tile)
+    tile_buf[...] = tile
+    pl.semaphore_wait(barrier, len(brick_peers) + len(grp_peers))
+    share(
+        tile_buf, xy_buf, z_buf, total_ref, xy_out, z_out, landed_b, landed_g, landed_xy, landed_z,
+        send_b, recv_b, send_g, recv_g, send_xy, recv_xy, send_z, recv_z, brick_peers, grp_peers,
+    )
+
+
+def one_round(field, bonds, masks, diag, rows, faces, coef, smooth):
+    slots, _, lanes = field.shape
+    n_brick = lax.axis_size("brick")
+    n_grp = lax.axis_size("grp")
+    tile = (8, 128)
+    xy = (2 * slots + 2, lanes)
+    z = (2 * slots, lanes)
     vmem = pl.BlockSpec(memory_space=pltpu.VMEM)
     smem = pl.BlockSpec(memory_space=pltpu.SMEM)
+    dma = pltpu.SemaphoreType.DMA
     return pl.pallas_call(
-        functools.partial(stencil_kernel, smooth=smooth),
+        functools.partial(round_kernel, smooth=smooth),
         out_shape=(
             jax.ShapeDtypeStruct(field.shape, jnp.float32),
-            jax.ShapeDtypeStruct((1 + slots,), jnp.float32),
-            jax.ShapeDtypeStruct((2 * slots + 2, field.shape[2]), jnp.float32),
-            jax.ShapeDtypeStruct((2 * slots, field.shape[2]), jnp.float32),
+            jax.ShapeDtypeStruct(tile, jnp.float32),
+            jax.ShapeDtypeStruct((n_brick,) + xy, jnp.float32),
+            jax.ShapeDtypeStruct((2,) + z, jnp.float32),
         ),
         in_specs=[smem, vmem, vmem, smem, vmem, vmem, vmem],
-        out_specs=(vmem, smem, vmem, vmem),
+        out_specs=(vmem, vmem, vmem, vmem),
+        scratch_shapes=[
+            pltpu.VMEM(xy, jnp.float32),
+            pltpu.VMEM(z, jnp.float32),
+            pltpu.VMEM(tile, jnp.float32),
+            pltpu.VMEM((n_brick,) + tile, jnp.float32),
+            pltpu.VMEM((n_grp,) + tile, jnp.float32),
+            pltpu.VMEM((n_brick,) + xy, jnp.float32),
+            pltpu.VMEM((2,) + z, jnp.float32),
+            dma((n_brick,)),
+            dma((n_brick,)),
+            dma((n_grp,)),
+            dma((n_grp,)),
+            dma((n_brick,)),
+            dma((n_brick,)),
+            dma((2,)),
+            dma((2,)),
+        ],
+        compiler_params=pltpu.CompilerParams(
+            collective_id=3 if smooth else 1, has_side_effects=True
+        ),
     )(coef, field, bonds, masks, diag, rows, faces)
 
 
@@ -409,36 +479,33 @@
         )
         return lax.dynamic_slice_in_dim(result[:, 0], slab_index * slot_count, slot_count)
 
+    def round_trip(field, field_halo, coef, smooth):
+        out, total, xy_land, z_land = one_round(
+            field, bonds, masks, diagonal, *field_halo, coef, smooth
+        )
+        total = total.reshape(-1)
+        out_halo = halo(out, xy_land, z_land, 0.0)
+        if smooth:
+            return out, total[0], None, out_halo
+        count = brick_count * grp_count * slot_count
+        mine = lax.dynamic_index_in_dim(
+            total[1 : 1 + count].reshape(brick_count, -1), brick_index, keepdims=False
+        )
+        return out, total[0], mine, out_halo
+
     def precondition(residual_field, field_halo, terms):
         smoothed_halo = [OMEGA * part / scale for part, scale in zip(field_halo, diagonal_halo)]
-        return stencil(
-            residual_field, bonds, masks, diagonal, *smoothed_halo, coef=coarse_solve(terms)
-        )
-
-    def sum_and_share(part, field, xy, z, with_sums):
-        values = [part[:1]]
-        if with_sums:
-            sums = slab_slot(part[1:][None])[:, 0]
-            values.append((brick_here[:, None, None] * sums[None]).reshape(-1))
-        packed = jnp.concatenate(values)
-        total, xy_land, z_land = exchange(as_tile(packed), xy, z, 1)
-        total = total.reshape(-1)[: packed.shape[0]]
-        field_halo = halo(field, xy_land, z_land, 0.0)
-        if not with_sums:
-            return total[0], None, field_halo
-        mine = lax.dynamic_index_in_dim(
-            total[1:].reshape(brick_count, -1), brick_index, keepdims=False
-        )
-        return total[0], mine, field_halo
-
+        return round_trip(residual_field, smoothed_halo, coarse_solve(terms), True)
+
+    no_coarse = jnp.zeros((slot_count,), jnp.float32)
     terms = columns[4]
     solution_field = jnp.zeros_like(forcing)
     residual = forcing
-    search, part, xy, z = precondition(residual, residual_halo, terms)
-    energy, _, search_halo = sum_and_share(part, search, xy, z, False)
+    search, energy, _, search_halo = precondition(residual, residual_halo, terms)
     for iteration in range(ITERS):
-        mapped, part, xy, z = stencil(search, bonds, masks, diagonal, *search_halo)
-        curvature, mapped_terms, mapped_halo = sum_and_share(part, mapped, xy, z, True)
+        mapped, curvature, mapped_terms, mapped_halo = round_trip(
+            search, search_halo, no_coarse, False
+        )
         step_size = energy / curvature
         solution_field = solution_field + step_size * search
         residual = residual - step_size * mapped
@@ -447,8 +514,7 @@
                 part - step_size * change for part, change in zip(residual_halo, mapped_halo)
             ]
             terms = terms - step_size * mapped_terms
-            smoothed, part, xy, z = precondition(residual, residual_halo, terms)
-            renewed, _, smoothed_halo = sum_and_share(part, smoothed, xy, z, False)
+            smoothed, renewed, _, smoothed_halo = precondition(residual, residual_halo, terms)
             search = smoothed + renewed / energy * search
             search_halo = [
                 part + renewed / energy * old for part, old in zip(smoothed_halo, search_halo)

time: 246 us -> 211 us (0.86)
  Pallas kernels: 150 us -> 127 us
  local copies, waits for them, and re-layouts: 40.3 us -> 33.9 us
  other arithmetic: 35.7 us -> 31.5 us
    pallas_call x7 -> x1, Pallas kernels: 113 us -> 23 us  [exchange(): pl.pallas_call(exchange_kernel, out_shape=(jax.ShapeDtypeStruct(tile.shap...]
    pallas_call x6, Pallas kernels: 37.3 us -> 104 us  [one_round(): pl.pallas_call(functools.partial(round_kernel, smooth=smooth), out_shape=...]
    pallas_call x0 -> x5, local copies, waits for them, and re-layouts: none -> 5.4 us  [one_round(): pl.pallas_call(functools.partial(round_kernel, smooth=smooth), out_shape=...]
    pallas_call x6 -> x1, local copies, waits for them, and re-layouts: 6.67 us -> 1.3 us  [exchange(): pl.pallas_call(exchange_kernel, out_shape=(jax.ShapeDtypeStruct(tile.shap...]
    reshape x3 -> x0, other arithmetic: 3.88 us -> none  [as_tile(): return jnp.pad(values, (0, rows * 128 - values.shape[0])).reshape(rows, 128)]
    reshape x4 -> x1, local copies, waits for them, and re-layouts: 4.16 us -> 0.6 us  [as_tile(): return jnp.pad(values, (0, rows * 128 - values.shape[0])).reshape(rows, 128)]
    slice x11 -> x8, local copies, waits for them, and re-layouts: 11.1 us -> 8.82 us  [the longest x3 3.76 us: round_trip(): return (out, total[0], None, out_halo)]
where the time goes in v3:
time: 211 us; the launch traced here: 209 us
  Pallas kernels  127 us (60%)
  local copies, waits for them, and re-layouts  33.9 us (16%)
  other arithmetic  31.5 us (15%)
  between operations  13.1 us (6%)
  matrix products  3.51 us (2%)
    pallas_call x6, Pallas kernels, one_round(): pl.pallas_call(functools.partial(round_kernel, smooth=smooth), out_shape=...  104 us
    pallas_call x1, Pallas kernels, exchange(): pl.pallas_call(exchange_kernel, out_shape=(jax.ShapeDtypeStruct(tile.shap...  23 us
    pallas_call x5, local copies, waits for them, and re-layouts, one_round(): pl.pallas_call(functools.partial(round_kernel, smooth=smooth), out_shape=...  5.4 us
    select_n x6, other arithmetic, halo(): above = jnp.where(slab_index < grp_count - 1, z_land[1, :slot_count], fill)  4.59 us

profile of v3, /device:TPU:0, one launch (start us, length us, event | category | flops | bytes accessed | tf_op | source)
XLA Modules:
  0.0 209.3 jit_solution(2733142825635075013)
XLA Ops:
  0.6 1.2 dynamic_slice.117
  4.6 1.4 fusion.101
  8.7 1.1 reduce_sum.122
  9.8 0.8 fusion.74
  11.5 0.7 reshape.1625.masks_ref
  12.4 2.2 %convolution_bitcast_fusion = f32[2,2,32,32]{3,2,0,1:T(8,128)S(1)} fusion(pred[2,32,1024,1]{2,1,0,3:T(32,128)(4,1)S(1)} %bitcast.344, f32[1,1,2,32,1024]{4,3,2,1,0:T(8,128)} %param.10, f32[1,1,6,2,32,1024]{5,4,3,2,1,0:T(8,128)} %param.11, f32[2]{0:T(128)S(1)} %get-tuple-element.171, f32[2]{0:T(128)S(1)} %get-tuple-element.172, f32[2]{0:T(128)S(1)} %get-tuple-element.170, ...), kind=kOutput, calls=%fused_computation | convolution fusion | flops 51511296 | bytes 2048120 | tf_op jit(solution)/shard_map/dot_general | solution.py:368
  15.3 0.6 pad_maximum_fusion.3.z_ref
  17.9 1.3 concatenate.95.xy_ref
  20.1 23.0 %shard_map.68 = (f32[16,128]{1,0:T(8,128)}, f32[8,12,1024]{2,1,0:T(8,128)}, f32[2,8,1024]{2,1,0:T(8,128)}) custom-call(f32[16,128]{1,0:T(8,128)} %pad_bitcast_fusion.x_ref, f32[12,1024]{1,0:T(8,128)} %concatenate.95.xy_ref, f32[8,1024]{1,0:T(8,128)} %pad_maximum_fusion.3.z_ref), custom_call_target="tpu_custom_call" | custom-call | tf_op jit(solution)/shard_map/pallas_call | solution.py:106
  43.1 0.9 slice_select_fusion.11
  44.3 1.3 copy.256
  46.1 0.6 copy.258.rows_ref
  46.8 0.7 multiply_divide_fusion.1.faces_ref
  49.1 2.9 %cholesky.19 = f32[32,32]{1,0:T(8,128)S(1)} custom-call(f32[32,32]{1,0:T(8,128)S(1)} %add_multiply_fusion), custom_call_target="Cholesky" | custom-call | tf_op jit(solution)/shard_map/jit(cholesky)/cholesky | solution.py:473
  52.0 0.7 compare_reduce_fusion
  52.7 0.6 fusion.50
  53.3 2.4 %custom-call.14 = f32[1,32,32]{1,2,0:T(8,128)S(1)} custom-call(f32[1,32,32]{2,1,0:T(8,128)S(1)} %fusion.50), custom_call_target="InvertDiagBlocksLowerTriangular" | custom-call | tf_op jit(solution)/shard_map/triangular_solve/custom-call.2 | solution.py:477
  56.1 0.6 fusion.103.coef_ref
  56.7 18.0 %shard_map.69 = (f32[2,32,1024]{2,1,0:T(8,128)}, f32[8,128]{1,0:T(8,128)}, f32[8,6,1024]{2,1,0:T(8,128)}, f32[2,4,1024]{2,1,0:T(4,128)}) custom-call(f32[2]{0:T(128)} %fusion.103.coef_ref, f32[2,32,1024]{2,1,0:T(8,128)} %copy-done.3, f32[6,2,32,1024]{3,2,1,0:T(8,128)} %bitcast.338, f32[24]{0:T(128)} %reshape.1625.masks_ref, f32[2,32,1024]{2,1,0:T(8,128)} %copy-done.1, ...), custom_call_target="tpu_custom_call" | custom-call | tf_op jit(solution)/shard_map/pallas_call | solution.py:251
  74.7 1.3 slice.413
  75.9 0.7 slice_select_fusion.9
  76.8 0.8 fusion.122
  77.7 1.1 copy.259
  79.0 0.6 copy.263.rows_ref
  79.7 0.7 pad_maximum_fusion.2.faces_ref
  80.8 17.4 %shard_map.70 = (f32[2,32,1024]{2,1,0:T(8,128)}, f32[8,128]{1,0:T(8,128)}, f32[8,6,1024]{2,1,0:T(8,128)}, f32[2,4,1024]{2,1,0:T(4,128)}) custom-call(f32[2]{0:T(128)} %broadcast_18_coef_ref.2.coef_ref, f32[2,32,1024]{2,1,0:T(8,128)} %get-tuple-element.33.f_ref, f32[6,2,32,1024]{3,2,1,0:T(8,128)} %bitcast.339, f32[24]{0:T(128)} %reshape.1625.masks_ref, ...), custom_call_target="tpu_custom_call" | custom-call | tf_op jit(solution)/shard_map/pallas_call | solution.py:251
  98.3 1.2 slice.422
  100.7 0.7 slice.423
  101.5 1.7 multiply_subtract_fusion.1.f_ref
  103.2 0.8 fusion.121
  104.9 0.7 slice_select_fusion.7
  105.8 1.1 copy.264
  107.2 0.6 copy.268.rows_ref
  107.8 0.7 multiply_divide_fusion.faces_ref
  108.5 17.3 %shard_map.71 = (f32[2,32,1024]{2,1,0:T(8,128)}, f32[8,128]{1,0:T(8,128)}, f32[8,6,1024]{2,1,0:T(8,128)}, f32[2,4,1024]{2,1,0:T(4,128)}) custom-call(f32[2]{0:T(128)} %fusion.107.coef_ref, f32[2,32,1024]{2,1,0:T(8,128)} %multiply_subtract_fusion.1.f_ref, f32[6,2,32,1024]{3,2,1,0:T(8,128)} %bitcast.340, f32[24]{0:T(128)} %reshape.1625.masks_ref, ...), custom_call_target="tpu_custom_call" | custom-call | tf_op jit(solution)/shard_map/pallas_call | solution.py:251
  125.8 1.2 slice.432
  128.3 0.7 slice_select_fusion.5
  129.2 0.8 fusion.120
  130.0 1.7 multiply_add_fusion.1.f_ref
  131.7 1.1 copy.269
  133.0 0.6 fusion.52.rows_ref
  133.6 0.7 maximum_add_fusion.faces_ref
  134.3 17.1 %shard_map.72 = (f32[2,32,1024]{2,1,0:T(8,128)}, f32[8,128]{1,0:T(8,128)}, f32[8,6,1024]{2,1,0:T(8,128)}, f32[2,4,1024]{2,1,0:T(4,128)}) custom-call(f32[2]{0:T(128)} %broadcast_18_coef_ref.2.coef_ref, f32[2,32,1024]{2,1,0:T(8,128)} %multiply_add_fusion.1.f_ref, f32[6,2,32,1024]{3,2,1,0:T(8,128)} %bitcast.341, f32[24]{0:T(128)} %reshape.1625.masks_ref, ...), custom_call_target="tpu_custom_call" | custom-call | tf_op jit(solution)/shard_map/pallas_call | solution.py:251
  151.4 1.2 slice.441
  153.9 0.7 slice.442
  154.6 1.7 multiply_subtract_fusion.f_ref
  156.3 0.8 fusion.119
  157.5 0.7 fusion.112.coef_ref
  158.2 0.7 slice_select_fusion.3
  159.1 1.1 copy.276
  160.5 0.6 copy.280.rows_ref
  161.3 0.7 fusion.35.faces_ref
  162.0 17.1 %shard_map.73 = (f32[2,32,1024]{2,1,0:T(8,128)}, f32[8,128]{1,0:T(8,128)}, f32[8,6,1024]{2,1,0:T(8,128)}, f32[2,4,1024]{2,1,0:T(4,128)}) custom-call(f32[2]{0:T(128)} %fusion.112.coef_ref, f32[2,32,1024]{2,1,0:T(8,128)} %multiply_subtract_fusion.f_ref, f32[6,2,32,1024]{3,2,1,0:T(8,128)} %bitcast.342, f32[24]{0:T(128)} %reshape.1625.masks_ref, ...), custom_call_target="tpu_custom_call" | custom-call | tf_op jit(solution)/shard_map/pallas_call | solution.py:251
  179.2 1.3 slice.451
  181.8 0.7 slice_select_fusion.1
  182.7 0.8 fusion.118
  183.5 1.1 copy.281
  184.7 0.6 copy_add_fusion.rows_ref
  185.5 0.7 maximum_add_fusion.1.faces_ref
  186.2 0.7 multiply_add_fusion.f_ref
  186.9 17.4 %shard_map.74 = (f32[2,32,1024]{2,1,0:T(8,128)}, f32[8,128]{1,0:T(8,128)}, f32[8,6,1024]{2,1,0:T(8,128)}, f32[2,4,1024]{2,1,0:T(4,128)}) custom-call(f32[2]{0:T(128)} %broadcast_18_coef_ref.2.coef_ref, f32[2,32,1024]{2,1,0:T(8,128)} %multiply_add_fusion.f_ref, f32[6,2,32,1024]{3,2,1,0:T(8,128)} %bitcast.343, f32[24]{0:T(128)} %reshape.1625.masks_ref, ...), custom_call_target="tpu_custom_call" | custom-call | tf_op jit(solution)/shard_map/pallas_call | solution.py:251
  204.3 1.2 slice.460
  206.8 0.8 add_bitcast_fusion
  207.6 1.7 subtract_bitcast_fusion
  (179 shorter events, 11.5 us)
Async XLA Ops:
  6.6 8.1 %copy-start.9 = (f32[1,1,2,32,1024]{4,3,2,1,0:T(8,128)S(1)}, f32[1,1,2,32,1024]{4,3,2,1,0:T(8,128)}, u32[]{:S(2)}) copy-start(f32[1,1,2,32,1024]{4,3,2,1,0:T(8,128)} %param.9) | copy-start | bytes 786436
  12.4 3.5 %copy-start = (f32[1,1,6,2,32,1024]{5,4,3,2,1,0:T(8,128)S(1)}, f32[1,1,6,2,32,1024]{5,4,3,2,1,0:T(8,128)}, u32[]{:S(2)}) copy-start(f32[1,1,6,2,32,1024]{5,4,3,2,1,0:T(8,128)} %param.11) | copy-start | bytes 4718596
  14.6 1.9 copy-start.10
  16.2 0.7 copy-start.3
  17.0 28.7 %copy-start.1 = (f32[2,32,1024]{2,1,0:T(8,128)}, f32[2,32,1024]{2,1,0:T(8,128)S(1)}, u32[]{:S(2)}) copy-start(f32[2,32,1024]{2,1,0:T(8,128)S(1)} %get-tuple-element.81.diag_ref) | copy-start | bytes 786436
  43.1 4.4 %copy-start.11 = (f32[16,128]{1,0:T(8,128)S(1)}, f32[16,128]{1,0:T(8,128)}, u32[]{:S(2)}) copy-start(f32[16,128]{1,0:T(8,128)} %get-tuple-element.29) | copy-start | bytes 24580
  44.3 4.5 %copy-start.12 = (pred[32]{0:T(512)(128)(4,1)S(1)}, pred[32]{0:T(512)(128)(4,1)}, u32[]{:S(2)}) copy-start(pred[32]{0:T(512)(128)(4,1)} %constant.263.clone.1) | copy-start | bytes 100
  77.7 23.8 %copy-start.4 = (f32[2,32,1024]{2,1,0:T(8,128)S(1)}, f32[2,32,1024]{2,1,0:T(8,128)}, u32[]{:S(2)}) copy-start(f32[2,32,1024]{2,1,0:T(8,128)} %copy-done.3) | copy-start | bytes 786436
  107.1 22.9 %copy-start.5 = (f32[2,32,1024]{2,1,0:T(8,128)S(1)}, f32[2,32,1024]{2,1,0:T(8,128)}, u32[]{:S(2)}) copy-start(f32[2,32,1024]{2,1,0:T(8,128)} %get-tuple-element.33.f_ref) | copy-start | bytes 786436
  132.7 21.9 %copy-start.7 = (f32[2,32,1024]{2,1,0:T(8,128)S(1)}, f32[2,32,1024]{2,1,0:T(8,128)}, u32[]{:S(2)}) copy-start(f32[2,32,1024]{2,1,0:T(8,128)} %multiply_subtract_fusion.1.f_ref) | copy-start | bytes 786436
  162.0 24.2 %copy-start.2 = (f32[2,32,1024]{2,1,0:T(8,128)S(1)}, f32[2,32,1024]{2,1,0:T(8,128)}, u32[]{:S(2)}) copy-start(f32[2,32,1024]{2,1,0:T(8,128)} %multiply_add_fusion.1.f_ref) | copy-start | bytes 786436
  179.2 7.0 %copy-start.8 = (f32[2,32,1024]{2,1,0:T(8,128)S(1)}, f32[2,32,1024]{2,1,0:T(8,128)}, u32[]{:S(2)}) copy-start(f32[2,32,1024]{2,1,0:T(8,128)} %get-tuple-element.49) | copy-start | bytes 786436
  186.9 20.7 %copy-start.6 = (f32[2,32,1024]{2,1,0:T(8,128)S(1)}, f32[2,32,1024]{2,1,0:T(8,128)}, u32[]{:S(2)}) copy-start(f32[2,32,1024]{2,1,0:T(8,128)} %multiply_subtract_fusion.f_ref) | copy-start | bytes 786436

commit v4 on v3

--- a/solution.py
+++ b/solution.py
@@ -142,7 +142,15 @@
     spread_y = (spot % BS == pick).astype(jnp.float32)
 
     def spread(face, table):
-        return jnp.dot(face, table, precision=lax.Precision.HIGHEST, preferred_element_type=jnp.float32)
+        high = face.astype(jnp.bfloat16)
+        rest = face - high.astype(jnp.float32)
+        middle = rest.astype(jnp.bfloat16)
+        low = (rest - middle.astype(jnp.float32)).astype(jnp.bfloat16)
+        table = table.astype(jnp.bfloat16)
+        parts = [
+            jnp.dot(part, table, preferred_element_type=jnp.float32) for part in (high, middle, low)
+        ]
+        return (parts[0] + parts[1]) + parts[2]
 
     borders = [
         row == width - 1,

time: 211 us -> 204 us (0.967)
  Pallas kernels: 127 us -> 120 us
    pallas_call x6, Pallas kernels: 104 us -> 96.8 us  [one_round(): pl.pallas_call(functools.partial(round_kernel, smooth=smooth), out_shape=...]
where the time goes in v4:
time: 204 us; the launch traced here: 202 us
  Pallas kernels  120 us (59%)
  local copies, waits for them, and re-layouts  33.9 us (17%)
  other arithmetic  31.3 us (15%)
  between operations  13.1 us (6%)
  matrix products  3.51 us (2%)
    pallas_call x6, Pallas kernels, one_round(): pl.pallas_call(functools.partial(round_kernel, smooth=smooth), out_shape=...  96.8 us
    pallas_call x1, Pallas kernels, exchange(): pl.pallas_call(exchange_kernel, out_shape=(jax.ShapeDtypeStruct(tile.shap...  23 us
    pallas_call x5, local copies, waits for them, and re-layouts, one_round(): pl.pallas_call(functools.partial(round_kernel, smooth=smooth), out_shape=...  5.4 us
    select_n x6, other arithmetic, halo(): above = jnp.where(slab_index < grp_count - 1, z_land[1, :slot_count], fill)  4.59 us
    slice x7, local copies, waits for them, and re-layouts, halo(): field[1, :, :BS]  4.2 us

profile of v4, /device:TPU:0, one launch (start us, length us, event | category | flops | bytes accessed | tf_op | source)
XLA Modules:
  0.0 201.6 jit_solution(2927795353781287815)
XLA Ops:
  0.6 1.2 dynamic_slice.117
  4.6 1.4 fusion.101
  8.7 1.1 reduce_sum.122
  9.8 0.8 fusion.74
  11.5 0.7 reshape.1625.masks_ref
  12.4 2.2 %convolution_bitcast_fusion = f32[2,2,32,32]{3,2,0,1:T(8,128)S(1)} fusion(pred[2,32,1024,1]{2,1,0,3:T(32,128)(4,1)S(1)} %bitcast.344, f32[1,1,2,32,1024]{4,3,2,1,0:T(8,128)} %param.10, f32[1,1,6,2,32,1024]{5,4,3,2,1,0:T(8,128)} %param.11, f32[2]{0:T(128)S(1)} %get-tuple-element.171, f32[2]{0:T(128)S(1)} %get-tuple-element.172, f32[2]{0:T(128)S(1)} %get-tuple-element.170, ...), kind=kOutput, calls=%fused_computation | convolution fusion | flops 51511296 | bytes 2048120 | tf_op jit(solution)/shard_map/dot_general | solution.py:376
  15.3 0.6 pad_maximum_fusion.3.z_ref
  17.9 1.3 concatenate.95.xy_ref
  20.1 23.0 %shard_map.68 = (f32[16,128]{1,0:T(8,128)}, f32[8,12,1024]{2,1,0:T(8,128)}, f32[2,8,1024]{2,1,0:T(8,128)}) custom-call(f32[16,128]{1,0:T(8,128)} %pad_bitcast_fusion.x_ref, f32[12,1024]{1,0:T(8,128)} %concatenate.95.xy_ref, f32[8,1024]{1,0:T(8,128)} %pad_maximum_fusion.3.z_ref), custom_call_target="tpu_custom_call" | custom-call | tf_op jit(solution)/shard_map/pallas_call | solution.py:106
  43.1 0.9 slice_select_fusion.11
  44.3 1.3 copy.256
  46.1 0.6 copy.258.rows_ref
  46.8 0.7 multiply_divide_fusion.1.faces_ref
  49.1 2.9 %cholesky.19 = f32[32,32]{1,0:T(8,128)S(1)} custom-call(f32[32,32]{1,0:T(8,128)S(1)} %add_multiply_fusion), custom_call_target="Cholesky" | custom-call | tf_op jit(solution)/shard_map/jit(cholesky)/cholesky | solution.py:481
  52.0 0.7 compare_reduce_fusion
  52.7 0.6 fusion.50
  53.3 2.4 %custom-call.14 = f32[1,32,32]{1,2,0:T(8,128)S(1)} custom-call(f32[1,32,32]{2,1,0:T(8,128)S(1)} %fusion.50), custom_call_target="InvertDiagBlocksLowerTriangular" | custom-call | tf_op jit(solution)/shard_map/triangular_solve/custom-call.2 | solution.py:485
  56.1 0.6 fusion.103.coef_ref
  56.7 16.6 %shard_map.69 = (f32[2,32,1024]{2,1,0:T(8,128)}, f32[8,128]{1,0:T(8,128)}, f32[8,6,1024]{2,1,0:T(8,128)}, f32[2,4,1024]{2,1,0:T(4,128)}) custom-call(f32[2]{0:T(128)} %fusion.103.coef_ref, f32[2,32,1024]{2,1,0:T(8,128)} %copy-done.3, f32[6,2,32,1024]{3,2,1,0:T(8,128)} %bitcast.338, f32[24]{0:T(128)} %reshape.1625.masks_ref, f32[2,32,1024]{2,1,0:T(8,128)} %copy-done.1, ...), custom_call_target="tpu_custom_call" | custom-call | tf_op jit(solution)/shard_map/pallas_call | solution.py:259
  73.3 1.3 slice.413
  74.6 0.7 slice_select_fusion.9
  75.5 0.8 fusion.122
  76.3 1.1 copy.259
  77.7 0.6 copy.263.rows_ref
  78.3 0.7 pad_maximum_fusion.2.faces_ref
  79.5 16.5 %shard_map.70 = (f32[2,32,1024]{2,1,0:T(8,128)}, f32[8,128]{1,0:T(8,128)}, f32[8,6,1024]{2,1,0:T(8,128)}, f32[2,4,1024]{2,1,0:T(4,128)}) custom-call(f32[2]{0:T(128)} %broadcast_18_coef_ref.2.coef_ref, f32[2,32,1024]{2,1,0:T(8,128)} %get-tuple-element.33.f_ref, f32[6,2,32,1024]{3,2,1,0:T(8,128)} %bitcast.339, f32[24]{0:T(128)} %reshape.1625.masks_ref, ...), custom_call_target="tpu_custom_call" | custom-call | tf_op jit(solution)/shard_map/pallas_call | solution.py:259
  96.0 1.2 slice.422
  98.4 0.7 slice.423
  99.2 1.7 multiply_subtract_fusion.1.f_ref
  100.9 0.8 fusion.121
  102.6 0.7 slice_select_fusion.7
  103.5 1.1 copy.264
  104.9 0.6 copy.268.rows_ref
  105.5 0.7 multiply_divide_fusion.faces_ref
  106.2 15.7 %shard_map.71 = (f32[2,32,1024]{2,1,0:T(8,128)}, f32[8,128]{1,0:T(8,128)}, f32[8,6,1024]{2,1,0:T(8,128)}, f32[2,4,1024]{2,1,0:T(4,128)}) custom-call(f32[2]{0:T(128)} %fusion.107.coef_ref, f32[2,32,1024]{2,1,0:T(8,128)} %multiply_subtract_fusion.1.f_ref, f32[6,2,32,1024]{3,2,1,0:T(8,128)} %bitcast.340, f32[24]{0:T(128)} %reshape.1625.masks_ref, ...), custom_call_target="tpu_custom_call" | custom-call | tf_op jit(solution)/shard_map/pallas_call | solution.py:259
  121.9 1.2 slice.432
  124.4 0.7 slice_select_fusion.5
  125.3 0.8 fusion.120
  126.1 1.7 multiply_add_fusion.1.f_ref
  127.8 1.1 copy.269
  129.2 0.6 fusion.52.rows_ref
  129.8 0.7 maximum_add_fusion.faces_ref
  130.5 16.1 %shard_map.72 = (f32[2,32,1024]{2,1,0:T(8,128)}, f32[8,128]{1,0:T(8,128)}, f32[8,6,1024]{2,1,0:T(8,128)}, f32[2,4,1024]{2,1,0:T(4,128)}) custom-call(f32[2]{0:T(128)} %broadcast_18_coef_ref.2.coef_ref, f32[2,32,1024]{2,1,0:T(8,128)} %multiply_add_fusion.1.f_ref, f32[6,2,32,1024]{3,2,1,0:T(8,128)} %bitcast.341, f32[24]{0:T(128)} %reshape.1625.masks_ref, ...), custom_call_target="tpu_custom_call" | custom-call | tf_op jit(solution)/shard_map/pallas_call | solution.py:259
  146.6 1.2 slice.441
  149.0 0.7 slice.442
  149.8 1.7 multiply_subtract_fusion.f_ref
  151.4 0.8 fusion.119
  152.6 0.7 fusion.112.coef_ref
  153.3 0.7 slice_select_fusion.3
  154.2 1.1 copy.276
  155.4 0.6 copy.280.rows_ref
  156.2 0.7 fusion.35.faces_ref
  156.9 15.7 %shard_map.73 = (f32[2,32,1024]{2,1,0:T(8,128)}, f32[8,128]{1,0:T(8,128)}, f32[8,6,1024]{2,1,0:T(8,128)}, f32[2,4,1024]{2,1,0:T(4,128)}) custom-call(f32[2]{0:T(128)} %fusion.112.coef_ref, f32[2,32,1024]{2,1,0:T(8,128)} %multiply_subtract_fusion.f_ref, f32[6,2,32,1024]{3,2,1,0:T(8,128)} %bitcast.342, f32[24]{0:T(128)} %reshape.1625.masks_ref, ...), custom_call_target="tpu_custom_call" | custom-call | tf_op jit(solution)/shard_map/pallas_call | solution.py:259
  172.6 1.3 slice.451
  175.2 0.7 slice_select_fusion.1
  176.1 0.8 fusion.118
  177.0 1.1 copy.281
  178.1 0.6 copy_add_fusion.rows_ref
  178.9 0.7 maximum_add_fusion.1.faces_ref
  179.6 0.7 multiply_add_fusion.f_ref
  180.4 16.2 %shard_map.74 = (f32[2,32,1024]{2,1,0:T(8,128)}, f32[8,128]{1,0:T(8,128)}, f32[8,6,1024]{2,1,0:T(8,128)}, f32[2,4,1024]{2,1,0:T(4,128)}) custom-call(f32[2]{0:T(128)} %broadcast_18_coef_ref.2.coef_ref, f32[2,32,1024]{2,1,0:T(8,128)} %multiply_add_fusion.f_ref, f32[6,2,32,1024]{3,2,1,0:T(8,128)} %bitcast.343, f32[24]{0:T(128)} %reshape.1625.masks_ref, ...), custom_call_target="tpu_custom_call" | custom-call | tf_op jit(solution)/shard_map/pallas_call | solution.py:259
  196.6 1.2 slice.460
  199.1 0.8 add_bitcast_fusion
  199.9 1.7 subtract_bitcast_fusion
  (179 shorter events, 11.3 us)
Async XLA Ops:
  6.6 8.1 %copy-start.9 = (f32[1,1,2,32,1024]{4,3,2,1,0:T(8,128)S(1)}, f32[1,1,2,32,1024]{4,3,2,1,0:T(8,128)}, u32[]{:S(2)}) copy-start(f32[1,1,2,32,1024]{4,3,2,1,0:T(8,128)} %param.9) | copy-start | bytes 786436
  12.4 3.5 %copy-start = (f32[1,1,6,2,32,1024]{5,4,3,2,1,0:T(8,128)S(1)}, f32[1,1,6,2,32,1024]{5,4,3,2,1,0:T(8,128)}, u32[]{:S(2)}) copy-start(f32[1,1,6,2,32,1024]{5,4,3,2,1,0:T(8,128)} %param.11) | copy-start | bytes 4718596
  14.6 1.9 copy-start.10
  16.2 0.7 copy-start.3
  17.0 28.7 %copy-start.1 = (f32[2,32,1024]{2,1,0:T(8,128)}, f32[2,32,1024]{2,1,0:T(8,128)S(1)}, u32[]{:S(2)}) copy-start(f32[2,32,1024]{2,1,0:T(8,128)S(1)} %get-tuple-element.81.diag_ref) | copy-start | bytes 786436
  43.1 4.4 %copy-start.11 = (f32[16,128]{1,0:T(8,128)S(1)}, f32[16,128]{1,0:T(8,128)}, u32[]{:S(2)}) copy-start(f32[16,128]{1,0:T(8,128)} %get-tuple-element.29) | copy-start | bytes 24580
  44.3 4.5 %copy-start.12 = (pred[32]{0:T(512)(128)(4,1)S(1)}, pred[32]{0:T(512)(128)(4,1)}, u32[]{:S(2)}) copy-start(pred[32]{0:T(512)(128)(4,1)} %constant.263.clone.1) | copy-start | bytes 100
  76.3 22.8 %copy-start.4 = (f32[2,32,1024]{2,1,0:T(8,128)S(1)}, f32[2,32,1024]{2,1,0:T(8,128)}, u32[]{:S(2)}) copy-start(f32[2,32,1024]{2,1,0:T(8,128)} %copy-done.3) | copy-start | bytes 786436
  104.8 21.4 %copy-start.5 = (f32[2,32,1024]{2,1,0:T(8,128)S(1)}, f32[2,32,1024]{2,1,0:T(8,128)}, u32[]{:S(2)}) copy-start(f32[2,32,1024]{2,1,0:T(8,128)} %get-tuple-element.33.f_ref) | copy-start | bytes 786436
  128.9 20.9 %copy-start.7 = (f32[2,32,1024]{2,1,0:T(8,128)S(1)}, f32[2,32,1024]{2,1,0:T(8,128)}, u32[]{:S(2)}) copy-start(f32[2,32,1024]{2,1,0:T(8,128)} %multiply_subtract_fusion.1.f_ref) | copy-start | bytes 786436
  156.9 22.7 %copy-start.2 = (f32[2,32,1024]{2,1,0:T(8,128)S(1)}, f32[2,32,1024]{2,1,0:T(8,128)}, u32[]{:S(2)}) copy-start(f32[2,32,1024]{2,1,0:T(8,128)} %multiply_add_fusion.1.f_ref) | copy-start | bytes 786436
  172.6 7.0 %copy-start.8 = (f32[2,32,1024]{2,1,0:T(8,128)S(1)}, f32[2,32,1024]{2,1,0:T(8,128)}, u32[]{:S(2)}) copy-start(f32[2,32,1024]{2,1,0:T(8,128)} %get-tuple-element.49) | copy-start | bytes 786436
  180.4 19.6 %copy-start.6 = (f32[2,32,1024]{2,1,0:T(8,128)S(1)}, f32[2,32,1024]{2,1,0:T(8,128)}, u32[]{:S(2)}) copy-start(f32[2,32,1024]{2,1,0:T(8,128)} %multiply_subtract_fusion.f_ref) | copy-start | bytes 786436

commit v5 on v4

--- a/solution.py
+++ b/solution.py
@@ -21,6 +21,7 @@
 def share(
     x_ref, xy_ref, z_ref, o_ref, xy_out, z_out, landed_b, landed_g, landed_xy, landed_z,
     send_b, recv_b, send_g, recv_g, send_xy, recv_xy, send_z, recv_z, brick_peers, grp_peers,
+    dot_ref=None,
 ):
     here_brick = lax.axis_index("brick")
     here_grp = lax.axis_index("grp")
@@ -74,6 +75,11 @@
     landed_xy[0] = xy_ref[...]
     xy_out[...] = landed_xy[...]
     z_out[...] = landed_z[...]
+    if dot_ref is not None:
+        tile_rows, tile_lanes = o_ref.shape
+        first = lax.broadcasted_iota(jnp.int32, (tile_rows, tile_lanes), 0) * tile_lanes
+        first = first + lax.broadcasted_iota(jnp.int32, (tile_rows, tile_lanes), 1)
+        dot_ref[0] = jnp.sum(jnp.where(first == 0, total, 0.0))
 
 
 def exchange_kernel(
@@ -213,7 +219,7 @@
 
 def round_kernel(
     coef_ref, f_ref, bonds_ref, masks_ref, diag_ref, rows_ref, faces_ref,
-    o_ref, total_ref, xy_out, z_out,
+    o_ref, total_ref, xy_out, z_out, dot_ref,
     xy_buf, z_buf, tile_buf, landed_b, landed_g, landed_xy, landed_z,
     send_b, recv_b, send_g, recv_g, send_xy, recv_xy, send_z, recv_z, *, smooth
 ):
@@ -243,6 +249,7 @@
     share(
         tile_buf, xy_buf, z_buf, total_ref, xy_out, z_out, landed_b, landed_g, landed_xy, landed_z,
         send_b, recv_b, send_g, recv_g, send_xy, recv_xy, send_z, recv_z, brick_peers, grp_peers,
+        dot_ref=dot_ref,
     )
 
 
@@ -263,9 +270,10 @@
             jax.ShapeDtypeStruct(tile, jnp.float32),
             jax.ShapeDtypeStruct((n_brick,) + xy, jnp.float32),
             jax.ShapeDtypeStruct((2,) + z, jnp.float32),
+            jax.ShapeDtypeStruct((1,), jnp.float32),
         ),
         in_specs=[smem, vmem, vmem, smem, vmem, vmem, vmem],
-        out_specs=(vmem, vmem, vmem, vmem),
+        out_specs=(vmem, vmem, vmem, vmem, smem),
         scratch_shapes=[
             pltpu.VMEM(xy, jnp.float32),
             pltpu.VMEM(z, jnp.float32),
@@ -488,18 +496,18 @@
         return lax.dynamic_slice_in_dim(result[:, 0], slab_index * slot_count, slot_count)
 
     def round_trip(field, field_halo, coef, smooth):
-        out, total, xy_land, z_land = one_round(
+        out, total, xy_land, z_land, dot = one_round(
             field, bonds, masks, diagonal, *field_halo, coef, smooth
         )
         total = total.reshape(-1)
         out_halo = halo(out, xy_land, z_land, 0.0)
         if smooth:
-            return out, total[0], None, out_halo
+            return out, dot[0], None, out_halo
         count = brick_count * grp_count * slot_count
         mine = lax.dynamic_index_in_dim(
             total[1 : 1 + count].reshape(brick_count, -1), brick_index, keepdims=False
         )
-        return out, total[0], mine, out_halo
+        return out, dot[0], mine, out_halo
 
     def precondition(residual_field, field_halo, terms):
         smoothed_halo = [OMEGA * part / scale for part, scale in zip(field_halo, diagonal_halo)]

time: 204 us -> 197 us (0.966)
  local copies, waits for them, and re-layouts: 33.9 us -> 26.5 us
    slice x6 -> x0, local copies, waits for them, and re-layouts: 7.33 us -> none  [the longest x3 3.76 us: round_trip(): return (out, total[0], None, out_halo)]
where the time goes in v5:
time: 197 us; the launch traced here: 195 us
  Pallas kernels  120 us (61%)
  other arithmetic  31.3 us (16%)
  local copies, waits for them, and re-layouts  26.5 us (13%)
  between operations  13.6 us (7%)
  matrix products  3.5 us (2%)
    pallas_call x6, Pallas kernels, one_round(): pl.pallas_call(functools.partial(round_kernel, smooth=smooth), out_shape=...  97 us
    pallas_call x1, Pallas kernels, exchange(): pl.pallas_call(exchange_kernel, out_shape=(jax.ShapeDtypeStruct(tile.shap...  23 us
    pallas_call x5, local copies, waits for them, and re-layouts, one_round(): pl.pallas_call(functools.partial(round_kernel, smooth=smooth), out_shape=...  5.35 us
    select_n x6, other arithmetic, halo(): above = jnp.where(slab_index < grp_count - 1, z_land[1, :slot_count], fill)  4.59 us
    slice x7, local copies, waits for them, and re-layouts, halo(): field[1, :, :BS]  4.22 us

profile of v5, /device:TPU:0, one launch (start us, length us, event | category | flops | bytes accessed | tf_op | source)
XLA Modules:
  0.0 194.8 jit_solution(5202654177863737024)
XLA Ops:
  0.6 1.2 dynamic_slice.117
  4.6 1.4 fusion.101
  8.7 1.1 reduce_sum.122
  9.8 0.8 fusion.74
  11.5 0.7 reshape.1613.masks_ref
  12.4 2.2 %convolution_bitcast_fusion = f32[2,2,32,32]{3,2,0,1:T(8,128)S(1)} fusion(pred[2,32,1024,1]{2,1,0,3:T(32,128)(4,1)S(1)} %bitcast.340, f32[1,1,2,32,1024]{4,3,2,1,0:T(8,128)} %param.10, f32[1,1,6,2,32,1024]{5,4,3,2,1,0:T(8,128)} %param.11, f32[2]{0:T(128)S(1)} %get-tuple-element.175, f32[2]{0:T(128)S(1)} %get-tuple-element.176, f32[2]{0:T(128)S(1)} %get-tuple-element.174, ...), kind=kOutput, calls=%fused_computation | convolution fusion | flops 51511296 | bytes 2048120 | tf_op jit(solution)/shard_map/dot_general | solution.py:384
  14.6 0.5 convolution_bitcast_fusion.1
  15.3 0.6 pad_maximum_fusion.3.z_ref
  15.9 0.3 fusion.116
  16.5 0.4 fusion.18
  17.9 1.3 concatenate.95.xy_ref
  19.5 0.6 pad_bitcast_fusion.x_ref
  20.1 23.0 %shard_map.68 = (f32[16,128]{1,0:T(8,128)}, f32[8,12,1024]{2,1,0:T(8,128)}, f32[2,8,1024]{2,1,0:T(8,128)}) custom-call(f32[16,128]{1,0:T(8,128)} %pad_bitcast_fusion.x_ref, f32[12,1024]{1,0:T(8,128)} %concatenate.95.xy_ref, f32[8,1024]{1,0:T(8,128)} %pad_maximum_fusion.3.z_ref), custom_call_target="tpu_custom_call" | custom-call | tf_op jit(solution)/shard_map/pallas_call | solution.py:112
  43.1 0.9 slice_select_fusion.11
  44.3 1.3 copy.256
  46.1 0.6 copy.258.rows_ref
  46.8 0.7 multiply_divide_fusion.1.faces_ref
  49.1 2.9 %cholesky.19 = f32[32,32]{1,0:T(8,128)S(1)} custom-call(f32[32,32]{1,0:T(8,128)S(1)} %add_multiply_fusion), custom_call_target="Cholesky" | custom-call | tf_op jit(solution)/shard_map/jit(cholesky)/cholesky | solution.py:489
  52.0 0.7 compare_reduce_fusion
  52.7 0.6 fusion.50
  53.3 2.4 %custom-call.14 = f32[1,32,32]{1,2,0:T(8,128)S(1)} custom-call(f32[1,32,32]{2,1,0:T(8,128)S(1)} %fusion.50), custom_call_target="InvertDiagBlocksLowerTriangular" | custom-call | tf_op jit(solution)/shard_map/triangular_solve/custom-call.2 | solution.py:493
  56.1 0.6 fusion.103.coef_ref
  56.6 16.6 %shard_map.69 = (f32[2,32,1024]{2,1,0:T(8,128)}, f32[8,128]{1,0:T(8,128)}, f32[8,6,1024]{2,1,0:T(8,128)}, f32[2,4,1024]{2,1,0:T(4,128)}, f32[1]{0:T(128)}) custom-call(f32[2]{0:T(128)} %fusion.103.coef_ref, f32[2,32,1024]{2,1,0:T(8,128)} %copy-done.3, f32[6,2,32,1024]{3,2,1,0:T(8,128)} %bitcast.334, f32[24]{0:T(128)} %reshape.1613.masks_ref, ...), custom_call_target="tpu_custom_call" | custom-call | tf_op jit(solution)/shard_map/pallas_call | solution.py:266
  73.3 1.1 copy.259
  74.6 0.6 copy.263.rows_ref
  75.2 0.7 slice_select_fusion.9
  76.1 0.8 fusion.122
  77.0 0.7 pad_maximum_fusion.2.faces_ref
  77.6 0.5 broadcast_18_coef_ref.2.coef_ref
  78.2 16.5 %shard_map.70 = (f32[2,32,1024]{2,1,0:T(8,128)}, f32[8,128]{1,0:T(8,128)}, f32[8,6,1024]{2,1,0:T(8,128)}, f32[2,4,1024]{2,1,0:T(4,128)}, f32[1]{0:T(128)}) custom-call(f32[2]{0:T(128)} %broadcast_18_coef_ref.2.coef_ref, f32[2,32,1024]{2,1,0:T(8,128)} %get-tuple-element.35.f_ref, f32[6,2,32,1024]{3,2,1,0:T(8,128)} %bitcast.335, f32[24]{0:T(128)} %reshape.1613.masks_ref, ...), custom_call_target="tpu_custom_call" | custom-call | tf_op jit(solution)/shard_map/pallas_call | solution.py:266
  96.1 1.7 multiply_subtract_fusion.1.f_ref
  97.8 0.7 slice.403
  98.9 0.6 fusion.107.coef_ref
  99.5 0.7 slice_select_fusion.7
  100.4 0.8 fusion.121
  101.2 1.1 copy.264
  102.6 0.6 copy.268.rows_ref
  103.2 0.7 multiply_divide_fusion.faces_ref
  103.9 15.8 %shard_map.71 = (f32[2,32,1024]{2,1,0:T(8,128)}, f32[8,128]{1,0:T(8,128)}, f32[8,6,1024]{2,1,0:T(8,128)}, f32[2,4,1024]{2,1,0:T(4,128)}, f32[1]{0:T(128)}) custom-call(f32[2]{0:T(128)} %fusion.107.coef_ref, f32[2,32,1024]{2,1,0:T(8,128)} %multiply_subtract_fusion.1.f_ref, f32[6,2,32,1024]{3,2,1,0:T(8,128)} %bitcast.336, f32[24]{0:T(128)} %reshape.1613.masks_ref, ...), custom_call_target="tpu_custom_call" | custom-call | tf_op jit(solution)/shard_map/pallas_call | solution.py:266
  121.1 1.1 copy.269
  122.4 0.6 fusion.52.rows_ref
  123.0 0.7 slice_select_fusion.5
  123.9 0.8 fusion.120
  124.7 1.7 multiply_add_fusion.1.f_ref
  126.4 0.7 maximum_add_fusion.faces_ref
  127.1 16.1 %shard_map.72 = (f32[2,32,1024]{2,1,0:T(8,128)}, f32[8,128]{1,0:T(8,128)}, f32[8,6,1024]{2,1,0:T(8,128)}, f32[2,4,1024]{2,1,0:T(4,128)}, f32[1]{0:T(128)}) custom-call(f32[2]{0:T(128)} %broadcast_18_coef_ref.2.coef_ref, f32[2,32,1024]{2,1,0:T(8,128)} %multiply_add_fusion.1.f_ref, f32[6,2,32,1024]{3,2,1,0:T(8,128)} %bitcast.337, f32[24]{0:T(128)} %reshape.1613.masks_ref, ...), custom_call_target="tpu_custom_call" | custom-call | tf_op jit(solution)/shard_map/pallas_call | solution.py:266
  144.6 1.7 multiply_subtract_fusion.f_ref
  146.3 0.7 slice.420
  147.4 0.7 fusion.112.coef_ref
  148.1 0.7 slice_select_fusion.3
  149.0 0.8 fusion.119
  149.8 1.1 copy.276
  151.0 0.6 copy.280.rows_ref
  151.8 0.7 fusion.35.faces_ref
  152.5 15.7 %shard_map.73 = (f32[2,32,1024]{2,1,0:T(8,128)}, f32[8,128]{1,0:T(8,128)}, f32[8,6,1024]{2,1,0:T(8,128)}, f32[2,4,1024]{2,1,0:T(4,128)}, f32[1]{0:T(128)}) custom-call(f32[2]{0:T(128)} %fusion.112.coef_ref, f32[2,32,1024]{2,1,0:T(8,128)} %multiply_subtract_fusion.f_ref, f32[6,2,32,1024]{3,2,1,0:T(8,128)} %bitcast.338, f32[24]{0:T(128)} %reshape.1613.masks_ref, ...), custom_call_target="tpu_custom_call" | custom-call | tf_op jit(solution)/shard_map/pallas_call | solution.py:266
  169.6 1.1 copy.281
  170.8 0.6 copy_add_fusion.rows_ref
  171.5 0.7 slice_select_fusion.1
  172.5 0.8 fusion.118
  173.3 0.7 maximum_add_fusion.1.faces_ref
  174.0 0.7 multiply_add_fusion.f_ref
  174.8 16.2 %shard_map.74 = (f32[2,32,1024]{2,1,0:T(8,128)}, f32[8,128]{1,0:T(8,128)}, f32[8,6,1024]{2,1,0:T(8,128)}, f32[2,4,1024]{2,1,0:T(4,128)}, f32[1]{0:T(128)}) custom-call(f32[2]{0:T(128)} %broadcast_18_coef_ref.2.coef_ref, f32[2,32,1024]{2,1,0:T(8,128)} %multiply_add_fusion.f_ref, f32[6,2,32,1024]{3,2,1,0:T(8,128)} %bitcast.339, f32[24]{0:T(128)} %reshape.1613.masks_ref, ...), custom_call_target="tpu_custom_call" | custom-call | tf_op jit(solution)/shard_map/pallas_call | solution.py:266
  192.4 0.8 add_bitcast_fusion
  193.2 1.7 subtract_bitcast_fusion
  (173 shorter events, 8.4 us)
Async XLA Ops:
  6.6 8.1 %copy-start.9 = (f32[1,1,2,32,1024]{4,3,2,1,0:T(8,128)S(1)}, f32[1,1,2,32,1024]{4,3,2,1,0:T(8,128)}, u32[]{:S(2)}) copy-start(f32[1,1,2,32,1024]{4,3,2,1,0:T(8,128)} %param.9) | copy-start | bytes 786436
  12.4 3.5 %copy-start = (f32[1,1,6,2,32,1024]{5,4,3,2,1,0:T(8,128)S(1)}, f32[1,1,6,2,32,1024]{5,4,3,2,1,0:T(8,128)}, u32[]{:S(2)}) copy-start(f32[1,1,6,2,32,1024]{5,4,3,2,1,0:T(8,128)} %param.11) | copy-start | bytes 4718596
  14.6 1.9 copy-start.10
  16.2 0.7 copy-start.3
  17.0 28.7 %copy-start.1 = (f32[2,32,1024]{2,1,0:T(8,128)}, f32[2,32,1024]{2,1,0:T(8,128)S(1)}, u32[]{:S(2)}) copy-start(f32[2,32,1024]{2,1,0:T(8,128)S(1)} %get-tuple-element.85.diag_ref) | copy-start | bytes 786436
  43.1 4.4 %copy-start.11 = (f32[16,128]{1,0:T(8,128)S(1)}, f32[16,128]{1,0:T(8,128)}, u32[]{:S(2)}) copy-start(f32[16,128]{1,0:T(8,128)} %get-tuple-element.31) | copy-start | bytes 24580
  44.3 4.5 %copy-start.12 = (pred[32]{0:T(512)(128)(4,1)S(1)}, pred[32]{0:T(512)(128)(4,1)}, u32[]{:S(2)}) copy-start(pred[32]{0:T(512)(128)(4,1)} %constant.263.clone.1) | copy-start | bytes 100
  74.4 21.7 %copy-start.4 = (f32[2,32,1024]{2,1,0:T(8,128)S(1)}, f32[2,32,1024]{2,1,0:T(8,128)}, u32[]{:S(2)}) copy-start(f32[2,32,1024]{2,1,0:T(8,128)} %copy-done.3) | copy-start | bytes 786436
  103.9 20.9 %copy-start.5 = (f32[2,32,1024]{2,1,0:T(8,128)S(1)}, f32[2,32,1024]{2,1,0:T(8,128)}, u32[]{:S(2)}) copy-start(f32[2,32,1024]{2,1,0:T(8,128)} %get-tuple-element.35.f_ref) | copy-start | bytes 786436
  126.4 18.2 %copy-start.7 = (f32[2,32,1024]{2,1,0:T(8,128)S(1)}, f32[2,32,1024]{2,1,0:T(8,128)}, u32[]{:S(2)}) copy-start(f32[2,32,1024]{2,1,0:T(8,128)} %multiply_subtract_fusion.1.f_ref) | copy-start | bytes 786436
  152.5 21.5 %copy-start.2 = (f32[2,32,1024]{2,1,0:T(8,128)S(1)}, f32[2,32,1024]{2,1,0:T(8,128)}, u32[]{:S(2)}) copy-start(f32[2,32,1024]{2,1,0:T(8,128)} %multiply_add_fusion.1.f_ref) | copy-start | bytes 786436
  168.2 5.8 %copy-start.8 = (f32[2,32,1024]{2,1,0:T(8,128)S(1)}, f32[2,32,1024]{2,1,0:T(8,128)}, u32[]{:S(2)}) copy-start(f32[2,32,1024]{2,1,0:T(8,128)} %get-tuple-element.53) | copy-start | bytes 786436
  174.8 18.4 %copy-start.6 = (f32[2,32,1024]{2,1,0:T(8,128)S(1)}, f32[2,32,1024]{2,1,0:T(8,128)}, u32[]{:S(2)}) copy-start(f32[2,32,1024]{2,1,0:T(8,128)} %multiply_subtract_fusion.f_ref) | copy-start | bytes 786436

commit v6 on v5

--- a/solution.py
+++ b/solution.py
@@ -381,9 +381,16 @@
     picker = picker.astype(jnp.float32)
 
     def side_faces(field):
-        picked = jnp.dot(
-            field.reshape(slot_count * BS, face_size), picker, precision=lax.Precision.HIGHEST
-        )
+        rows_of = field.reshape(slot_count * BS, face_size)
+        high = rows_of.astype(jnp.bfloat16)
+        rest = rows_of - high.astype(jnp.float32)
+        middle = rest.astype(jnp.bfloat16)
+        low = (rest - middle.astype(jnp.float32)).astype(jnp.bfloat16)
+        table = picker.astype(jnp.bfloat16)
+        parts = [
+            jnp.dot(part, table, preferred_element_type=jnp.float32) for part in (high, middle, low)
+        ]
+        picked = (parts[0] + parts[1]) + parts[2]
         z = picked.reshape(slot_count, BS, 2, BS).transpose(2, 0, 1, 3)
         xy = jnp.concatenate(
             [

time: 197 us -> 198 us (level)
  local copies, waits for them, and re-layouts: 26.5 us -> 30.3 us
where the time goes in v6:
time: 198 us; the launch traced here: 196 us
  Pallas kernels  120 us (61%)
  other arithmetic  30.8 us (16%)
  local copies, waits for them, and re-layouts  30.3 us (15%)
  between operations  13.1 us (7%)
    pallas_call x6, Pallas kernels, one_round(): pl.pallas_call(functools.partial(round_kernel, smooth=smooth), out_shape=...  97 us
    pallas_call x1, Pallas kernels, exchange(): pl.pallas_call(exchange_kernel, out_shape=(jax.ShapeDtypeStruct(tile.shap...  23 us
    pallas_call x5, local copies, waits for them, and re-layouts, one_round(): pl.pallas_call(functools.partial(round_kernel, smooth=smooth), out_shape=...  5.47 us
    slice x7, local copies, waits for them, and re-layouts, halo(): field[1, :, :BS]  4.19 us

profile of v6, /device:TPU:0, one launch (start us, length us, event | category | flops | bytes accessed | tf_op | source)
XLA Modules:
  0.0 196.1 jit_solution(17225434818211090617)
XLA Ops:
  0.6 1.2 dynamic_slice.117
  4.5 0.8 fusion.46
  6.8 1.5 fusion.89
  11.0 0.6 pad_maximum_fusion.3.z_ref
  11.6 0.9 fusion.12
  12.8 1.5 fusion.88
  14.6 1.3 concatenate.95.xy_ref
  16.1 0.9 slice_reduce_fusion.2
  17.3 0.6 compare_select_fusion.5
  17.9 0.7 stack.226
  19.0 0.6 pad_bitcast_fusion.x_ref
  19.6 23.0 %shard_map.68 = (f32[16,128]{1,0:T(8,128)}, f32[8,12,1024]{2,1,0:T(8,128)}, f32[2,8,1024]{2,1,0:T(8,128)}) custom-call(f32[16,128]{1,0:T(8,128)} %pad_bitcast_fusion.x_ref, f32[12,1024]{1,0:T(8,128)} %concatenate.95.xy_ref, f32[8,1024]{1,0:T(8,128)} %pad_maximum_fusion.3.z_ref), custom_call_target="tpu_custom_call" | custom-call | tf_op jit(solution)/shard_map/pallas_call | solution.py:112
  42.7 1.3 copy.256
  44.1 0.7 fusion.73
  46.8 0.7 multiply_divide_fusion.1.faces_ref
  48.9 0.6 copy.258.rows_ref
  50.2 0.6 reshape.1438.masks_ref
  52.3 2.9 %cholesky.19 = f32[32,32]{1,0:T(8,128)S(1)} custom-call(f32[32,32]{1,0:T(8,128)S(1)} %add_multiply_fusion), custom_call_target="Cholesky" | custom-call | tf_op jit(solution)/shard_map/jit(cholesky)/cholesky | solution.py:496
  55.2 0.7 compare_reduce_fusion
  55.9 0.6 fusion.22
  56.6 2.4 %custom-call.14 = f32[1,32,32]{1,2,0:T(8,128)S(1)} custom-call(f32[1,32,32]{2,1,0:T(8,128)S(1)} %fusion.22), custom_call_target="InvertDiagBlocksLowerTriangular" | custom-call | tf_op jit(solution)/shard_map/triangular_solve/custom-call.2 | solution.py:500
  59.5 0.7 fusion.75.coef_ref
  60.2 16.7 %shard_map.69 = (f32[2,32,1024]{2,1,0:T(8,128)}, f32[8,128]{1,0:T(8,128)}, f32[8,6,1024]{2,1,0:T(8,128)}, f32[2,4,1024]{2,1,0:T(4,128)}, f32[1]{0:T(128)}) custom-call(f32[2]{0:T(128)} %fusion.75.coef_ref, f32[2,32,1024]{2,1,0:T(8,128)} %copy-done.3, f32[6,2,32,1024]{3,2,1,0:T(8,128)} %bitcast.336, f32[24]{0:T(128)} %reshape.1438.masks_ref, ...), custom_call_target="tpu_custom_call" | custom-call | tf_op jit(solution)/shard_map/pallas_call | solution.py:266
  76.8 1.1 copy.259
  78.0 0.8 fusion.95
  78.9 0.7 slice_select_fusion.9
  79.8 0.7 pad_maximum_fusion.2.faces_ref
  80.6 0.6 copy.263.rows_ref
  81.2 0.5 broadcast_18_coef_ref.2.coef_ref
  81.7 16.5 %shard_map.70 = (f32[2,32,1024]{2,1,0:T(8,128)}, f32[8,128]{1,0:T(8,128)}, f32[8,6,1024]{2,1,0:T(8,128)}, f32[2,4,1024]{2,1,0:T(4,128)}, f32[1]{0:T(128)}) custom-call(f32[2]{0:T(128)} %broadcast_18_coef_ref.2.coef_ref, f32[2,32,1024]{2,1,0:T(8,128)} %get-tuple-element.35.f_ref, f32[6,2,32,1024]{3,2,1,0:T(8,128)} %bitcast.337, f32[24]{0:T(128)} %reshape.1438.masks_ref, ...), custom_call_target="tpu_custom_call" | custom-call | tf_op jit(solution)/shard_map/pallas_call | solution.py:266
  98.2 1.1 copy.264
  99.5 0.8 fusion.94
  100.3 0.7 slice_select_fusion.7
  102.6 0.7 multiply_divide_fusion.faces_ref
  103.4 0.6 copy.268.rows_ref
  104.0 0.7 multiply_subtract_fusion.1.f_ref
  104.8 0.7 slice.403
  105.9 0.6 fusion.79.coef_ref
  106.5 15.8 %shard_map.71 = (f32[2,32,1024]{2,1,0:T(8,128)}, f32[8,128]{1,0:T(8,128)}, f32[8,6,1024]{2,1,0:T(8,128)}, f32[2,4,1024]{2,1,0:T(4,128)}, f32[1]{0:T(128)}) custom-call(f32[2]{0:T(128)} %fusion.79.coef_ref, f32[2,32,1024]{2,1,0:T(8,128)} %multiply_subtract_fusion.1.f_ref, f32[6,2,32,1024]{3,2,1,0:T(8,128)} %bitcast.338, f32[24]{0:T(128)} %reshape.1438.masks_ref, ...), custom_call_target="tpu_custom_call" | custom-call | tf_op jit(solution)/shard_map/pallas_call | solution.py:266
  122.2 1.1 copy.269
  123.4 0.8 fusion.93
  124.3 0.7 slice_select_fusion.5
  126.6 0.7 maximum_add_fusion.faces_ref
  127.3 0.6 fusion.24.rows_ref
  128.0 1.7 multiply_add_fusion.1.f_ref
  129.7 16.2 %shard_map.72 = (f32[2,32,1024]{2,1,0:T(8,128)}, f32[8,128]{1,0:T(8,128)}, f32[8,6,1024]{2,1,0:T(8,128)}, f32[2,4,1024]{2,1,0:T(4,128)}, f32[1]{0:T(128)}) custom-call(f32[2]{0:T(128)} %broadcast_18_coef_ref.2.coef_ref, f32[2,32,1024]{2,1,0:T(8,128)} %multiply_add_fusion.1.f_ref, f32[6,2,32,1024]{3,2,1,0:T(8,128)} %bitcast.339, f32[24]{0:T(128)} %reshape.1438.masks_ref, ...), custom_call_target="tpu_custom_call" | custom-call | tf_op jit(solution)/shard_map/pallas_call | solution.py:266
  145.8 1.1 copy.276
  147.1 0.8 fusion.92
  148.0 0.7 slice_select_fusion.3
  150.2 0.7 fusion.21.faces_ref
  151.0 0.6 copy.280.rows_ref
  151.6 0.7 multiply_subtract_fusion.f_ref
  152.3 0.7 slice.420
  153.4 0.7 fusion.84.coef_ref
  154.1 15.7 %shard_map.73 = (f32[2,32,1024]{2,1,0:T(8,128)}, f32[8,128]{1,0:T(8,128)}, f32[8,6,1024]{2,1,0:T(8,128)}, f32[2,4,1024]{2,1,0:T(4,128)}, f32[1]{0:T(128)}) custom-call(f32[2]{0:T(128)} %fusion.84.coef_ref, f32[2,32,1024]{2,1,0:T(8,128)} %multiply_subtract_fusion.f_ref, f32[6,2,32,1024]{3,2,1,0:T(8,128)} %bitcast.340, f32[24]{0:T(128)} %reshape.1438.masks_ref, ...), custom_call_target="tpu_custom_call" | custom-call | tf_op jit(solution)/shard_map/pallas_call | solution.py:266
  169.9 1.1 copy.281
  171.1 0.8 fusion.91
  172.0 0.7 slice_select_fusion.1
  174.2 0.7 maximum_add_fusion.1.faces_ref
  175.0 0.6 copy_add_fusion.rows_ref
  175.6 0.7 multiply_add_fusion.f_ref
  176.3 16.1 %shard_map.74 = (f32[2,32,1024]{2,1,0:T(8,128)}, f32[8,128]{1,0:T(8,128)}, f32[8,6,1024]{2,1,0:T(8,128)}, f32[2,4,1024]{2,1,0:T(4,128)}, f32[1]{0:T(128)}) custom-call(f32[2]{0:T(128)} %broadcast_18_coef_ref.2.coef_ref, f32[2,32,1024]{2,1,0:T(8,128)} %multiply_add_fusion.f_ref, f32[6,2,32,1024]{3,2,1,0:T(8,128)} %bitcast.341, f32[24]{0:T(128)} %reshape.1438.masks_ref, ...), custom_call_target="tpu_custom_call" | custom-call | tf_op jit(solution)/shard_map/pallas_call | solution.py:266
  193.6 1.7 subtract_bitcast_fusion
  195.3 0.8 add_bitcast_fusion
  (220 shorter events, 11.6 us)
Async XLA Ops:
  5.6 2.7 %copy-start.15 = (f32[2]{0:T(128)}, f32[2]{0:T(128)S(1)}, u32[]{:S(2)}) copy-start(f32[2]{0:T(128)S(1)} %get-tuple-element.78) | copy-start | bytes 28
  5.6 2.7 %copy-start.17 = (f32[2]{0:T(128)}, f32[2]{0:T(128)S(1)}, u32[]{:S(2)}) copy-start(f32[2]{0:T(128)S(1)} %get-tuple-element.79) | copy-start | bytes 28
  5.6 6.0 %copy-start.19 = (f32[2]{0:T(128)}, f32[2]{0:T(128)S(1)}, u32[]{:S(2)}) copy-start(f32[2]{0:T(128)S(1)} %get-tuple-element.184) | copy-start | bytes 28
  5.6 6.0 %copy-start.20 = (f32[2]{0:T(128)}, f32[2]{0:T(128)S(1)}, u32[]{:S(2)}) copy-start(f32[2]{0:T(128)S(1)} %get-tuple-element.185) | copy-start | bytes 28
  6.8 1.8 copy-start.6
  8.8 1.2 copy-start.10
  9.6 2.0 copy-start
  12.5 6.6 %copy-start.1 = (f32[2,32,1024]{2,1,0:T(8,128)}, f32[2,32,1024]{2,1,0:T(8,128)S(1)}, u32[]{:S(2)}) copy-start(f32[2,32,1024]{2,1,0:T(8,128)S(1)} %get-tuple-element.85.diag_ref) | copy-start | bytes 786436
  14.3 29.7 %copy-start.3 = (f32[2,32,1024]{2,1,0:T(8,128)}, f32[2,32,1024]{2,1,0:T(8,128)S(1)}, u32[]{:S(2)}) copy-start(f32[2,32,1024]{2,1,0:T(8,128)S(1)} %get-tuple-element.91.f_ref) | copy-start | bytes 786436
  17.3 26.7 %copy-start.21 = (s32[8]{0:T(128)S(1)}, s32[8]{0:T(128)}, u32[]{:S(2)}) copy-start(s32[8]{0:T(128)} %param.13) | copy-start | bytes 100
  42.6 3.8 %copy-start.13 = (f32[2,8,1024]{2,1,0:T(8,128)S(1)}, f32[2,8,1024]{2,1,0:T(8,128)}, u32[]{:S(2)}) copy-start(f32[2,8,1024]{2,1,0:T(8,128)} %get-tuple-element.33) | copy-start | bytes 196612
  42.7 6.9 %copy-start.16 = (f32[2]{0:T(128)S(1)}, f32[2]{0:T(128)}, u32[]{:S(2)}) copy-start(f32[2]{0:T(128)} %copy-done.15) | copy-start | bytes 28
  42.7 6.9 %copy-start.18 = (f32[2]{0:T(128)S(1)}, f32[2]{0:T(128)}, u32[]{:S(2)}) copy-start(f32[2]{0:T(128)} %copy-done.17) | copy-start | bytes 28
  42.7 8.1 %copy-start.14 = (f32[16,128]{1,0:T(8,128)S(1)}, f32[16,128]{1,0:T(8,128)}, u32[]{:S(2)}) copy-start(f32[16,128]{1,0:T(8,128)} %get-tuple-element.31) | copy-start | bytes 24580
  44.0 7.3 %copy-start.22 = (pred[32]{0:T(512)(128)(4,1)S(1)}, pred[32]{0:T(512)(128)(4,1)}, u32[]{:S(2)}) copy-start(pred[32]{0:T(512)(128)(4,1)} %constant.263.clone.1) | copy-start | bytes 100
  81.7 22.4 %copy-start.4 = (f32[2,32,1024]{2,1,0:T(8,128)S(1)}, f32[2,32,1024]{2,1,0:T(8,128)}, u32[]{:S(2)}) copy-start(f32[2,32,1024]{2,1,0:T(8,128)} %copy-done.3) | copy-start | bytes 786436
  98.2 5.8 %copy-start.12 = (f32[2,32,1024]{2,1,0:T(8,128)S(1)}, f32[2,32,1024]{2,1,0:T(8,128)}, u32[]{:S(2)}) copy-start(f32[2,32,1024]{2,1,0:T(8,128)} %get-tuple-element.40) | copy-start | bytes 786436
  106.5 21.5 %copy-start.5 = (f32[2,32,1024]{2,1,0:T(8,128)S(1)}, f32[2,32,1024]{2,1,0:T(8,128)}, u32[]{:S(2)}) copy-start(f32[2,32,1024]{2,1,0:T(8,128)} %get-tuple-element.35.f_ref) | copy-start | bytes 786436
  129.7 21.9 %copy-start.7 = (f32[2,32,1024]{2,1,0:T(8,128)S(1)}, f32[2,32,1024]{2,1,0:T(8,128)}, u32[]{:S(2)}) copy-start(f32[2,32,1024]{2,1,0:T(8,128)} %multiply_subtract_fusion.1.f_ref) | copy-start | bytes 786436
  145.8 5.8 %copy-start.11 = (f32[2,32,1024]{2,1,0:T(8,128)S(1)}, f32[2,32,1024]{2,1,0:T(8,128)}, u32[]{:S(2)}) copy-start(f32[2,32,1024]{2,1,0:T(8,128)} %get-tuple-element.49) | copy-start | bytes 786436
  154.1 21.5 %copy-start.2 = (f32[2,32,1024]{2,1,0:T(8,128)S(1)}, f32[2,32,1024]{2,1,0:T(8,128)}, u32[]{:S(2)}) copy-start(f32[2,32,1024]{2,1,0:T(8,128)} %multiply_add_fusion.1.f_ref) | copy-start | bytes 786436
  169.8 5.7 %copy-start.9 = (f32[2,32,1024]{2,1,0:T(8,128)S(1)}, f32[2,32,1024]{2,1,0:T(8,128)}, u32[]{:S(2)}) copy-start(f32[2,32,1024]{2,1,0:T(8,128)} %get-tuple-element.53) | copy-start | bytes 786436
  174.9 18.7 %copy-start.8 = (f32[2,32,1024]{2,1,0:T(8,128)S(1)}, f32[2,32,1024]{2,1,0:T(8,128)}, u32[]{:S(2)}) copy-start(f32[2,32,1024]{2,1,0:T(8,128)} %multiply_subtract_fusion.f_ref) | copy-start | bytes 786436

commit v7 on v5

--- a/solution.py
+++ b/solution.py
@@ -21,7 +21,7 @@
 def share(
     x_ref, xy_ref, z_ref, o_ref, xy_out, z_out, landed_b, landed_g, landed_xy, landed_z,
     send_b, recv_b, send_g, recv_g, send_xy, recv_xy, send_z, recv_z, brick_peers, grp_peers,
-    dot_ref=None,
+    dot_ref=None, with_faces=True,
 ):
     here_brick = lax.axis_index("brick")
     here_grp = lax.axis_index("grp")
@@ -40,14 +40,16 @@
         copy.start()
         return copy
 
-    face_copies = [
-        send(z_ref, landed_z, send_z, recv_z, 0, grp_peers[0]),
-        send(z_ref, landed_z, send_z, recv_z, 1, grp_peers[-1]),
-    ]
-    face_copies += [
-        send(xy_ref, landed_xy, send_xy, recv_xy, k, peer)
-        for k, peer in enumerate(brick_peers, start=1)
-    ]
+    face_copies = []
+    if with_faces:
+        face_copies = [
+            send(z_ref, landed_z, send_z, recv_z, 0, grp_peers[0]),
+            send(z_ref, landed_z, send_z, recv_z, 1, grp_peers[-1]),
+        ]
+        face_copies += [
+            send(xy_ref, landed_xy, send_xy, recv_xy, k, peer)
+            for k, peer in enumerate(brick_peers, start=1)
+        ]
     copies = [
         send(x_ref, landed_b, send_b, recv_b, k, peer)
         for k, peer in enumerate(brick_peers, start=1)
@@ -72,9 +74,13 @@
     o_ref[...] = total
     for copy in face_copies:
         copy.wait()
-    landed_xy[0] = xy_ref[...]
-    xy_out[...] = landed_xy[...]
-    z_out[...] = landed_z[...]
+    if with_faces:
+        landed_xy[0] = xy_ref[...]
+        xy_out[...] = landed_xy[...]
+        z_out[...] = landed_z[...]
+    else:
+        xy_out[...] = jnp.zeros(xy_out.shape, jnp.float32)
+        z_out[...] = jnp.zeros(z_out.shape, jnp.float32)
     if dot_ref is not None:
         tile_rows, tile_lanes = o_ref.shape
         first = lax.broadcasted_iota(jnp.int32, (tile_rows, tile_lanes), 0) * tile_lanes
@@ -137,7 +143,8 @@
 
 
 def stencil_body(
-    coef_ref, f_ref, bonds_ref, masks_ref, diag_ref, rows_ref, faces_ref, o_ref, xy_ref, z_ref, smooth
+    coef_ref, f_ref, bonds_ref, masks_ref, diag_ref, rows_ref, faces_ref, o_ref, xy_ref, z_ref, smooth,
+    with_faces=True,
 ):
     slots, width, lanes = f_ref.shape
     row = lax.broadcasted_iota(jnp.int32, (width, lanes), 0)
@@ -206,6 +213,8 @@
             dot = dot + jnp.sum(fs * total)
             sums.append(jnp.sum(total))
         o_ref[s] = total
+        if not with_faces:
+            continue
         xy_ref[pl.ds(s, 1), :] = total[0:1, :]
         xy_ref[pl.ds(slots + s, 1), :] = total[width - 1 : width, :]
         if s == 0:
@@ -221,7 +230,7 @@
     coef_ref, f_ref, bonds_ref, masks_ref, diag_ref, rows_ref, faces_ref,
     o_ref, total_ref, xy_out, z_out, dot_ref,
     xy_buf, z_buf, tile_buf, landed_b, landed_g, landed_xy, landed_z,
-    send_b, recv_b, send_g, recv_g, send_xy, recv_xy, send_z, recv_z, *, smooth
+    send_b, recv_b, send_g, recv_g, send_xy, recv_xy, send_z, recv_z, *, smooth, with_faces
 ):
     here_brick = lax.axis_index("brick")
     here_grp = lax.axis_index("grp")
@@ -234,7 +243,7 @@
         pl.semaphore_signal(barrier, inc=1, device_id=peer, device_id_type=MESH_IDS)
     dot, sums = stencil_body(
         coef_ref, f_ref, bonds_ref, masks_ref, diag_ref, rows_ref, faces_ref, o_ref, xy_buf, z_buf,
-        smooth,
+        smooth, with_faces,
     )
     tile_rows, tile_lanes = tile_buf.shape
     flat = lax.broadcasted_iota(jnp.int32, (tile_rows, tile_lanes), 0) * tile_lanes
@@ -249,11 +258,11 @@
     share(
         tile_buf, xy_buf, z_buf, total_ref, xy_out, z_out, landed_b, landed_g, landed_xy, landed_z,
         send_b, recv_b, send_g, recv_g, send_xy, recv_xy, send_z, recv_z, brick_peers, grp_peers,
-        dot_ref=dot_ref,
-    )
-
-
-def one_round(field, bonds, masks, diag, rows, faces, coef, smooth):
+        dot_ref=dot_ref, with_faces=with_faces,
+    )
+
+
+def one_round(field, bonds, masks, diag, rows, faces, coef, smooth, with_faces=True):
     slots, _, lanes = field.shape
     n_brick = lax.axis_size("brick")
     n_grp = lax.axis_size("grp")
@@ -264,7 +273,7 @@
     smem = pl.BlockSpec(memory_space=pltpu.SMEM)
     dma = pltpu.SemaphoreType.DMA
     return pl.pallas_call(
-        functools.partial(round_kernel, smooth=smooth),
+        functools.partial(round_kernel, smooth=smooth, with_faces=with_faces),
         out_shape=(
             jax.ShapeDtypeStruct(field.shape, jnp.float32),
             jax.ShapeDtypeStruct(tile, jnp.float32),
@@ -292,7 +301,7 @@
             dma((2,)),
         ],
         compiler_params=pltpu.CompilerParams(
-            collective_id=3 if smooth else 1, has_side_effects=True
+            collective_id=(3 if smooth else 1) if with_faces else 4, has_side_effects=True
         ),
     )(coef, field, bonds, masks, diag, rows, faces)
 
@@ -495,12 +504,12 @@
         )
         return lax.dynamic_slice_in_dim(result[:, 0], slab_index * slot_count, slot_count)
 
-    def round_trip(field, field_halo, coef, smooth):
+    def round_trip(field, field_halo, coef, smooth, with_faces=True):
         out, total, xy_land, z_land, dot = one_round(
-            field, bonds, masks, diagonal, *field_halo, coef, smooth
+            field, bonds, masks, diagonal, *field_halo, coef, smooth, with_faces
         )
         total = total.reshape(-1)
-        out_halo = halo(out, xy_land, z_land, 0.0)
+        out_halo = halo(out, xy_land, z_land, 0.0) if with_faces else None
         if smooth:
             return out, dot[0], None, out_halo
         count = brick_count * grp_count * slot_count
@@ -520,7 +529,7 @@
     search, energy, _, search_halo = precondition(residual, residual_halo, terms)
     for iteration in range(ITERS):
         mapped, curvature, mapped_terms, mapped_halo = round_trip(
-            search, search_halo, no_coarse, False
+            search, search_halo, no_coarse, False, iteration + 1 < ITERS
         )
         step_size = energy / curvature
         solution_field = solution_field + step_size * search

time: 197 us -> 195 us (0.990)
  Pallas kernels: 120 us -> 118 us
where the time goes in v7:
time: 195 us; the launch traced here: 193 us
  Pallas kernels  118 us (61%)
  other arithmetic  31.3 us (16%)
  local copies, waits for them, and re-layouts  26.5 us (14%)
  between operations  13.6 us (7%)
  matrix products  3.5 us (2%)
    pallas_call x6, Pallas kernels, one_round(): pl.pallas_call(functools.partial(round_kernel, smooth=smooth, with_faces=...  95.4 us
    pallas_call x1, Pallas kernels, exchange(): pl.pallas_call(exchange_kernel, out_shape=(jax.ShapeDtypeStruct(tile.shap...  23 us
    pallas_call x5, local copies, waits for them, and re-layouts, one_round(): pl.pallas_call(functools.partial(round_kernel, smooth=smooth, with_faces=...  5.35 us
    select_n x6, other arithmetic, halo(): above = jnp.where(slab_index < grp_count - 1, z_land[1, :slot_count], fill)  4.59 us
    slice x7, local copies, waits for them, and re-layouts, halo(): field[1, :, :BS]  4.22 us

profile of v7, /device:TPU:0, one launch (start us, length us, event | category | flops | bytes accessed | tf_op | source)
XLA Modules:
  0.0 193.3 jit_solution(4246635711186350703)
XLA Ops:
  0.6 1.2 dynamic_slice.117
  4.6 1.4 fusion.101
  8.7 1.1 reduce_sum.122
  9.8 0.8 fusion.74
  11.5 0.7 reshape.1613.masks_ref
  12.4 2.2 %convolution_bitcast_fusion = f32[2,2,32,32]{3,2,0,1:T(8,128)S(1)} fusion(pred[2,32,1024,1]{2,1,0,3:T(32,128)(4,1)S(1)} %bitcast.340, f32[1,1,2,32,1024]{4,3,2,1,0:T(8,128)} %param.10, f32[1,1,6,2,32,1024]{5,4,3,2,1,0:T(8,128)} %param.11, f32[2]{0:T(128)S(1)} %get-tuple-element.175, f32[2]{0:T(128)S(1)} %get-tuple-element.176, f32[2]{0:T(128)S(1)} %get-tuple-element.174, ...), kind=kOutput, calls=%fused_computation | convolution fusion | flops 51511296 | bytes 2048120 | tf_op jit(solution)/shard_map/dot_general | solution.py:393
  14.6 0.5 convolution_bitcast_fusion.1
  15.3 0.6 pad_maximum_fusion.3.z_ref
  15.9 0.3 fusion.116
  16.5 0.4 fusion.18
  17.9 1.3 concatenate.95.xy_ref
  19.5 0.6 pad_bitcast_fusion.x_ref
  20.1 23.0 %shard_map.68 = (f32[16,128]{1,0:T(8,128)}, f32[8,12,1024]{2,1,0:T(8,128)}, f32[2,8,1024]{2,1,0:T(8,128)}) custom-call(f32[16,128]{1,0:T(8,128)} %pad_bitcast_fusion.x_ref, f32[12,1024]{1,0:T(8,128)} %concatenate.95.xy_ref, f32[8,1024]{1,0:T(8,128)} %pad_maximum_fusion.3.z_ref), custom_call_target="tpu_custom_call" | custom-call | tf_op jit(solution)/shard_map/pallas_call | solution.py:118
  43.1 0.9 slice_select_fusion.11
  44.3 1.3 copy.256
  46.1 0.6 copy.258.rows_ref
  46.8 0.7 multiply_divide_fusion.1.faces_ref
  49.1 2.9 %cholesky.19 = f32[32,32]{1,0:T(8,128)S(1)} custom-call(f32[32,32]{1,0:T(8,128)S(1)} %add_multiply_fusion), custom_call_target="Cholesky" | custom-call | tf_op jit(solution)/shard_map/jit(cholesky)/cholesky | solution.py:498
  52.0 0.7 compare_reduce_fusion
  52.7 0.6 fusion.50
  53.3 2.4 %custom-call.14 = f32[1,32,32]{1,2,0:T(8,128)S(1)} custom-call(f32[1,32,32]{2,1,0:T(8,128)S(1)} %fusion.50), custom_call_target="InvertDiagBlocksLowerTriangular" | custom-call | tf_op jit(solution)/shard_map/triangular_solve/custom-call.2 | solution.py:502
  56.1 0.6 fusion.103.coef_ref
  56.6 16.6 %shard_map.69 = (f32[2,32,1024]{2,1,0:T(8,128)}, f32[8,128]{1,0:T(8,128)}, f32[8,6,1024]{2,1,0:T(8,128)}, f32[2,4,1024]{2,1,0:T(4,128)}, f32[1]{0:T(128)}) custom-call(f32[2]{0:T(128)} %fusion.103.coef_ref, f32[2,32,1024]{2,1,0:T(8,128)} %copy-done.3, f32[6,2,32,1024]{3,2,1,0:T(8,128)} %bitcast.334, f32[24]{0:T(128)} %reshape.1613.masks_ref, ...), custom_call_target="tpu_custom_call" | custom-call | tf_op jit(solution)/shard_map/pallas_call | solution.py:275
  73.3 1.1 copy.259
  74.6 0.6 copy.263.rows_ref
  75.2 0.7 slice_select_fusion.9
  76.1 0.8 fusion.122
  77.0 0.7 pad_maximum_fusion.2.faces_ref
  77.6 0.5 broadcast_18_coef_ref.2.coef_ref
  78.2 16.5 %shard_map.70 = (f32[2,32,1024]{2,1,0:T(8,128)}, f32[8,128]{1,0:T(8,128)}, f32[8,6,1024]{2,1,0:T(8,128)}, f32[2,4,1024]{2,1,0:T(4,128)}, f32[1]{0:T(128)}) custom-call(f32[2]{0:T(128)} %broadcast_18_coef_ref.2.coef_ref, f32[2,32,1024]{2,1,0:T(8,128)} %get-tuple-element.35.f_ref, f32[6,2,32,1024]{3,2,1,0:T(8,128)} %bitcast.335, f32[24]{0:T(128)} %reshape.1613.masks_ref, ...), custom_call_target="tpu_custom_call" | custom-call | tf_op jit(solution)/shard_map/pallas_call | solution.py:275
  96.1 1.7 multiply_subtract_fusion.1.f_ref
  97.8 0.7 slice.403
  98.9 0.6 fusion.107.coef_ref
  99.5 0.7 slice_select_fusion.7
  100.4 0.8 fusion.121
  101.2 1.1 copy.264
  102.6 0.6 copy.268.rows_ref
  103.2 0.7 multiply_divide_fusion.faces_ref
  103.9 15.8 %shard_map.71 = (f32[2,32,1024]{2,1,0:T(8,128)}, f32[8,128]{1,0:T(8,128)}, f32[8,6,1024]{2,1,0:T(8,128)}, f32[2,4,1024]{2,1,0:T(4,128)}, f32[1]{0:T(128)}) custom-call(f32[2]{0:T(128)} %fusion.107.coef_ref, f32[2,32,1024]{2,1,0:T(8,128)} %multiply_subtract_fusion.1.f_ref, f32[6,2,32,1024]{3,2,1,0:T(8,128)} %bitcast.336, f32[24]{0:T(128)} %reshape.1613.masks_ref, ...), custom_call_target="tpu_custom_call" | custom-call | tf_op jit(solution)/shard_map/pallas_call | solution.py:275
  121.1 1.1 copy.269
  122.4 0.6 fusion.52.rows_ref
  123.0 0.7 slice_select_fusion.5
  123.9 0.8 fusion.120
  124.7 1.7 multiply_add_fusion.1.f_ref
  126.4 0.7 maximum_add_fusion.faces_ref
  127.1 16.1 %shard_map.72 = (f32[2,32,1024]{2,1,0:T(8,128)}, f32[8,128]{1,0:T(8,128)}, f32[8,6,1024]{2,1,0:T(8,128)}, f32[2,4,1024]{2,1,0:T(4,128)}, f32[1]{0:T(128)}) custom-call(f32[2]{0:T(128)} %broadcast_18_coef_ref.2.coef_ref, f32[2,32,1024]{2,1,0:T(8,128)} %multiply_add_fusion.1.f_ref, f32[6,2,32,1024]{3,2,1,0:T(8,128)} %bitcast.337, f32[24]{0:T(128)} %reshape.1613.masks_ref, ...), custom_call_target="tpu_custom_call" | custom-call | tf_op jit(solution)/shard_map/pallas_call | solution.py:275
  144.6 1.7 multiply_subtract_fusion.f_ref
  146.3 0.7 slice.420
  147.4 0.7 fusion.112.coef_ref
  148.1 0.7 slice_select_fusion.3
  149.0 0.8 fusion.119
  149.8 1.1 copy.276
  151.0 0.6 copy.280.rows_ref
  151.8 0.7 fusion.35.faces_ref
  152.5 15.7 %shard_map.73 = (f32[2,32,1024]{2,1,0:T(8,128)}, f32[8,128]{1,0:T(8,128)}, f32[8,6,1024]{2,1,0:T(8,128)}, f32[2,4,1024]{2,1,0:T(4,128)}, f32[1]{0:T(128)}) custom-call(f32[2]{0:T(128)} %fusion.112.coef_ref, f32[2,32,1024]{2,1,0:T(8,128)} %multiply_subtract_fusion.f_ref, f32[6,2,32,1024]{3,2,1,0:T(8,128)} %bitcast.338, f32[24]{0:T(128)} %reshape.1613.masks_ref, ...), custom_call_target="tpu_custom_call" | custom-call | tf_op jit(solution)/shard_map/pallas_call | solution.py:275
  169.6 1.1 copy.281
  170.8 0.6 copy_add_fusion.rows_ref
  171.5 0.7 slice_select_fusion.1
  172.5 0.8 fusion.118
  173.3 0.7 maximum_add_fusion.1.faces_ref
  174.0 0.7 multiply_add_fusion.f_ref
  174.8 14.7 %shard_map.74 = (f32[2,32,1024]{2,1,0:T(8,128)}, f32[8,128]{1,0:T(8,128)}, f32[8,6,1024]{2,1,0:T(8,128)}, f32[2,4,1024]{2,1,0:T(4,128)}, f32[1]{0:T(128)}) custom-call(f32[2]{0:T(128)} %broadcast_18_coef_ref.2.coef_ref, f32[2,32,1024]{2,1,0:T(8,128)} %multiply_add_fusion.f_ref, f32[6,2,32,1024]{3,2,1,0:T(8,128)} %bitcast.339, f32[24]{0:T(128)} %reshape.1613.masks_ref, ...), custom_call_target="tpu_custom_call" | custom-call | tf_op jit(solution)/shard_map/pallas_call | solution.py:275
  190.9 0.8 add_bitcast_fusion
  191.6 1.7 subtract_bitcast_fusion
  (173 shorter events, 8.4 us)
Async XLA Ops:
  6.6 8.1 %copy-start.9 = (f32[1,1,2,32,1024]{4,3,2,1,0:T(8,128)S(1)}, f32[1,1,2,32,1024]{4,3,2,1,0:T(8,128)}, u32[]{:S(2)}) copy-start(f32[1,1,2,32,1024]{4,3,2,1,0:T(8,128)} %param.9) | copy-start | bytes 786436
  12.4 3.5 %copy-start = (f32[1,1,6,2,32,1024]{5,4,3,2,1,0:T(8,128)S(1)}, f32[1,1,6,2,32,1024]{5,4,3,2,1,0:T(8,128)}, u32[]{:S(2)}) copy-start(f32[1,1,6,2,32,1024]{5,4,3,2,1,0:T(8,128)} %param.11) | copy-start | bytes 4718596
  14.6 1.9 copy-start.10
  16.2 0.7 copy-start.3
  17.0 28.7 %copy-start.1 = (f32[2,32,1024]{2,1,0:T(8,128)}, f32[2,32,1024]{2,1,0:T(8,128)S(1)}, u32[]{:S(2)}) copy-start(f32[2,32,1024]{2,1,0:T(8,128)S(1)} %get-tuple-element.85.diag_ref) | copy-start | bytes 786436
  43.1 4.4 %copy-start.11 = (f32[16,128]{1,0:T(8,128)S(1)}, f32[16,128]{1,0:T(8,128)}, u32[]{:S(2)}) copy-start(f32[16,128]{1,0:T(8,128)} %get-tuple-element.31) | copy-start | bytes 24580
  44.3 4.5 %copy-start.12 = (pred[32]{0:T(512)(128)(4,1)S(1)}, pred[32]{0:T(512)(128)(4,1)}, u32[]{:S(2)}) copy-start(pred[32]{0:T(512)(128)(4,1)} %constant.263.clone.1) | copy-start | bytes 100
  74.4 21.7 %copy-start.4 = (f32[2,32,1024]{2,1,0:T(8,128)S(1)}, f32[2,32,1024]{2,1,0:T(8,128)}, u32[]{:S(2)}) copy-start(f32[2,32,1024]{2,1,0:T(8,128)} %copy-done.3) | copy-start | bytes 786436
  103.9 20.9 %copy-start.5 = (f32[2,32,1024]{2,1,0:T(8,128)S(1)}, f32[2,32,1024]{2,1,0:T(8,128)}, u32[]{:S(2)}) copy-start(f32[2,32,1024]{2,1,0:T(8,128)} %get-tuple-element.35.f_ref) | copy-start | bytes 786436
  126.4 18.2 %copy-start.7 = (f32[2,32,1024]{2,1,0:T(8,128)S(1)}, f32[2,32,1024]{2,1,0:T(8,128)}, u32[]{:S(2)}) copy-start(f32[2,32,1024]{2,1,0:T(8,128)} %multiply_subtract_fusion.1.f_ref) | copy-start | bytes 786436
  152.5 21.5 %copy-start.2 = (f32[2,32,1024]{2,1,0:T(8,128)S(1)}, f32[2,32,1024]{2,1,0:T(8,128)}, u32[]{:S(2)}) copy-start(f32[2,32,1024]{2,1,0:T(8,128)} %multiply_add_fusion.1.f_ref) | copy-start | bytes 786436
  168.2 5.8 %copy-start.8 = (f32[2,32,1024]{2,1,0:T(8,128)S(1)}, f32[2,32,1024]{2,1,0:T(8,128)}, u32[]{:S(2)}) copy-start(f32[2,32,1024]{2,1,0:T(8,128)} %get-tuple-element.53) | copy-start | bytes 786436
  174.8 16.9 %copy-start.6 = (f32[2,32,1024]{2,1,0:T(8,128)S(1)}, f32[2,32,1024]{2,1,0:T(8,128)}, u32[]{:S(2)}) copy-start(f32[2,32,1024]{2,1,0:T(8,128)} %multiply_subtract_fusion.f_ref) | copy-start | bytes 786436

commit v8 on v7

--- a/solution.py
+++ b/solution.py
@@ -76,7 +76,8 @@
         copy.wait()
     if with_faces:
         landed_xy[0] = xy_ref[...]
-        xy_out[...] = landed_xy[...]
+        for k in range(landed_xy.shape[0]):
+            xy_out[:, k, :] = landed_xy[k]
         z_out[...] = landed_z[...]
     else:
         xy_out[...] = jnp.zeros(xy_out.shape, jnp.float32)
@@ -119,7 +120,7 @@
         exchange_kernel,
         out_shape=(
             jax.ShapeDtypeStruct(tile.shape, jnp.float32),
-            jax.ShapeDtypeStruct((n_brick,) + xy.shape, jnp.float32),
+            jax.ShapeDtypeStruct((xy.shape[0], n_brick, xy.shape[1]), jnp.float32),
             jax.ShapeDtypeStruct((2,) + z.shape, jnp.float32),
         ),
         in_specs=[vmem] * 3,
@@ -277,7 +278,7 @@
         out_shape=(
             jax.ShapeDtypeStruct(field.shape, jnp.float32),
             jax.ShapeDtypeStruct(tile, jnp.float32),
-            jax.ShapeDtypeStruct((n_brick,) + xy, jnp.float32),
+            jax.ShapeDtypeStruct((xy[0], n_brick, xy[1]), jnp.float32),
             jax.ShapeDtypeStruct((2,) + z, jnp.float32),
             jax.ShapeDtypeStruct((1,), jnp.float32),
         ),
@@ -406,7 +407,7 @@
 
     def pick(landed, holder, fill):
         offset = lax.rem(brick_index - holder + brick_count, brick_count)
-        got = lax.dynamic_index_in_dim(landed, offset, keepdims=False)
+        got = lax.dynamic_index_in_dim(landed, offset, axis=1, keepdims=False)
         return jnp.where(holder >= 0, got, fill)
 
     def halo(field, xy_land, z_land, fill):
@@ -488,8 +489,8 @@
     summed = summed.reshape(-1)[: spread.shape[0]]
     xy_rows = forcing_xy.shape[0]
     z_rows = forcing_z.shape[0]
-    residual_halo = halo(forcing, xy_land[:, :xy_rows], z_land[:, :z_rows], 0.0)
-    diagonal_halo = halo(diagonal, xy_land[:, xy_rows:], z_land[:, z_rows:], 1.0)
+    residual_halo = halo(forcing, xy_land[:xy_rows], z_land[:, :z_rows], 0.0)
+    diagonal_halo = halo(diagonal, xy_land[xy_rows:], z_land[:, z_rows:], 1.0)
     gathered = lax.dynamic_index_in_dim(
         summed.reshape(brick_count, grp_count, 5, slot_count), brick_index, keepdims=False
     )

time: 195 us -> 198 us (1.015)
  other arithmetic: 31.3 us -> 42.3 us
  local copies, waits for them, and re-layouts: 26.5 us -> 19.2 us
    pallas_call x6 -> x0, local copies, waits for them, and re-layouts: 6.64 us -> none  [the longest x5 5.35 us: one_round(): pl.pallas_call(functools.partial(round_kernel, smooth=smooth, with_faces=...]
    another operation x8 -> x7, other arithmetic: 0.19 us -> 4.55 us  [halo(): jnp.stack([xplus[:slot_count], xminus[slot_count:2 * slot_count]])]
    select_n x8 -> x7, other arithmetic: 0.29 us -> 4.13 us  [pick(): return jnp.where(holder >= 0, got, fill)]
where the time goes in v8:
time: 198 us; the launch traced here: 196 us
  Pallas kernels  118 us (60%)
  other arithmetic  42.3 us (21%)
  local copies, waits for them, and re-layouts  19.2 us (10%)
  between operations  12.9 us (7%)
  matrix products  3.5 us (2%)
    pallas_call x6, Pallas kernels, one_round(): pl.pallas_call(functools.partial(round_kernel, smooth=smooth, with_faces=...  95.4 us
    pallas_call x1, Pallas kernels, exchange(): pl.pallas_call(exchange_kernel, out_shape=(jax.ShapeDtypeStruct(tile.shap...  23 us
    select_n x6, other arithmetic, halo(): above = jnp.where(slab_index < grp_count - 1, z_land[1, :slot_count], fill)  4.64 us
    another operation x7, other arithmetic, halo(): jnp.stack([xplus[:slot_count], xminus[slot_count:2 * slot_count]])  4.55 us
    slice x7, local copies, waits for them, and re-layouts, halo(): field[1, :, :BS]  4.22 us
    select_n x7, other arithmetic, pick(): return jnp.where(holder >= 0, got, fill)  4.13 us
    div x6, other arithmetic, precondition(): OMEGA * part / scale  4.01 us

profile of v8, /device:TPU:0, one launch (start us, length us, event | category | flops | bytes accessed | tf_op | source)
XLA Modules:
  0.0 196.3 jit_solution(17706610250752245609)
XLA Ops:
  0.6 1.2 dynamic_slice.117
  4.6 1.4 fusion.98
  8.7 1.1 reduce_sum.122
  9.8 0.8 fusion.71
  11.5 0.7 reshape.1613.masks_ref
  12.4 2.2 %convolution_bitcast_fusion = f32[2,2,32,32]{3,2,0,1:T(8,128)S(1)} fusion(pred[2,32,1024,1]{2,1,0,3:T(32,128)(4,1)S(1)} %bitcast.344, f32[1,1,2,32,1024]{4,3,2,1,0:T(8,128)} %param.10, f32[1,1,6,2,32,1024]{5,4,3,2,1,0:T(8,128)} %param.11, f32[2]{0:T(128)S(1)} %get-tuple-element.179, f32[2]{0:T(128)S(1)} %get-tuple-element.180, f32[2]{0:T(128)S(1)} %get-tuple-element.178, ...), kind=kOutput, calls=%fused_computation | convolution fusion | flops 51511296 | bytes 2048120 | tf_op jit(solution)/shard_map/dot_general | solution.py:394
  15.3 0.6 pad_maximum_fusion.3.z_ref
  17.9 1.3 concatenate.95.xy_ref
  19.5 0.6 pad_bitcast_fusion.x_ref
  20.1 23.0 %shard_map.68 = (f32[16,128]{1,0:T(8,128)}, f32[12,8,1024]{2,1,0:T(8,128)}, f32[2,8,1024]{2,1,0:T(8,128)}) custom-call(f32[16,128]{1,0:T(8,128)} %pad_bitcast_fusion.x_ref, f32[12,1024]{1,0:T(8,128)} %concatenate.95.xy_ref, f32[8,1024]{1,0:T(8,128)} %pad_maximum_fusion.3.z_ref), custom_call_target="tpu_custom_call" | custom-call | tf_op jit(solution)/shard_map/pallas_call | solution.py:119
  43.1 0.9 slice_select_fusion.11
  44.3 1.1 fusion.119
  45.8 0.6 multiply_divide_fusion.4.rows_ref
  46.5 0.7 multiply_divide_fusion.1.faces_ref
  48.8 2.9 %cholesky.19 = f32[32,32]{1,0:T(8,128)S(1)} custom-call(f32[32,32]{1,0:T(8,128)S(1)} %add_multiply_fusion), custom_call_target="Cholesky" | custom-call | tf_op jit(solution)/shard_map/jit(cholesky)/cholesky | solution.py:499
  51.7 0.6 compare_reduce_fusion
  53.0 2.4 %custom-call.14 = f32[1,32,32]{1,2,0:T(8,128)S(1)} custom-call(f32[1,32,32]{2,1,0:T(8,128)S(1)} %fusion.50), custom_call_target="InvertDiagBlocksLowerTriangular" | custom-call | tf_op jit(solution)/shard_map/triangular_solve/custom-call.2 | solution.py:503
  55.7 0.7 fusion.100.coef_ref
  56.4 16.6 %shard_map.69 = (f32[2,32,1024]{2,1,0:T(8,128)}, f32[8,128]{1,0:T(8,128)}, f32[6,8,1024]{2,1,0:T(8,128)}, f32[2,4,1024]{2,1,0:T(4,128)}, f32[1]{0:T(128)}) custom-call(f32[2]{0:T(128)} %fusion.100.coef_ref, f32[2,32,1024]{2,1,0:T(8,128)} %copy-done.3, f32[6,2,32,1024]{3,2,1,0:T(8,128)} %bitcast.338, f32[24]{0:T(128)} %reshape.1613.masks_ref, ...), custom_call_target="tpu_custom_call" | custom-call | tf_op jit(solution)/shard_map/pallas_call | solution.py:276
  73.0 0.8 slice_select_fusion.9
  73.8 0.8 fusion.79
  74.6 0.9 fusion.112
  75.6 0.6 copy.98.rows_ref
  76.5 0.8 fusion.124
  77.3 0.7 pad_maximum_fusion.2.faces_ref
  78.5 16.5 %shard_map.70 = (f32[2,32,1024]{2,1,0:T(8,128)}, f32[8,128]{1,0:T(8,128)}, f32[6,8,1024]{2,1,0:T(8,128)}, f32[2,4,1024]{2,1,0:T(4,128)}, f32[1]{0:T(128)}) custom-call(f32[2]{0:T(128)} %broadcast_18_coef_ref.2.coef_ref, f32[2,32,1024]{2,1,0:T(8,128)} %get-tuple-element.35.f_ref, f32[6,2,32,1024]{3,2,1,0:T(8,128)} %bitcast.339, f32[24]{0:T(128)} %reshape.1613.masks_ref, ...), custom_call_target="tpu_custom_call" | custom-call | tf_op jit(solution)/shard_map/pallas_call | solution.py:276
  96.3 1.7 multiply_subtract_fusion.1.f_ref
  98.0 0.7 slice.403
  99.1 0.7 fusion.104.coef_ref
  99.8 0.8 fusion.80
  100.6 0.9 fusion.61
  101.5 0.7 multiply_divide_fusion.3
  102.3 0.7 slice_select_fusion.7
  103.2 0.8 fusion.123
  104.0 0.7 multiply_divide_fusion.faces_ref
  104.7 15.7 %shard_map.71 = (f32[2,32,1024]{2,1,0:T(8,128)}, f32[8,128]{1,0:T(8,128)}, f32[6,8,1024]{2,1,0:T(8,128)}, f32[2,4,1024]{2,1,0:T(4,128)}, f32[1]{0:T(128)}) custom-call(f32[2]{0:T(128)} %fusion.104.coef_ref, f32[2,32,1024]{2,1,0:T(8,128)} %multiply_subtract_fusion.1.f_ref, f32[6,2,32,1024]{3,2,1,0:T(8,128)} %bitcast.340, f32[24]{0:T(128)} %reshape.1613.masks_ref, ...), custom_call_target="tpu_custom_call" | custom-call | tf_op jit(solution)/shard_map/pallas_call | solution.py:276
  121.7 0.7 slice_select_fusion.5
  122.5 0.8 fusion.81
  123.3 0.9 fusion.62
  124.4 0.6 maximum_add_fusion.2.rows_ref
  125.2 0.8 fusion.122
  126.0 1.7 multiply_add_fusion.1.f_ref
  127.7 0.7 maximum_add_fusion.faces_ref
  128.3 16.3 %shard_map.72 = (f32[2,32,1024]{2,1,0:T(8,128)}, f32[8,128]{1,0:T(8,128)}, f32[6,8,1024]{2,1,0:T(8,128)}, f32[2,4,1024]{2,1,0:T(4,128)}, f32[1]{0:T(128)}) custom-call(f32[2]{0:T(128)} %broadcast_18_coef_ref.2.coef_ref, f32[2,32,1024]{2,1,0:T(8,128)} %multiply_add_fusion.1.f_ref, f32[6,2,32,1024]{3,2,1,0:T(8,128)} %bitcast.341, f32[24]{0:T(128)} %reshape.1613.masks_ref, ...), custom_call_target="tpu_custom_call" | custom-call | tf_op jit(solution)/shard_map/pallas_call | solution.py:276
  146.0 1.7 multiply_subtract_fusion.f_ref
  147.6 0.7 slice.420
  148.7 0.7 fusion.109.coef_ref
  149.4 0.8 fusion.82
  150.2 0.9 fusion.63
  151.1 0.6 multiply_divide_fusion.2.rows_ref
  151.9 0.7 slice_select_fusion.3
  152.8 0.8 fusion.121
  153.7 0.7 fusion.35.faces_ref
  154.4 15.7 %shard_map.73 = (f32[2,32,1024]{2,1,0:T(8,128)}, f32[8,128]{1,0:T(8,128)}, f32[6,8,1024]{2,1,0:T(8,128)}, f32[2,4,1024]{2,1,0:T(4,128)}, f32[1]{0:T(128)}) custom-call(f32[2]{0:T(128)} %fusion.109.coef_ref, f32[2,32,1024]{2,1,0:T(8,128)} %multiply_subtract_fusion.f_ref, f32[6,2,32,1024]{3,2,1,0:T(8,128)} %bitcast.342, f32[24]{0:T(128)} %reshape.1613.masks_ref, ...), custom_call_target="tpu_custom_call" | custom-call | tf_op jit(solution)/shard_map/pallas_call | solution.py:276
  171.2 0.7 slice_select_fusion.1
  172.0 0.8 fusion.83
  172.8 0.9 fusion.64
  173.7 0.6 maximum_add_fusion.3.rows_ref
  174.7 0.8 fusion.120
  175.5 0.7 maximum_add_fusion.1.faces_ref
  176.2 1.8 multiply_add_fusion.f_ref
  178.0 14.7 %shard_map.74 = (f32[2,32,1024]{2,1,0:T(8,128)}, f32[8,128]{1,0:T(8,128)}, f32[6,8,1024]{2,1,0:T(8,128)}, f32[2,4,1024]{2,1,0:T(4,128)}, f32[1]{0:T(128)}) custom-call(f32[2]{0:T(128)} %broadcast_18_coef_ref.2.coef_ref, f32[2,32,1024]{2,1,0:T(8,128)} %multiply_add_fusion.f_ref, f32[6,2,32,1024]{3,2,1,0:T(8,128)} %bitcast.343, f32[24]{0:T(128)} %reshape.1613.masks_ref, ...), custom_call_target="tpu_custom_call" | custom-call | tf_op jit(solution)/shard_map/pallas_call | solution.py:276
  193.8 0.8 add_bitcast_fusion
  194.6 1.7 subtract_bitcast_fusion
  (162 shorter events, 10.1 us)
Async XLA Ops:
  6.6 8.0 %copy-start.9 = (f32[1,1,2,32,1024]{4,3,2,1,0:T(8,128)S(1)}, f32[1,1,2,32,1024]{4,3,2,1,0:T(8,128)}, u32[]{:S(2)}) copy-start(f32[1,1,2,32,1024]{4,3,2,1,0:T(8,128)} %param.9) | copy-start | bytes 786436
  12.4 3.5 %copy-start = (f32[1,1,6,2,32,1024]{5,4,3,2,1,0:T(8,128)S(1)}, f32[1,1,6,2,32,1024]{5,4,3,2,1,0:T(8,128)}, u32[]{:S(2)}) copy-start(f32[1,1,6,2,32,1024]{5,4,3,2,1,0:T(8,128)} %param.11) | copy-start | bytes 4718596
  14.6 1.9 copy-start.10
  16.2 0.7 copy-start.3
  17.0 28.8 %copy-start.1 = (f32[2,32,1024]{2,1,0:T(8,128)}, f32[2,32,1024]{2,1,0:T(8,128)S(1)}, u32[]{:S(2)}) copy-start(f32[2,32,1024]{2,1,0:T(8,128)S(1)} %get-tuple-element.87.diag_ref) | copy-start | bytes 786436
  19.5 29.0 %copy-start.12 = (pred[32]{0:T(512)(128)(4,1)S(1)}, pred[32]{0:T(512)(128)(4,1)}, u32[]{:S(2)}) copy-start(pred[32]{0:T(512)(128)(4,1)} %constant.263.clone.1) | copy-start | bytes 100
  43.1 4.1 %copy-start.11 = (f32[16,128]{1,0:T(8,128)S(1)}, f32[16,128]{1,0:T(8,128)}, u32[]{:S(2)}) copy-start(f32[16,128]{1,0:T(8,128)} %get-tuple-element.31) | copy-start | bytes 24580
  73.0 23.3 %copy-start.4 = (f32[2,32,1024]{2,1,0:T(8,128)S(1)}, f32[2,32,1024]{2,1,0:T(8,128)}, u32[]{:S(2)}) copy-start(f32[2,32,1024]{2,1,0:T(8,128)} %copy-done.3) | copy-start | bytes 786436
  104.0 21.9 %copy-start.5 = (f32[2,32,1024]{2,1,0:T(8,128)S(1)}, f32[2,32,1024]{2,1,0:T(8,128)}, u32[]{:S(2)}) copy-start(f32[2,32,1024]{2,1,0:T(8,128)} %get-tuple-element.35.f_ref) | copy-start | bytes 786436
  127.6 18.3 %copy-start.7 = (f32[2,32,1024]{2,1,0:T(8,128)S(1)}, f32[2,32,1024]{2,1,0:T(8,128)}, u32[]{:S(2)}) copy-start(f32[2,32,1024]{2,1,0:T(8,128)} %multiply_subtract_fusion.1.f_ref) | copy-start | bytes 786436
  154.4 21.8 %copy-start.2 = (f32[2,32,1024]{2,1,0:T(8,128)S(1)}, f32[2,32,1024]{2,1,0:T(8,128)}, u32[]{:S(2)}) copy-start(f32[2,32,1024]{2,1,0:T(8,128)} %multiply_add_fusion.1.f_ref) | copy-start | bytes 786436
  176.2 17.6 %copy-start.8 = (f32[2,32,1024]{2,1,0:T(8,128)S(1)}, f32[2,32,1024]{2,1,0:T(8,128)}, u32[]{:S(2)}) copy-start(f32[2,32,1024]{2,1,0:T(8,128)} %get-tuple-element.53) | copy-start | bytes 786436
  178.0 16.6 %copy-start.6 = (f32[2,32,1024]{2,1,0:T(8,128)S(1)}, f32[2,32,1024]{2,1,0:T(8,128)}, u32[]{:S(2)}) copy-start(f32[2,32,1024]{2,1,0:T(8,128)} %multiply_subtract_fusion.f_ref) | copy-start | bytes 786436

commit v9 on v7

--- a/solution.py
+++ b/solution.py
@@ -88,9 +88,48 @@
         dot_ref[0] = jnp.sum(jnp.where(first == 0, total, 0.0))
 
 
+def setup_faces(f_ref, xy_ref, z_ref, xy_base, z_base):
+    slots, width, lanes = f_ref.shape
+    pick = lax.broadcasted_iota(jnp.int32, (BS, lanes), 0)
+    spot = lax.broadcasted_iota(jnp.int32, (BS, lanes), 1)
+    spread_y = (spot % BS == pick).astype(jnp.float32)
+    flat_mask = spot // BS == pick
+    source_lane = lax.broadcasted_iota(jnp.int32, (lanes, BS), 0)
+    place = lax.broadcasted_iota(jnp.int32, (lanes, BS), 1)
+    layers = [
+        (source_lane == offset + step * place).astype(jnp.float32)
+        for offset, step in ((0, 1), (lanes - BS, 1), (0, BS), (BS - 1, BS))
+    ]
+
+    def spread(face, table):
+        high = face.astype(jnp.bfloat16)
+        rest = face - high.astype(jnp.float32)
+        middle = rest.astype(jnp.bfloat16)
+        low = (rest - middle.astype(jnp.float32)).astype(jnp.bfloat16)
+        table = table.astype(jnp.bfloat16)
+        parts = [
+            jnp.dot(part, table, preferred_element_type=jnp.float32) for part in (high, middle, low)
+        ]
+        return (parts[0] + parts[1]) + parts[2]
+
+    def flatten(layer):
+        return jnp.sum(jnp.where(flat_mask, spread(layer, spread_y), 0.0), axis=0, keepdims=True)
+
+    for s in range(slots):
+        total = f_ref[s]
+        xy_ref[pl.ds(xy_base + s, 1), :] = total[0:1, :]
+        xy_ref[pl.ds(xy_base + slots + s, 1), :] = total[width - 1 : width, :]
+        if s == 0:
+            xy_ref[pl.ds(xy_base + 2 * slots, 1), :] = flatten(spread(total, layers[0]))
+        if s == slots - 1:
+            xy_ref[pl.ds(xy_base + 2 * slots + 1, 1), :] = flatten(spread(total, layers[1]))
+        z_ref[pl.ds(z_base + s, 1), :] = flatten(spread(total, layers[2]))
+        z_ref[pl.ds(z_base + slots + s, 1), :] = flatten(spread(total, layers[3]))
+
+
 def exchange_kernel(
-    x_ref, xy_ref, z_ref, o_ref, xy_out, z_out,
-    landed_b, landed_g, landed_xy, landed_z,
+    x_ref, forcing_ref, diag_ref, o_ref, xy_out, z_out,
+    xy_ref, z_ref, landed_b, landed_g, landed_xy, landed_z,
     send_b, recv_b, send_g, recv_g, send_xy, recv_xy, send_z, recv_z,
 ):
     here_brick = lax.axis_index("brick")
@@ -102,6 +141,9 @@
     barrier = pltpu.get_barrier_semaphore()
     for peer in brick_peers + grp_peers:
         pl.semaphore_signal(barrier, inc=1, device_id=peer, device_id_type=MESH_IDS)
+    slots = forcing_ref.shape[0]
+    setup_faces(forcing_ref, xy_ref, z_ref, 0, 0)
+    setup_faces(diag_ref, xy_ref, z_ref, 2 * slots + 2, 2 * slots)
     pl.semaphore_wait(barrier, len(brick_peers) + len(grp_peers))
 
     share(
@@ -110,7 +152,10 @@
     )
 
 
-def exchange(tile, xy, z, kernel_id):
+def exchange(tile, forcing, diag, kernel_id):
+    slots, _, lanes = forcing.shape
+    xy = jax.ShapeDtypeStruct((2 * (2 * slots + 2), lanes), jnp.float32)
+    z = jax.ShapeDtypeStruct((2 * (2 * slots), lanes), jnp.float32)
     n_brick = lax.axis_size("brick")
     n_grp = lax.axis_size("grp")
     vmem = pl.BlockSpec(memory_space=pltpu.VMEM)
@@ -125,6 +170,8 @@
         in_specs=[vmem] * 3,
         out_specs=(vmem, vmem, vmem),
         scratch_shapes=[
+            pltpu.VMEM(xy.shape, jnp.float32),
+            pltpu.VMEM(z.shape, jnp.float32),
             pltpu.VMEM((n_brick,) + tile.shape, jnp.float32),
             pltpu.VMEM((n_grp,) + tile.shape, jnp.float32),
             pltpu.VMEM((n_brick,) + xy.shape, jnp.float32),
@@ -139,7 +186,7 @@
             dma((2,)),
         ],
         compiler_params=pltpu.CompilerParams(collective_id=kernel_id, has_side_effects=True),
-    )(tile, xy, z)
+    )(tile, forcing, diag)
 
 
 def stencil_body(
@@ -477,17 +524,10 @@
     )
     brick_here = (peer_ids == brick_index).astype(jnp.float32)
     spread = (brick_here[:, None, None, None] * slab_slot(record)[None]).reshape(-1)
-    forcing_xy, forcing_z = side_faces(forcing)
-    diagonal_xy, diagonal_z = side_faces(diagonal)
-    summed, xy_land, z_land = exchange(
-        as_tile(spread),
-        jnp.concatenate([forcing_xy, diagonal_xy]),
-        jnp.concatenate([forcing_z, diagonal_z]),
-        2,
-    )
+    summed, xy_land, z_land = exchange(as_tile(spread), forcing, diagonal, 2)
     summed = summed.reshape(-1)[: spread.shape[0]]
-    xy_rows = forcing_xy.shape[0]
-    z_rows = forcing_z.shape[0]
+    xy_rows = 2 * slot_count + 2
+    z_rows = 2 * slot_count
     residual_halo = halo(forcing, xy_land[:, :xy_rows], z_land[:, :z_rows], 0.0)
     diagonal_halo = halo(diagonal, xy_land[:, xy_rows:], z_land[:, z_rows:], 1.0)
     gathered = lax.dynamic_index_in_dim(

time: 195 us -> 192 us (0.985)
  matrix products: 3.5 us -> 0.85 us
    dot_general x2 -> x0, matrix products: 2.66 us -> none  [side_faces(): jnp.dot(field.reshape(slot_count * BS, face_size), picker, precision=lax....]
    pallas_call x1, Pallas kernels: 23 us -> 25.2 us  [exchange(): pl.pallas_call(exchange_kernel, out_shape=(jax.ShapeDtypeStruct(tile.shap...]
where the time goes in v9:
time: 192 us; the launch traced here: 190 us
  Pallas kernels  119 us (62%)
  other arithmetic  31.7 us (17%)
  local copies, waits for them, and re-layouts  24.9 us (13%)
  between operations  13.4 us (7%)
    pallas_call x6, Pallas kernels, one_round(): pl.pallas_call(functools.partial(round_kernel, smooth=smooth, with_faces=...  94.1 us
    pallas_call x1, Pallas kernels, exchange(): pl.pallas_call(exchange_kernel, out_shape=(jax.ShapeDtypeStruct(tile.shap...  25.2 us
    pallas_call x5, local copies, waits for them, and re-layouts, one_round(): pl.pallas_call(functools.partial(round_kernel, smooth=smooth, with_faces=...  5.35 us
    select_n x6, other arithmetic, halo(): above = jnp.where(slab_index < grp_count - 1, z_land[1, :slot_count], fill)  4.59 us
    slice x7, local copies, waits for them, and re-layouts, halo(): field[1, :, :BS]  4.21 us

profile of v9, /device:TPU:0, one launch (start us, length us, event | category | flops | bytes accessed | tf_op | source)
XLA Modules:
  0.0 190.2 jit_solution(7230116318680745112)
XLA Ops:
  0.7 1.4 dynamic_slice.117
  4.7 1.4 fusion.60
  8.8 1.1 reduce_sum.122
  9.9 0.8 fusion.33
  10.7 0.3 slice_reduce_fusion.7
  11.6 0.7 reshape.1382.masks_ref
  12.4 1.4 fusion.75
  13.9 0.5 fusion.4
  14.5 0.2 slice_reduce_fusion.1
  15.3 0.2 mul.430
  15.5 0.6 pad_bitcast_fusion.x_ref
  16.1 25.2 %shard_map.68 = (f32[16,128]{1,0:T(8,128)}, f32[8,12,1024]{2,1,0:T(8,128)}, f32[2,8,1024]{2,1,0:T(8,128)}) custom-call(f32[16,128]{1,0:T(8,128)} %pad_bitcast_fusion.x_ref, f32[2,32,1024]{2,1,0:T(8,128)} %copy-done.2, f32[2,32,1024]{2,1,0:T(8,128)} %copy-done.1), custom_call_target="tpu_custom_call" | custom-call | tf_op jit(solution)/shard_map/pallas_call | solution.py:163
  41.3 0.9 slice_select_fusion.11
  42.5 1.3 copy.226
  44.3 0.6 copy.228.rows_ref
  45.0 0.7 multiply_divide_fusion.1.faces_ref
  45.7 0.2 reshape.1381
  47.3 2.9 %cholesky.19 = f32[32,32]{1,0:T(8,128)S(1)} custom-call(f32[32,32]{1,0:T(8,128)S(1)} %add_multiply_fusion), custom_call_target="Cholesky" | custom-call | tf_op jit(solution)/shard_map/jit(cholesky)/cholesky | solution.py:538
  50.3 0.7 compare_reduce_fusion
  50.9 0.6 fusion.9
  51.5 2.4 %custom-call.14 = f32[1,32,32]{1,2,0:T(8,128)S(1)} custom-call(f32[1,32,32]{2,1,0:T(8,128)S(1)} %fusion.9), custom_call_target="InvertDiagBlocksLowerTriangular" | custom-call | tf_op jit(solution)/shard_map/triangular_solve/custom-call.2 | solution.py:542
  54.3 0.6 fusion.62.coef_ref
  54.9 15.4 %shard_map.69 = (f32[2,32,1024]{2,1,0:T(8,128)}, f32[8,128]{1,0:T(8,128)}, f32[8,6,1024]{2,1,0:T(8,128)}, f32[2,4,1024]{2,1,0:T(4,128)}, f32[1]{0:T(128)}) custom-call(f32[2]{0:T(128)} %fusion.62.coef_ref, f32[2,32,1024]{2,1,0:T(8,128)} %copy-done.2, f32[6,2,32,1024]{3,2,1,0:T(8,128)} %bitcast.251, f32[24]{0:T(128)} %reshape.1382.masks_ref, ...), custom_call_target="tpu_custom_call" | custom-call | tf_op jit(solution)/shard_map/pallas_call | solution.py:322
  70.3 1.1 copy.229
  71.6 0.6 copy.233.rows_ref
  72.2 0.7 slice_select_fusion.9
  73.1 0.8 fusion.81
  74.0 0.7 pad_maximum_fusion.2.faces_ref
  74.6 0.5 broadcast_17_coef_ref.2.coef_ref
  75.1 16.4 %shard_map.70 = (f32[2,32,1024]{2,1,0:T(8,128)}, f32[8,128]{1,0:T(8,128)}, f32[8,6,1024]{2,1,0:T(8,128)}, f32[2,4,1024]{2,1,0:T(4,128)}, f32[1]{0:T(128)}) custom-call(f32[2]{0:T(128)} %broadcast_17_coef_ref.2.coef_ref, f32[2,32,1024]{2,1,0:T(8,128)} %get-tuple-element.35.f_ref, f32[6,2,32,1024]{3,2,1,0:T(8,128)} %bitcast.252, f32[24]{0:T(128)} %reshape.1382.masks_ref, ...), custom_call_target="tpu_custom_call" | custom-call | tf_op jit(solution)/shard_map/pallas_call | solution.py:322
  93.0 1.7 multiply_subtract_fusion.1.f_ref
  94.7 0.7 slice.371
  95.8 0.6 fusion.66.coef_ref
  96.4 0.7 slice_select_fusion.7
  97.3 0.8 fusion.80
  98.1 1.1 copy.234
  99.5 0.6 copy.238.rows_ref
  100.1 0.7 multiply_divide_fusion.faces_ref
  100.8 15.7 %shard_map.71 = (f32[2,32,1024]{2,1,0:T(8,128)}, f32[8,128]{1,0:T(8,128)}, f32[8,6,1024]{2,1,0:T(8,128)}, f32[2,4,1024]{2,1,0:T(4,128)}, f32[1]{0:T(128)}) custom-call(f32[2]{0:T(128)} %fusion.66.coef_ref, f32[2,32,1024]{2,1,0:T(8,128)} %multiply_subtract_fusion.1.f_ref, f32[6,2,32,1024]{3,2,1,0:T(8,128)} %bitcast.253, f32[24]{0:T(128)} %reshape.1382.masks_ref, ...), custom_call_target="tpu_custom_call" | custom-call | tf_op jit(solution)/shard_map/pallas_call | solution.py:322
  117.9 1.1 copy.239
  119.2 0.6 fusion.11.rows_ref
  119.8 0.7 slice_select_fusion.5
  120.7 0.8 fusion.79
  121.6 1.7 multiply_add_fusion.1.f_ref
  123.3 0.7 maximum_add_fusion.faces_ref
  123.9 16.1 %shard_map.72 = (f32[2,32,1024]{2,1,0:T(8,128)}, f32[8,128]{1,0:T(8,128)}, f32[8,6,1024]{2,1,0:T(8,128)}, f32[2,4,1024]{2,1,0:T(4,128)}, f32[1]{0:T(128)}) custom-call(f32[2]{0:T(128)} %broadcast_17_coef_ref.2.coef_ref, f32[2,32,1024]{2,1,0:T(8,128)} %multiply_add_fusion.1.f_ref, f32[6,2,32,1024]{3,2,1,0:T(8,128)} %bitcast.254, f32[24]{0:T(128)} %reshape.1382.masks_ref, ...), custom_call_target="tpu_custom_call" | custom-call | tf_op jit(solution)/shard_map/pallas_call | solution.py:322
  141.4 1.7 multiply_subtract_fusion.f_ref
  143.1 0.7 slice.388
  144.2 0.7 fusion.71.coef_ref
  144.9 0.7 slice_select_fusion.3
  145.8 0.8 fusion.78
  146.6 1.1 copy.246
  147.8 0.6 copy.250.rows_ref
  148.6 0.7 fusion.8.faces_ref
  149.3 15.8 %shard_map.73 = (f32[2,32,1024]{2,1,0:T(8,128)}, f32[8,128]{1,0:T(8,128)}, f32[8,6,1024]{2,1,0:T(8,128)}, f32[2,4,1024]{2,1,0:T(4,128)}, f32[1]{0:T(128)}) custom-call(f32[2]{0:T(128)} %fusion.71.coef_ref, f32[2,32,1024]{2,1,0:T(8,128)} %multiply_subtract_fusion.f_ref, f32[6,2,32,1024]{3,2,1,0:T(8,128)} %bitcast.255, f32[24]{0:T(128)} %reshape.1382.masks_ref, ...), custom_call_target="tpu_custom_call" | custom-call | tf_op jit(solution)/shard_map/pallas_call | solution.py:322
  166.5 1.1 copy.251
  167.7 0.6 copy_add_fusion.rows_ref
  168.4 0.7 slice_select_fusion.1
  169.3 0.8 fusion.77
  170.2 0.7 maximum_add_fusion.1.faces_ref
  170.9 0.7 multiply_add_fusion.f_ref
  171.6 14.7 %shard_map.74 = (f32[2,32,1024]{2,1,0:T(8,128)}, f32[8,128]{1,0:T(8,128)}, f32[8,6,1024]{2,1,0:T(8,128)}, f32[2,4,1024]{2,1,0:T(4,128)}, f32[1]{0:T(128)}) custom-call(f32[2]{0:T(128)} %broadcast_17_coef_ref.2.coef_ref, f32[2,32,1024]{2,1,0:T(8,128)} %multiply_add_fusion.f_ref, f32[6,2,32,1024]{3,2,1,0:T(8,128)} %bitcast.256, f32[24]{0:T(128)} %reshape.1382.masks_ref, ...), custom_call_target="tpu_custom_call" | custom-call | tf_op jit(solution)/shard_map/pallas_call | solution.py:322
  187.7 0.8 add_bitcast_fusion
  188.5 1.7 subtract_bitcast_fusion
  (149 shorter events, 7.0 us)
Async XLA Ops:
  0.6 13.2 %copy-start = (f32[1,1,6,2,32,1024]{5,4,3,2,1,0:T(8,128)S(1)}, f32[1,1,6,2,32,1024]{5,4,3,2,1,0:T(8,128)}, u32[]{:S(2)}) copy-start(f32[1,1,6,2,32,1024]{5,4,3,2,1,0:T(8,128)} %param.11) | copy-start | bytes 4718596
  0.6 13.2 %copy-start.9 = (f32[1,1,2,32,1024]{4,3,2,1,0:T(8,128)S(1)}, f32[1,1,2,32,1024]{4,3,2,1,0:T(8,128)}, u32[]{:S(2)}) copy-start(f32[1,1,2,32,1024]{4,3,2,1,0:T(8,128)} %param.10) | copy-start | bytes 786436
  13.8 0.7 copy-start.2
  14.5 1.6 copy-start.1
  41.3 4.4 %copy-start.10 = (f32[16,128]{1,0:T(8,128)S(1)}, f32[16,128]{1,0:T(8,128)}, u32[]{:S(2)}) copy-start(f32[16,128]{1,0:T(8,128)} %get-tuple-element.31) | copy-start | bytes 24580
  42.5 4.5 %copy-start.11 = (pred[32]{0:T(512)(128)(4,1)S(1)}, pred[32]{0:T(512)(128)(4,1)}, u32[]{:S(2)}) copy-start(pred[32]{0:T(512)(128)(4,1)} %constant.259.clone.1) | copy-start | bytes 100
  71.3 21.6 %copy-start.3 = (f32[2,32,1024]{2,1,0:T(8,128)S(1)}, f32[2,32,1024]{2,1,0:T(8,128)}, u32[]{:S(2)}) copy-start(f32[2,32,1024]{2,1,0:T(8,128)} %copy-done.2) | copy-start | bytes 786436
  100.8 20.8 %copy-start.5 = (f32[2,32,1024]{2,1,0:T(8,128)S(1)}, f32[2,32,1024]{2,1,0:T(8,128)}, u32[]{:S(2)}) copy-start(f32[2,32,1024]{2,1,0:T(8,128)} %get-tuple-element.35.f_ref) | copy-start | bytes 786436
  123.2 18.2 %copy-start.7 = (f32[2,32,1024]{2,1,0:T(8,128)S(1)}, f32[2,32,1024]{2,1,0:T(8,128)}, u32[]{:S(2)}) copy-start(f32[2,32,1024]{2,1,0:T(8,128)} %multiply_subtract_fusion.1.f_ref) | copy-start | bytes 786436
  149.3 21.6 %copy-start.4 = (f32[2,32,1024]{2,1,0:T(8,128)S(1)}, f32[2,32,1024]{2,1,0:T(8,128)}, u32[]{:S(2)}) copy-start(f32[2,32,1024]{2,1,0:T(8,128)} %multiply_add_fusion.1.f_ref) | copy-start | bytes 786436
  165.1 5.8 %copy-start.8 = (f32[2,32,1024]{2,1,0:T(8,128)S(1)}, f32[2,32,1024]{2,1,0:T(8,128)}, u32[]{:S(2)}) copy-start(f32[2,32,1024]{2,1,0:T(8,128)} %get-tuple-element.53) | copy-start | bytes 786436
  171.6 16.9 %copy-start.6 = (f32[2,32,1024]{2,1,0:T(8,128)S(1)}, f32[2,32,1024]{2,1,0:T(8,128)}, u32[]{:S(2)}) copy-start(f32[2,32,1024]{2,1,0:T(8,128)} %multiply_subtract_fusion.f_ref) | copy-start | bytes 786436

commit v10 on v9

--- a/solution.py
+++ b/solution.py
@@ -128,8 +128,8 @@
 
 
 def exchange_kernel(
-    x_ref, forcing_ref, diag_ref, o_ref, xy_out, z_out,
-    xy_ref, z_ref, landed_b, landed_g, landed_xy, landed_z,
+    record_ref, forcing_ref, diag_ref, o_ref, xy_out, z_out,
+    x_ref, xy_ref, z_ref, landed_b, landed_g, landed_xy, landed_z,
     send_b, recv_b, send_g, recv_g, send_xy, recv_xy, send_z, recv_z,
 ):
     here_brick = lax.axis_index("brick")
@@ -144,6 +144,15 @@
     slots = forcing_ref.shape[0]
     setup_faces(forcing_ref, xy_ref, z_ref, 0, 0)
     setup_faces(diag_ref, xy_ref, z_ref, 2 * slots + 2, 2 * slots)
+    tile_rows, tile_lanes = x_ref.shape
+    flat = lax.broadcasted_iota(jnp.int32, (tile_rows, tile_lanes), 0) * tile_lanes
+    flat = flat + lax.broadcasted_iota(jnp.int32, (tile_rows, tile_lanes), 1)
+    count = record_ref.shape[0]
+    base = (here_brick * n_grp + here_grp) * count
+    tile = jnp.zeros((tile_rows, tile_lanes), jnp.float32)
+    for i in range(count):
+        tile = jnp.where(flat == base + i, record_ref[i], tile)
+    x_ref[...] = tile
     pl.semaphore_wait(barrier, len(brick_peers) + len(grp_peers))
 
     share(
@@ -152,8 +161,11 @@
     )
 
 
-def exchange(tile, forcing, diag, kernel_id):
+def exchange(record, forcing, diag, kernel_id):
     slots, _, lanes = forcing.shape
+    total = lax.axis_size("brick") * lax.axis_size("grp") * record.shape[0]
+    rows = -(-total // 128)
+    tile = jax.ShapeDtypeStruct((-(-rows // 8) * 8, 128), jnp.float32)
     xy = jax.ShapeDtypeStruct((2 * (2 * slots + 2), lanes), jnp.float32)
     z = jax.ShapeDtypeStruct((2 * (2 * slots), lanes), jnp.float32)
     n_brick = lax.axis_size("brick")
@@ -167,9 +179,10 @@
             jax.ShapeDtypeStruct((n_brick,) + xy.shape, jnp.float32),
             jax.ShapeDtypeStruct((2,) + z.shape, jnp.float32),
         ),
-        in_specs=[vmem] * 3,
+        in_specs=[pl.BlockSpec(memory_space=pltpu.SMEM), vmem, vmem],
         out_specs=(vmem, vmem, vmem),
         scratch_shapes=[
+            pltpu.VMEM(tile.shape, jnp.float32),
             pltpu.VMEM(xy.shape, jnp.float32),
             pltpu.VMEM(z.shape, jnp.float32),
             pltpu.VMEM((n_brick,) + tile.shape, jnp.float32),
@@ -186,7 +199,7 @@
             dma((2,)),
         ],
         compiler_params=pltpu.CompilerParams(collective_id=kernel_id, has_side_effects=True),
-    )(tile, forcing, diag)
+    )(record, forcing, diag)
 
 
 def stencil_body(
@@ -523,9 +536,8 @@
         ]
     )
     brick_here = (peer_ids == brick_index).astype(jnp.float32)
-    spread = (brick_here[:, None, None, None] * slab_slot(record)[None]).reshape(-1)
-    summed, xy_land, z_land = exchange(as_tile(spread), forcing, diagonal, 2)
-    summed = summed.reshape(-1)[: spread.shape[0]]
+    summed, xy_land, z_land = exchange(record.reshape(-1), forcing, diagonal, 2)
+    summed = summed.reshape(-1)[: brick_count * grp_count * record.size]
     xy_rows = 2 * slot_count + 2
     z_rows = 2 * slot_count
     residual_halo = halo(forcing, xy_land[:, :xy_rows], z_land[:, :z_rows], 0.0)

time: 192 us -> 192 us (level)
  no operation moved by 1% of the time
where the time goes in v10:
time: 192 us; the launch traced here: 190 us
  Pallas kernels  120 us (62%)
  other arithmetic  31.5 us (16%)
  local copies, waits for them, and re-layouts  24.7 us (13%)
  between operations  13.4 us (7%)
    pallas_call x6, Pallas kernels, one_round(): pl.pallas_call(functools.partial(round_kernel, smooth=smooth, with_faces=...  94.2 us
    pallas_call x1, Pallas kernels, exchange(): pl.pallas_call(exchange_kernel, out_shape=(jax.ShapeDtypeStruct(tile.shap...  25.4 us
    pallas_call x5, local copies, waits for them, and re-layouts, one_round(): pl.pallas_call(functools.partial(round_kernel, smooth=smooth, with_faces=...  5.35 us
    select_n x6, other arithmetic, halo(): above = jnp.where(slab_index < grp_count - 1, z_land[1, :slot_count], fill)  4.59 us
    slice x7, local copies, waits for them, and re-layouts, halo(): field[1, :, :BS]  4.21 us

profile of v10, /device:TPU:0, one launch (start us, length us, event | category | flops | bytes accessed | tf_op | source)
XLA Modules:
  0.0 190.0 jit_solution(13577976000232583193)
XLA Ops:
  0.7 1.4 dynamic_slice.117
  4.7 1.4 fusion.60
  8.7 1.1 reduce_sum.122
  9.8 0.8 fusion.33
  10.7 0.3 slice_reduce_fusion.7
  11.6 0.7 reshape.1366.masks_ref
  12.3 1.4 fusion.75
  13.8 0.4 fusion.4
  14.3 0.2 copy-done.2
  14.5 0.2 slice_reduce_fusion.1
  15.0 0.6 reshape.1364.record_ref
  15.7 25.4 %shard_map.68 = (f32[16,128]{1,0:T(8,128)}, f32[8,12,1024]{2,1,0:T(8,128)}, f32[2,8,1024]{2,1,0:T(8,128)}) custom-call(f32[10]{0:T(128)} %reshape.1364.record_ref, f32[2,32,1024]{2,1,0:T(8,128)} %copy-done.2, f32[2,32,1024]{2,1,0:T(8,128)} %copy-done.1), custom_call_target="tpu_custom_call" | custom-call | tf_op jit(solution)/shard_map/pallas_call | solution.py:175
  41.1 0.9 slice_select_fusion.11
  42.3 1.3 copy.226
  44.1 0.6 copy.228.rows_ref
  44.8 0.7 multiply_divide_fusion.1.faces_ref
  45.4 0.2 reshape.1365
  47.1 2.9 %cholesky.19 = f32[32,32]{1,0:T(8,128)S(1)} custom-call(f32[32,32]{1,0:T(8,128)S(1)} %add_multiply_fusion), custom_call_target="Cholesky" | custom-call | tf_op jit(solution)/shard_map/jit(cholesky)/cholesky | solution.py:550
  50.0 0.7 compare_reduce_fusion
  50.7 0.6 fusion.9
  51.3 2.4 %custom-call.14 = f32[1,32,32]{1,2,0:T(8,128)S(1)} custom-call(f32[1,32,32]{2,1,0:T(8,128)S(1)} %fusion.9), custom_call_target="InvertDiagBlocksLowerTriangular" | custom-call | tf_op jit(solution)/shard_map/triangular_solve/custom-call.2 | solution.py:554
  54.0 0.6 fusion.62.coef_ref
  54.6 15.4 %shard_map.69 = (f32[2,32,1024]{2,1,0:T(8,128)}, f32[8,128]{1,0:T(8,128)}, f32[8,6,1024]{2,1,0:T(8,128)}, f32[2,4,1024]{2,1,0:T(4,128)}, f32[1]{0:T(128)}) custom-call(f32[2]{0:T(128)} %fusion.62.coef_ref, f32[2,32,1024]{2,1,0:T(8,128)} %copy-done.2, f32[6,2,32,1024]{3,2,1,0:T(8,128)} %bitcast.249, f32[24]{0:T(128)} %reshape.1366.masks_ref, ...), custom_call_target="tpu_custom_call" | custom-call | tf_op jit(solution)/shard_map/pallas_call | solution.py:335
  70.0 1.1 copy.229
  71.4 0.6 copy.233.rows_ref
  72.0 0.7 slice_select_fusion.9
  72.9 0.8 fusion.81
  73.7 0.7 pad_maximum_fusion.2.faces_ref
  74.4 0.5 broadcast_17_coef_ref.2.coef_ref
  74.9 16.4 %shard_map.70 = (f32[2,32,1024]{2,1,0:T(8,128)}, f32[8,128]{1,0:T(8,128)}, f32[8,6,1024]{2,1,0:T(8,128)}, f32[2,4,1024]{2,1,0:T(4,128)}, f32[1]{0:T(128)}) custom-call(f32[2]{0:T(128)} %broadcast_17_coef_ref.2.coef_ref, f32[2,32,1024]{2,1,0:T(8,128)} %get-tuple-element.35.f_ref, f32[6,2,32,1024]{3,2,1,0:T(8,128)} %bitcast.250, f32[24]{0:T(128)} %reshape.1366.masks_ref, ...), custom_call_target="tpu_custom_call" | custom-call | tf_op jit(solution)/shard_map/pallas_call | solution.py:335
  92.7 1.7 multiply_subtract_fusion.1.f_ref
  94.4 0.7 slice.371
  95.5 0.6 fusion.66.coef_ref
  96.1 0.7 slice_select_fusion.7
  97.0 0.8 fusion.80
  97.8 1.1 copy.234
  99.2 0.6 copy.238.rows_ref
  99.8 0.7 multiply_divide_fusion.faces_ref
  100.5 15.8 %shard_map.71 = (f32[2,32,1024]{2,1,0:T(8,128)}, f32[8,128]{1,0:T(8,128)}, f32[8,6,1024]{2,1,0:T(8,128)}, f32[2,4,1024]{2,1,0:T(4,128)}, f32[1]{0:T(128)}) custom-call(f32[2]{0:T(128)} %fusion.66.coef_ref, f32[2,32,1024]{2,1,0:T(8,128)} %multiply_subtract_fusion.1.f_ref, f32[6,2,32,1024]{3,2,1,0:T(8,128)} %bitcast.251, f32[24]{0:T(128)} %reshape.1366.masks_ref, ...), custom_call_target="tpu_custom_call" | custom-call | tf_op jit(solution)/shard_map/pallas_call | solution.py:335
  117.7 1.1 copy.239
  119.0 0.6 fusion.11.rows_ref
  119.7 0.7 slice_select_fusion.5
  120.6 0.8 fusion.79
  121.4 1.7 multiply_add_fusion.1.f_ref
  123.1 0.7 maximum_add_fusion.faces_ref
  123.8 16.1 %shard_map.72 = (f32[2,32,1024]{2,1,0:T(8,128)}, f32[8,128]{1,0:T(8,128)}, f32[8,6,1024]{2,1,0:T(8,128)}, f32[2,4,1024]{2,1,0:T(4,128)}, f32[1]{0:T(128)}) custom-call(f32[2]{0:T(128)} %broadcast_17_coef_ref.2.coef_ref, f32[2,32,1024]{2,1,0:T(8,128)} %multiply_add_fusion.1.f_ref, f32[6,2,32,1024]{3,2,1,0:T(8,128)} %bitcast.252, f32[24]{0:T(128)} %reshape.1366.masks_ref, ...), custom_call_target="tpu_custom_call" | custom-call | tf_op jit(solution)/shard_map/pallas_call | solution.py:335
  141.3 1.7 multiply_subtract_fusion.f_ref
  142.9 0.7 slice.388
  144.0 0.7 fusion.71.coef_ref
  144.7 0.7 slice_select_fusion.3
  145.6 0.8 fusion.78
  146.4 1.1 copy.246
  147.7 0.6 copy.250.rows_ref
  148.4 0.7 fusion.8.faces_ref
  149.1 15.7 %shard_map.73 = (f32[2,32,1024]{2,1,0:T(8,128)}, f32[8,128]{1,0:T(8,128)}, f32[8,6,1024]{2,1,0:T(8,128)}, f32[2,4,1024]{2,1,0:T(4,128)}, f32[1]{0:T(128)}) custom-call(f32[2]{0:T(128)} %fusion.71.coef_ref, f32[2,32,1024]{2,1,0:T(8,128)} %multiply_subtract_fusion.f_ref, f32[6,2,32,1024]{3,2,1,0:T(8,128)} %bitcast.253, f32[24]{0:T(128)} %reshape.1366.masks_ref, ...), custom_call_target="tpu_custom_call" | custom-call | tf_op jit(solution)/shard_map/pallas_call | solution.py:335
  166.3 1.1 copy.251
  167.5 0.6 copy_add_fusion.rows_ref
  168.2 0.7 slice_select_fusion.1
  169.2 0.8 fusion.77
  170.0 0.7 maximum_add_fusion.1.faces_ref
  170.7 0.7 multiply_add_fusion.f_ref
  171.5 14.7 %shard_map.74 = (f32[2,32,1024]{2,1,0:T(8,128)}, f32[8,128]{1,0:T(8,128)}, f32[8,6,1024]{2,1,0:T(8,128)}, f32[2,4,1024]{2,1,0:T(4,128)}, f32[1]{0:T(128)}) custom-call(f32[2]{0:T(128)} %broadcast_17_coef_ref.2.coef_ref, f32[2,32,1024]{2,1,0:T(8,128)} %multiply_add_fusion.f_ref, f32[6,2,32,1024]{3,2,1,0:T(8,128)} %bitcast.254, f32[24]{0:T(128)} %reshape.1366.masks_ref, ...), custom_call_target="tpu_custom_call" | custom-call | tf_op jit(solution)/shard_map/pallas_call | solution.py:335
  187.6 0.8 add_bitcast_fusion
  188.3 1.7 subtract_bitcast_fusion
  (144 shorter events, 6.6 us)
Async XLA Ops:
  0.6 13.2 %copy-start = (f32[1,1,6,2,32,1024]{5,4,3,2,1,0:T(8,128)S(1)}, f32[1,1,6,2,32,1024]{5,4,3,2,1,0:T(8,128)}, u32[]{:S(2)}) copy-start(f32[1,1,6,2,32,1024]{5,4,3,2,1,0:T(8,128)} %param.11) | copy-start | bytes 4718596
  0.6 13.2 %copy-start.9 = (f32[1,1,2,32,1024]{4,3,2,1,0:T(8,128)S(1)}, f32[1,1,2,32,1024]{4,3,2,1,0:T(8,128)}, u32[]{:S(2)}) copy-start(f32[1,1,2,32,1024]{4,3,2,1,0:T(8,128)} %param.10) | copy-start | bytes 786436
  13.7 0.7 copy-start.2
  14.5 1.2 copy-start.1
  41.1 4.4 %copy-start.10 = (f32[16,128]{1,0:T(8,128)S(1)}, f32[16,128]{1,0:T(8,128)}, u32[]{:S(2)}) copy-start(f32[16,128]{1,0:T(8,128)} %get-tuple-element.31) | copy-start | bytes 24580
  42.3 4.5 %copy-start.11 = (pred[32]{0:T(512)(128)(4,1)S(1)}, pred[32]{0:T(512)(128)(4,1)}, u32[]{:S(2)}) copy-start(pred[32]{0:T(512)(128)(4,1)} %constant.258.clone.1) | copy-start | bytes 100
  71.1 21.6 %copy-start.3 = (f32[2,32,1024]{2,1,0:T(8,128)S(1)}, f32[2,32,1024]{2,1,0:T(8,128)}, u32[]{:S(2)}) copy-start(f32[2,32,1024]{2,1,0:T(8,128)} %copy-done.2) | copy-start | bytes 786436
  100.5 20.9 %copy-start.5 = (f32[2,32,1024]{2,1,0:T(8,128)S(1)}, f32[2,32,1024]{2,1,0:T(8,128)}, u32[]{:S(2)}) copy-start(f32[2,32,1024]{2,1,0:T(8,128)} %get-tuple-element.35.f_ref) | copy-start | bytes 786436
  123.1 18.2 %copy-start.7 = (f32[2,32,1024]{2,1,0:T(8,128)S(1)}, f32[2,32,1024]{2,1,0:T(8,128)}, u32[]{:S(2)}) copy-start(f32[2,32,1024]{2,1,0:T(8,128)} %multiply_subtract_fusion.1.f_ref) | copy-start | bytes 786436
  149.1 21.6 %copy-start.4 = (f32[2,32,1024]{2,1,0:T(8,128)S(1)}, f32[2,32,1024]{2,1,0:T(8,128)}, u32[]{:S(2)}) copy-start(f32[2,32,1024]{2,1,0:T(8,128)} %multiply_add_fusion.1.f_ref) | copy-start | bytes 786436
  164.9 5.8 %copy-start.8 = (f32[2,32,1024]{2,1,0:T(8,128)S(1)}, f32[2,32,1024]{2,1,0:T(8,128)}, u32[]{:S(2)}) copy-start(f32[2,32,1024]{2,1,0:T(8,128)} %get-tuple-element.53) | copy-start | bytes 786436
  171.4 16.9 %copy-start.6 = (f32[2,32,1024]{2,1,0:T(8,128)S(1)}, f32[2,32,1024]{2,1,0:T(8,128)}, u32[]{:S(2)}) copy-start(f32[2,32,1024]{2,1,0:T(8,128)} %multiply_subtract_fusion.f_ref) | copy-start | bytes 786436

commit v11 on v10

--- a/solution.py
+++ b/solution.py
@@ -549,12 +549,15 @@
     matrix = assemble(columns[0], (columns[1], columns[2], columns[3]), (PATCH_Y, 1, slot_count))
     factor = jnp.linalg.cholesky(matrix)
 
+    identity = jnp.eye(factor.shape[0], dtype=jnp.float32)
+    middle = lax.linalg.triangular_solve(factor, identity, left_side=True, lower=True)
+    inverse = lax.linalg.triangular_solve(
+        factor, middle, left_side=True, lower=True, transpose_a=True
+    )
+    own_rows = lax.dynamic_slice_in_dim(inverse, slab_index * slot_count, slot_count)
+
     def coarse_solve(terms):
-        middle = lax.linalg.triangular_solve(factor, terms[:, None], left_side=True, lower=True)
-        result = lax.linalg.triangular_solve(
-            factor, middle, left_side=True, lower=True, transpose_a=True
-        )
-        return lax.dynamic_slice_in_dim(result[:, 0], slab_index * slot_count, slot_count)
+        return jnp.dot(own_rows, terms, precision=lax.Precision.HIGHEST)
 
     def round_trip(field, field_halo, coef, smooth, with_faces=True):
         out, total, xy_land, z_land, dot = one_round(

time: 192 us -> 191 us (level)
    dot_general x0 -> x3, matrix products: none -> 2.01 us  [coarse_solve(): return jnp.dot(own_rows, terms, precision=lax.Precision.HIGHEST)]
where the time goes in v11:
time: 191 us; the launch traced here: 190 us
  Pallas kernels  119 us (62%)
  other arithmetic  31.5 us (16%)
  local copies, waits for them, and re-layouts  22.9 us (12%)
  between operations  13.4 us (7%)
  matrix products  2.38 us (1%)
    pallas_call x6, Pallas kernels, one_round(): pl.pallas_call(functools.partial(round_kernel, smooth=smooth, with_faces=...  94 us
    pallas_call x1, Pallas kernels, exchange(): pl.pallas_call(exchange_kernel, out_shape=(jax.ShapeDtypeStruct(tile.shap...  25.4 us
    pallas_call x5, local copies, waits for them, and re-layouts, one_round(): pl.pallas_call(functools.partial(round_kernel, smooth=smooth, with_faces=...  5.35 us
    select_n x6, other arithmetic, halo(): above = jnp.where(slab_index < grp_count - 1, z_land[1, :slot_count], fill)  4.59 us
    slice x7, local copies, waits for them, and re-layouts, halo(): field[1, :, :BS]  4.21 us

profile of v11, /device:TPU:0, one launch (start us, length us, event | category | flops | bytes accessed | tf_op | source)
XLA Modules:
  0.0 189.6 jit_solution(6989464282058023377)
XLA Ops:
  0.7 1.4 dynamic_slice.105
  4.7 1.4 fusion.58
  8.7 1.1 reduce_sum.122
  9.8 0.8 fusion.31
  10.7 0.3 slice_reduce_fusion.7
  11.6 0.7 reshape.1302.masks_ref
  12.3 1.4 fusion.72
  13.8 0.4 fusion.4
  14.5 0.2 slice_reduce_fusion.1
  15.0 0.6 reshape.1300.record_ref
  15.7 25.4 %shard_map.68 = (f32[16,128]{1,0:T(8,128)}, f32[8,12,1024]{2,1,0:T(8,128)}, f32[2,8,1024]{2,1,0:T(8,128)}) custom-call(f32[10]{0:T(128)} %reshape.1300.record_ref, f32[2,32,1024]{2,1,0:T(8,128)} %copy-done.2, f32[2,32,1024]{2,1,0:T(8,128)} %copy-done.1), custom_call_target="tpu_custom_call" | custom-call | tf_op jit(solution)/shard_map/pallas_call | solution.py:175
  41.1 0.9 slice_select_fusion.11
  42.3 1.3 copy.226
  44.1 0.6 copy.228.rows_ref
  44.8 0.7 multiply_divide_fusion.1.faces_ref
  45.4 0.2 reshape.1301
  47.2 2.9 %cholesky.17 = f32[32,32]{1,0:T(8,128)S(1)} custom-call(f32[32,32]{1,0:T(8,128)S(1)} %add_multiply_fusion), custom_call_target="Cholesky" | custom-call | tf_op jit(solution)/shard_map/jit(cholesky)/cholesky | solution.py:550
  50.1 0.7 compare_reduce_fusion
  50.8 0.6 fusion.9
  51.4 2.4 %custom-call.8 = f32[1,32,32]{1,2,0:T(8,128)S(1)} custom-call(f32[1,32,32]{2,1,0:T(8,128)S(1)} %fusion.9), custom_call_target="InvertDiagBlocksLowerTriangular" | custom-call | tf_op jit(solution)/shard_map/triangular_solve | solution.py:554
  53.8 0.2 fusion.17
  54.2 0.6 convolution_bitcast_fusion.2.coef_ref
  54.8 15.4 %shard_map.69 = (f32[2,32,1024]{2,1,0:T(8,128)}, f32[8,128]{1,0:T(8,128)}, f32[8,6,1024]{2,1,0:T(8,128)}, f32[2,4,1024]{2,1,0:T(4,128)}, f32[1]{0:T(128)}) custom-call(f32[2]{0:T(128)} %convolution_bitcast_fusion.2.coef_ref, f32[2,32,1024]{2,1,0:T(8,128)} %copy-done.2, f32[6,2,32,1024]{3,2,1,0:T(8,128)} %bitcast.213, f32[24]{0:T(128)} %reshape.1302.masks_ref, ...), custom_call_target="tpu_custom_call" | custom-call | tf_op jit(solution)/shard_map/pallas_call | solution.py:335
  70.3 1.1 copy.229
  71.6 0.6 copy.233.rows_ref
  72.2 0.7 slice_select_fusion.9
  73.1 0.8 fusion.78
  73.9 0.7 pad_maximum_fusion.2.faces_ref
  74.6 0.5 broadcast_17_coef_ref.2.coef_ref
  75.1 16.3 %shard_map.70 = (f32[2,32,1024]{2,1,0:T(8,128)}, f32[8,128]{1,0:T(8,128)}, f32[8,6,1024]{2,1,0:T(8,128)}, f32[2,4,1024]{2,1,0:T(4,128)}, f32[1]{0:T(128)}) custom-call(f32[2]{0:T(128)} %broadcast_17_coef_ref.2.coef_ref, f32[2,32,1024]{2,1,0:T(8,128)} %get-tuple-element.33.f_ref, f32[6,2,32,1024]{3,2,1,0:T(8,128)} %bitcast.214, f32[24]{0:T(128)} %reshape.1302.masks_ref, ...), custom_call_target="tpu_custom_call" | custom-call | tf_op jit(solution)/shard_map/pallas_call | solution.py:335
  92.9 1.7 multiply_subtract_fusion.1.f_ref
  94.6 0.7 slice.375
  95.4 0.7 convolution_bitcast_fusion.1.coef_ref
  96.0 0.7 slice_select_fusion.7
  96.9 0.8 fusion.77
  97.8 1.1 copy.234
  99.1 0.6 copy.238.rows_ref
  99.7 0.7 multiply_divide_fusion.faces_ref
  100.4 15.7 %shard_map.71 = (f32[2,32,1024]{2,1,0:T(8,128)}, f32[8,128]{1,0:T(8,128)}, f32[8,6,1024]{2,1,0:T(8,128)}, f32[2,4,1024]{2,1,0:T(4,128)}, f32[1]{0:T(128)}) custom-call(f32[2]{0:T(128)} %convolution_bitcast_fusion.1.coef_ref, f32[2,32,1024]{2,1,0:T(8,128)} %multiply_subtract_fusion.1.f_ref, f32[6,2,32,1024]{3,2,1,0:T(8,128)} %bitcast.215, ...), custom_call_target="tpu_custom_call" | custom-call | tf_op jit(solution)/shard_map/pallas_call | solution.py:335
  117.6 1.1 copy.239
  118.9 0.6 fusion.11.rows_ref
  119.5 0.7 slice_select_fusion.5
  120.4 0.8 fusion.76
  121.3 1.7 multiply_add_fusion.1.f_ref
  123.0 0.7 maximum_add_fusion.faces_ref
  123.6 16.1 %shard_map.72 = (f32[2,32,1024]{2,1,0:T(8,128)}, f32[8,128]{1,0:T(8,128)}, f32[8,6,1024]{2,1,0:T(8,128)}, f32[2,4,1024]{2,1,0:T(4,128)}, f32[1]{0:T(128)}) custom-call(f32[2]{0:T(128)} %broadcast_17_coef_ref.2.coef_ref, f32[2,32,1024]{2,1,0:T(8,128)} %multiply_add_fusion.1.f_ref, f32[6,2,32,1024]{3,2,1,0:T(8,128)} %bitcast.216, f32[24]{0:T(128)} %reshape.1302.masks_ref, ...), custom_call_target="tpu_custom_call" | custom-call | tf_op jit(solution)/shard_map/pallas_call | solution.py:335
  141.1 1.7 multiply_subtract_fusion.f_ref
  142.8 0.7 slice.392
  143.6 0.7 convolution_bitcast_fusion.coef_ref
  144.3 0.7 slice_select_fusion.3
  145.3 0.8 fusion.75
  146.1 1.1 copy.246
  147.3 0.6 copy.250.rows_ref
  148.1 0.7 fusion.8.faces_ref
  148.8 15.7 %shard_map.73 = (f32[2,32,1024]{2,1,0:T(8,128)}, f32[8,128]{1,0:T(8,128)}, f32[8,6,1024]{2,1,0:T(8,128)}, f32[2,4,1024]{2,1,0:T(4,128)}, f32[1]{0:T(128)}) custom-call(f32[2]{0:T(128)} %convolution_bitcast_fusion.coef_ref, f32[2,32,1024]{2,1,0:T(8,128)} %multiply_subtract_fusion.f_ref, f32[6,2,32,1024]{3,2,1,0:T(8,128)} %bitcast.217, ...), custom_call_target="tpu_custom_call" | custom-call | tf_op jit(solution)/shard_map/pallas_call | solution.py:335
  165.9 1.1 copy.251
  167.1 0.6 copy_add_fusion.rows_ref
  167.8 0.7 slice_select_fusion.1
  168.8 0.8 fusion.74
  169.6 0.7 maximum_add_fusion.1.faces_ref
  170.3 0.7 multiply_add_fusion.f_ref
  171.1 14.7 %shard_map.74 = (f32[2,32,1024]{2,1,0:T(8,128)}, f32[8,128]{1,0:T(8,128)}, f32[8,6,1024]{2,1,0:T(8,128)}, f32[2,4,1024]{2,1,0:T(4,128)}, f32[1]{0:T(128)}) custom-call(f32[2]{0:T(128)} %broadcast_17_coef_ref.2.coef_ref, f32[2,32,1024]{2,1,0:T(8,128)} %multiply_add_fusion.f_ref, f32[6,2,32,1024]{3,2,1,0:T(8,128)} %bitcast.218, f32[24]{0:T(128)} %reshape.1302.masks_ref, ...), custom_call_target="tpu_custom_call" | custom-call | tf_op jit(solution)/shard_map/pallas_call | solution.py:335
  187.2 0.8 add_bitcast_fusion
  187.9 1.7 subtract_bitcast_fusion
  (141 shorter events, 6.2 us)
Async XLA Ops:
  0.6 13.2 %copy-start = (f32[1,1,6,2,32,1024]{5,4,3,2,1,0:T(8,128)S(1)}, f32[1,1,6,2,32,1024]{5,4,3,2,1,0:T(8,128)}, u32[]{:S(2)}) copy-start(f32[1,1,6,2,32,1024]{5,4,3,2,1,0:T(8,128)} %param.7) | copy-start | bytes 4718596
  0.6 13.2 %copy-start.9 = (f32[1,1,2,32,1024]{4,3,2,1,0:T(8,128)S(1)}, f32[1,1,2,32,1024]{4,3,2,1,0:T(8,128)}, u32[]{:S(2)}) copy-start(f32[1,1,2,32,1024]{4,3,2,1,0:T(8,128)} %param.6) | copy-start | bytes 786436
  13.7 0.7 copy-start.2
  14.5 1.2 copy-start.1
  41.1 4.4 %copy-start.10 = (f32[16,128]{1,0:T(8,128)S(1)}, f32[16,128]{1,0:T(8,128)}, u32[]{:S(2)}) copy-start(f32[16,128]{1,0:T(8,128)} %get-tuple-element.29) | copy-start | bytes 24580
  42.3 4.6 %copy-start.11 = (pred[32]{0:T(512)(128)(4,1)S(1)}, pred[32]{0:T(512)(128)(4,1)}, u32[]{:S(2)}) copy-start(pred[32]{0:T(512)(128)(4,1)} %constant.257.clone.1) | copy-start | bytes 100
  71.3 21.5 %copy-start.3 = (f32[2,32,1024]{2,1,0:T(8,128)S(1)}, f32[2,32,1024]{2,1,0:T(8,128)}, u32[]{:S(2)}) copy-start(f32[2,32,1024]{2,1,0:T(8,128)} %copy-done.2) | copy-start | bytes 786436
  100.4 20.8 %copy-start.5 = (f32[2,32,1024]{2,1,0:T(8,128)S(1)}, f32[2,32,1024]{2,1,0:T(8,128)}, u32[]{:S(2)}) copy-start(f32[2,32,1024]{2,1,0:T(8,128)} %get-tuple-element.33.f_ref) | copy-start | bytes 786436
  122.9 18.2 %copy-start.7 = (f32[2,32,1024]{2,1,0:T(8,128)S(1)}, f32[2,32,1024]{2,1,0:T(8,128)}, u32[]{:S(2)}) copy-start(f32[2,32,1024]{2,1,0:T(8,128)} %multiply_subtract_fusion.1.f_ref) | copy-start | bytes 786436
  148.8 21.5 %copy-start.4 = (f32[2,32,1024]{2,1,0:T(8,128)S(1)}, f32[2,32,1024]{2,1,0:T(8,128)}, u32[]{:S(2)}) copy-start(f32[2,32,1024]{2,1,0:T(8,128)} %multiply_add_fusion.1.f_ref) | copy-start | bytes 786436
  164.5 5.8 %copy-start.8 = (f32[2,32,1024]{2,1,0:T(8,128)S(1)}, f32[2,32,1024]{2,1,0:T(8,128)}, u32[]{:S(2)}) copy-start(f32[2,32,1024]{2,1,0:T(8,128)} %get-tuple-element.51) | copy-start | bytes 786436
  171.1 16.9 %copy-start.6 = (f32[2,32,1024]{2,1,0:T(8,128)S(1)}, f32[2,32,1024]{2,1,0:T(8,128)}, u32[]{:S(2)}) copy-start(f32[2,32,1024]{2,1,0:T(8,128)} %multiply_subtract_fusion.f_ref) | copy-start | bytes 786436
